TPU v7x, 32 devices: a whole 2x2x4 slice. The times are simulated.
32 devices in a mesh: grp: 1, tm: 16 (over z, y, x), panel: 2 (over core).
Axes of the slice: x: 2, y: 2, z: 4, core: 2. Of those that a mesh axis runs over, the one named last changes fastest.
Arguments:
- series: bfloat16 [8192, 64], P(('grp', 'tm')), may hold values from -4 to 4
- test_matrix: bfloat16 [16384, 512], P('tm', 'panel'), may hold values from -0.046875 to 0.046875
Outputs:
- basis: float32 [8192, 512], P(('grp', 'tm'), 'panel')
- triangle: float32 [512, 512], P('grp', 'panel')
All inputs are finite; a program needn't handle non-finite values.
Results may differ from a plain program's by a relative error of at most 0.0003.
Values may be sent and summed in bfloat16 or wider, within the bound.
No kernel may reach another device: no remote copies, remote signals or barrier semaphores. Data moves between devices by JAX's collectives and lax.ppermute only.
A program may use at most 128 MiB of HBM per device.

v0:
```python
import jax
import jax.numpy as jnp
from jax import lax
from jax.sharding import PartitionSpec as P

WINDOW_LAGS = 256
LAG_SPACING = 8
PW = 64


HIGH = lax.Precision.HIGHEST


def passed_along(block, axis, distance):
    devices = range(lax.axis_size(axis))
    route = [(i - distance, i) for i in devices if i - distance in devices]
    return lax.ppermute(block, axis, route)


def inner(left, right):
    return jnp.dot(left.T, right, precision=HIGH, preferred_element_type=jnp.float32)


def lower_solve(lower, block):
    return jax.scipy.linalg.solve_triangular(lower, block.T, lower=True).T


def total_gram(block):
    return lax.psum(inner(block, block), "tm")


def factor_half(block):
    width = block.shape[1]
    panels = width // PW
    done = None
    columns = []
    for index in range(panels):
        panel_now = block[:, index * PW : (index + 1) * PW]
        if index == 0:
            gram_now = total_gram(panel_now)
            coef = None
        else:
            coef = lax.psum(inner(done, panel_now), "tm")
            panel_now = panel_now - jnp.dot(done, coef, precision=HIGH)
            gram_now = total_gram(panel_now)
        lower = jnp.linalg.cholesky(gram_now)
        final = lower_solve(lower, panel_now)
        pieces = [] if coef is None else [coef]
        pieces = pieces + [lower.T, jnp.zeros((width - (index + 1) * PW, PW), jnp.float32)]
        columns.append(jnp.concatenate(pieces, 0))
        done = final if done is None else jnp.concatenate([done, final], 1)
    return (done, jnp.concatenate(columns, 1))


def per_device(series, test_matrix):
    steps_per_device = series.shape[0]
    variable_count = series.shape[1]
    half_count = test_matrix.shape[1]
    window_span = LAG_SPACING * (WINDOW_LAGS - 1)
    later_count = (window_span + steps_per_device - 1) // steps_per_device
    pieces = [series]
    for offset in range(1, later_count + 1):
        pieces.append(passed_along(series, "tm", -offset))
    lengthened_series = jnp.concatenate(pieces, 0)
    rows_per_phase = steps_per_device // LAG_SPACING
    starting_rows = lengthened_series.shape[0] // LAG_SPACING
    grouped_by_phase = (
        lengthened_series.reshape(starting_rows, LAG_SPACING, variable_count)
        .transpose(1, 0, 2)
        .reshape(LAG_SPACING, starting_rows * variable_count)
    )
    required_length = rows_per_phase + WINDOW_LAGS + 1
    padding_values = jnp.zeros(
        (LAG_SPACING, (required_length - starting_rows) * variable_count), grouped_by_phase.dtype
    )
    grouped_by_phase = jnp.concatenate([grouped_by_phase, padding_values], 1)
    total_starts = jnp.zeros((LAG_SPACING, rows_per_phase, half_count), jnp.float32)
    piece = lax.all_gather(test_matrix, "tm", axis=0, tiled=True)
    row_count = piece.shape[0]
    blocks = (row_count + variable_count - 1) // variable_count
    window = lax.slice_in_dim(
        grouped_by_phase, 0, (rows_per_phase + blocks) * variable_count, axis=1
    )
    slices = [
        window[:, step * variable_count : (step + rows_per_phase) * variable_count].reshape(
            LAG_SPACING, rows_per_phase, variable_count
        )
        for step in range(blocks)
    ]
    lagged = jnp.concatenate(slices, 2)[:, :, :row_count]
    folded = total_starts + jnp.einsum(
        "ban,nh->bah", lagged, piece, preferred_element_type=jnp.float32
    )
    sketch = folded.transpose(1, 0, 2).reshape(steps_per_device, half_count)
    position = lax.axis_index("panel")
    first_basis, _ = factor_half(sketch)
    partner = passed_along(first_basis, "panel", 1)
    second = (position == 1).astype(jnp.float32)
    coef = lax.psum(inner(partner, sketch), "tm")
    reduced = sketch - jnp.dot(partner, coef, precision=HIGH)
    basis_half, upper_half = factor_half(reduced)
    top = second * coef + (1.0 - second) * upper_half
    bottom = second * upper_half
    block_upper = jnp.concatenate([top, bottom], 0)
    factor = jnp.sqrt(jnp.asarray(steps_per_device * lax.axis_size("tm"), jnp.float32))
    return (basis_half * factor, block_upper / factor)


def solution(mesh):
    placed = (P(("grp", "tm"), None), P("tm", "panel"))
    return jax.shard_map(
        per_device,
        mesh=mesh,
        in_specs=placed,
        out_specs=(P(("grp", "tm"), "panel"), P("grp", "panel")),
        check_vma=False,
    )
```

profile of v0, /device:TPU:0, one launch (start us, length us, event | category | flops | bytes accessed | tf_op | source)
XLA Modules:
  0.0 1753.9 jit_solution(6648902794935011099)
XLA Ops:
  15.3 3.4 collective-permute-done.1
  18.6 1.9 collective-permute-done.2
  20.6 3.3 collective-permute-done.3
  67.0 1.7 reshape.1044
  74.9 1.7 reshape.806
  86.7 1.7 reshape.813
  108.1 2.0 reshape.825
  161.8 1.7 reshape.856
  234.8 1.8 reshape.898
  241.2 1.7 reshape.901
  296.2 1.7 reshape.947
  329.3 1.7 reshape.966
  360.8 1.9 reshape.984
  384.5 1.7 reshape.998
  433.3 65.7 %concatenate.47 = bf16[8,64,16384]{2,1,0:T(8,128)(2,1)} concatenate(bf16[8,64,64]{2,1,0:T(8,128)(2,1)} %reshape.791, bf16[8,64,64]{2,1,0:T(8,128)(2,1)} %reshape.792, bf16[8,64,64]{2,1,0:T(8,128)(2,1)} %reshape.793, bf16[8,64,64]{2,1,0:T(8,128)(2,1)} %reshape.794, bf16[8,64,64]{2,1,0:T(8,128)(2,1)} %reshape.795, bf16[8,64,64]{2,1,0:T(8,128)(2,1)} %reshape.796, ...), dimensions={2} | concatenate | bytes 33554432 | tf_op jit(solution)/shard_map/concatenate | solution.py:90
  499.0 10.5 fusion.2
  510.6 76.7 %psum.105 = f32[64,64]{0,1:T(8,128)S(1)} all-reduce(f32[64,64]{0,1:T(8,128)S(1)} %fusion.12), channel_id=1, replica_groups=mesh['grp'=1,'tm'=16,'panel'=2] {'tm'}, use_global_device_ids=true, to_apply=%region_0.0 | all-reduce | flops 4096 | bytes 32768 | tf_op jit(solution)/shard_map/psum | solution.py:29
  587.5 5.8 cholesky.134
  594.7 4.9 custom-call.12
  600.3 71.8 %psum.106 = f32[64,64]{1,0:T(8,128)S(1)} all-reduce(f32[64,64]{1,0:T(8,128)S(1)} %fusion.33), channel_id=1, replica_groups=mesh['grp'=1,'tm'=16,'panel'=2] {'tm'}, use_global_device_ids=true, to_apply=%region_3.0 | all-reduce | flops 4096 | bytes 32768 | tf_op jit(solution)/shard_map/psum | solution.py:43
  672.6 71.8 %psum.107 = f32[64,64]{0,1:T(8,128)S(1)} all-reduce(f32[64,64]{0,1:T(8,128)S(1)} %fusion.91), channel_id=1, replica_groups=mesh['grp'=1,'tm'=16,'panel'=2] {'tm'}, use_global_device_ids=true, to_apply=%region_4.0 | all-reduce | flops 4096 | bytes 32768 | tf_op jit(solution)/shard_map/psum | solution.py:29
  744.5 5.8 cholesky.145
  751.7 4.9 custom-call.13
  757.3 71.8 %psum.108 = f32[128,64]{1,0:T(8,128)S(1)} all-reduce(f32[128,64]{1,0:T(8,128)S(1)} %fusion.15), channel_id=1, replica_groups=mesh['grp'=1,'tm'=16,'panel'=2] {'tm'}, use_global_device_ids=true, to_apply=%region_5.0 | all-reduce | flops 8192 | bytes 65536 | tf_op jit(solution)/shard_map/psum | solution.py:43
  829.7 71.7 %psum.109 = f32[64,64]{0,1:T(8,128)S(1)} all-reduce(f32[64,64]{0,1:T(8,128)S(1)} %fusion.92), channel_id=1, replica_groups=mesh['grp'=1,'tm'=16,'panel'=2] {'tm'}, use_global_device_ids=true, to_apply=%region_6.0 | all-reduce | flops 4096 | bytes 32768 | tf_op jit(solution)/shard_map/psum | solution.py:29
  901.5 5.8 cholesky.156
  908.7 4.9 custom-call.14
  914.4 72.6 %psum.110 = f32[192,64]{1,0:T(8,128)S(1)} all-reduce(f32[192,64]{1,0:T(8,128)S(1)} %fusion.6), channel_id=1, replica_groups=mesh['grp'=1,'tm'=16,'panel'=2] {'tm'}, use_global_device_ids=true, to_apply=%region_7.0 | all-reduce | flops 12288 | bytes 98304 | tf_op jit(solution)/shard_map/psum | solution.py:43
  987.7 73.9 %psum.111 = f32[64,64]{0,1:T(8,128)S(1)} all-reduce(f32[64,64]{0,1:T(8,128)S(1)} %fusion.93), channel_id=1, replica_groups=mesh['grp'=1,'tm'=16,'panel'=2] {'tm'}, use_global_device_ids=true, to_apply=%region_8.0 | all-reduce | flops 4096 | bytes 32768 | tf_op jit(solution)/shard_map/psum | solution.py:29
  1061.7 5.8 cholesky.167
  1068.9 4.9 custom-call.15
  1077.0 1.9 fusion.76
  1078.9 104.1 %all-reduce.3.cloned.1.call-done = f32[256,256]{0,1:T(8,128)} async-done(((f32[256,256]{0,1:T(8,128)}), f32[256,256]{0,1:T(8,128)}) %all-reduce.3.cloned.1.call-update) | async-done | bytes 262160 | tf_op jit(solution)/shard_map/psum | solution.py:99
  1184.8 74.9 %psum.113 = f32[64,64]{0,1:T(8,128)S(1)} all-reduce(f32[64,64]{0,1:T(8,128)S(1)} %fusion.29), channel_id=1, replica_groups=mesh['grp'=1,'tm'=16,'panel'=2] {'tm'}, use_global_device_ids=true, to_apply=%region_10.0 | all-reduce | flops 4096 | bytes 32768 | tf_op jit(solution)/shard_map/psum | solution.py:29
  1259.8 5.8 cholesky.178
  1267.0 4.9 custom-call.16
  1272.5 71.7 %psum.114 = f32[64,64]{0,1:T(8,128)S(1)} all-reduce(f32[64,64]{0,1:T(8,128)S(1)} %fusion.26), channel_id=1, replica_groups=mesh['grp'=1,'tm'=16,'panel'=2] {'tm'}, use_global_device_ids=true, to_apply=%region_11.0 | all-reduce | flops 4096 | bytes 32768 | tf_op jit(solution)/shard_map/psum | solution.py:43
  1344.8 71.8 %psum.115 = f32[64,64]{0,1:T(8,128)S(1)} all-reduce(f32[64,64]{0,1:T(8,128)S(1)} %fusion.94), channel_id=1, replica_groups=mesh['grp'=1,'tm'=16,'panel'=2] {'tm'}, use_global_device_ids=true, to_apply=%region_12.0 | all-reduce | flops 4096 | bytes 32768 | tf_op jit(solution)/shard_map/psum | solution.py:29
  1416.7 5.8 cholesky.189
  1423.9 4.9 custom-call.17
  1429.5 71.7 %psum.116 = f32[128,64]{0,1:T(8,128)S(1)} all-reduce(f32[128,64]{0,1:T(8,128)S(1)} %fusion.14), channel_id=1, replica_groups=mesh['grp'=1,'tm'=16,'panel'=2] {'tm'}, use_global_device_ids=true, to_apply=%region_13.0 | all-reduce | flops 8192 | bytes 65536 | tf_op jit(solution)/shard_map/psum | solution.py:43
  1501.8 72.0 %psum.117 = f32[64,64]{0,1:T(8,128)S(1)} all-reduce(f32[64,64]{0,1:T(8,128)S(1)} %fusion.95), channel_id=1, replica_groups=mesh['grp'=1,'tm'=16,'panel'=2] {'tm'}, use_global_device_ids=true, to_apply=%region_14.0 | all-reduce | flops 4096 | bytes 32768 | tf_op jit(solution)/shard_map/psum | solution.py:29
  1573.9 5.8 cholesky.200
  1581.1 4.9 custom-call.18
  1586.8 71.8 %psum.118 = f32[192,64]{0,1:T(8,128)S(1)} all-reduce(f32[192,64]{0,1:T(8,128)S(1)} %fusion.5), channel_id=1, replica_groups=mesh['grp'=1,'tm'=16,'panel'=2] {'tm'}, use_global_device_ids=true, to_apply=%region_15.18 | all-reduce | flops 12288 | bytes 98304 | tf_op jit(solution)/shard_map/psum | solution.py:43
  1659.2 71.7 %psum.119 = f32[64,64]{0,1:T(8,128)S(1)} all-reduce(f32[64,64]{0,1:T(8,128)S(1)} %fusion.96), channel_id=1, replica_groups=mesh['grp'=1,'tm'=16,'panel'=2] {'tm'}, use_global_device_ids=true, to_apply=%region_16.19 | all-reduce | flops 4096 | bytes 32768 | tf_op jit(solution)/shard_map/psum | solution.py:29
  1731.1 5.8 cholesky.211
  1740.5 4.9 custom-call.19
  (359 shorter events, 426.7 us)
Async XLA Ops:
  7.2 491.8 %all-gather.2.cloned.1.call-start = ((), (), s32[]{:S(2)}) async-start(), calls=%async_computation | async-start | bytes 8912896 | tf_op jit(solution)/shard_map/all_gather | solution.py:78
  7.9 1175.1 %all-reduce.3.cloned.1.call-start = ((), (), s32[]{:S(2)}) async-start(), calls=%async_computation.1 | async-start | bytes 524288 | tf_op jit(solution)/shard_map/psum | solution.py:99
  7.9 7.3 collective-permute-start
  9.2 9.4 collective-permute-start.1
  10.5 10.1 collective-permute-start.2
  11.8 12.1 collective-permute-start.3
  1074.1 2.8 collective-permute-start.4
Sparse Core Ops, SparseCore 0:
  10.7 115.0 all-gather.1
  1079.0 103.8 all-reduce.2
where the time goes:
time: 1780 us; the launch traced here: 1750 us
  blocking collectives  1020 us (57%)
  local copies, waits for them, and re-layouts  479 us (27%)
  waiting for transfers between devices  116 us (7%)
  other arithmetic  97.9 us (6%)
  matrix products  23.4 us (1%)
    psum x8, blocking collectives, total_gram(): return lax.psum(inner(block, block), 'tm')  585 us
    psum x6, blocking collectives, factor_half(): coef = lax.psum(inner(done, panel_now), 'tm')  431 us
    reshape x256, local copies, waits for them, and re-layouts, per_device(): window[:, step * variable_count:(step + rows_per_phase) * variable_count]  392 us
    psum x1, waiting for transfers between devices, per_device(): coef = lax.psum(inner(partner, sketch), 'tm')  104 us
    concatenate x1, local copies, waits for them, and re-layouts, per_device(): lagged = jnp.concatenate(slices, 2)[:, :, :row_count]  65.7 us
    another operation x24, other arithmetic, factor_half(): lower = jnp.linalg.cholesky(gram_now)  52.2 us
    another operation x12, other arithmetic, lower_solve(): return jax.scipy.linalg.solve_triangular(lower, block.T, lower=True).T  41.8 us
  transfers between devices with their start and end apart: 7, of which 6 were waited for; matrix products, arithmetic and copies ran while one was open for 27% of the time, Pallas kernels for 0%

commit v1 on v0

v1 whole, which is shorter than its diff:
```python
import functools
import math

import jax
import jax.numpy as jnp
import numpy as np
from jax import lax
from jax.experimental import pallas as pl
from jax.experimental.pallas import tpu as pltpu
from jax.sharding import PartitionSpec as P

WINDOW_LAGS = 256
LAG_SPACING = 8
NB = 128
IB = 16
TILE = 256
HI = lax.Precision.HIGHEST
BOTH = ("tm", "panel")


def dot_nn(a, b):
    return lax.dot_general(a, b, (((1,), (0,)), ((), ())), precision=HI, preferred_element_type=jnp.float32)


def dot_tn(a, b):
    return lax.dot_general(a, b, (((0,), (0,)), ((), ())), precision=HI, preferred_element_type=jnp.float32)


def dot_nt(a, b):
    return lax.dot_general(a, b, (((1,), (1,)), ((), ())), precision=HI, preferred_element_type=jnp.float32)


class Plan:
    def __init__(self, n):
        lo = 1
        while lo * lo < n:
            lo *= 2
        if n % lo or (n // lo) * lo != n:
            lo = n
        if lo * lo > n and n % (lo // 2) == 0:
            lo //= 2
        self.n, self.lo, self.hi = n, lo, n // lo
        self.mixed = self.lo == self.hi
        self.na, self.nb = self.hi, self.lo

    def index(self, a, b, panel):
        straight = a * self.lo + b
        if not self.mixed:
            return straight
        return (1 - panel) * (b * self.lo + a) + panel * straight

    def coords(self, i, panel):
        hi, lo = i // self.lo, i % self.lo
        if not self.mixed:
            return hi, lo
        return (1 - panel) * lo + panel * hi, (1 - panel) * hi + panel * lo

    def pairs(self, da, db):
        out = []
        for i in range(self.n):
            for panel in range(2):
                a, b = self.coords(i, panel)
                j = self.index((a + da) % self.na, (b + db) % self.nb, panel)
                out.append((i * 2 + panel, j * 2 + panel))
        return out

    def plain_pairs(self, dhi, dlo):
        out = []
        for i in range(self.n):
            hi, lo = i // self.lo, i % self.lo
            out.append((i, ((hi + dhi) % self.hi) * self.lo + (lo + dlo) % self.lo))
        return out


def sketch_kernel(plan, rows, depth, *refs):
    na, nb = plan.na, plan.nb
    stacks = refs[: plan.lo]
    omegas = refs[plan.lo : plan.lo + na]
    outs = refs[plan.lo + na : plan.lo + na + nb]
    flat, wide = refs[plan.lo + na + nb :]
    i = lax.axis_index("tm")
    panel = lax.axis_index("panel")
    hi, lo = i // plan.lo, i % plan.lo
    total = plan.n * rows
    variables = stacks[0].shape[1]
    flat[total:, :] = jnp.zeros((flat.shape[0] - total, variables), flat.dtype)
    for slo in range(plan.lo):

        @pl.loop(0, plan.hi)
        def _(shi):
            slab = lax.rem(hi - shi + plan.hi, plan.hi) * plan.lo + lax.rem(lo - slo + plan.lo, plan.lo)
            flat[pl.ds(pl.multiple_of(slab * rows, rows), rows), :] = stacks[slo][
                pl.ds(pl.multiple_of(shi * rows, rows), rows), :
            ]

    step = 256

    @pl.loop(0, wide.shape[0] // step)
    def _(k):
        start = pl.multiple_of(k * step, step)
        now = flat[pl.ds(start, step + 16), :]
        wide[pl.ds(start, step), :] = jnp.concatenate(
            [now[:step], now[LAG_SPACING : LAG_SPACING + step]], 1
        )

    a, b = plan.coords(i, panel)
    shift = depth // variables * LAG_SPACING
    chunk = min(256, depth)
    for sb in range(nb):
        slab = plan.index(a, lax.rem(b + sb, nb), panel)

        @pl.loop(0, rows // TILE)
        def _(k):
            start = pl.multiple_of(k * TILE, TILE)
            acc = jnp.zeros((TILE, outs[0].shape[1]), jnp.float32)
            for sa in range(na):
                block = plan.index(lax.rem(a - sa + na, na), b, panel)
                base = pl.multiple_of(slab * rows + block * shift + start, 16)
                for first in range(0, depth, chunk):
                    pieces = []
                    for col in range(first, first + chunk, 2 * variables):
                        offset = col // variables * LAG_SPACING
                        pieces.append(wide[pl.ds(base + offset, TILE), :])
                    left = jnp.concatenate(pieces, 1) if len(pieces) > 1 else pieces[0]
                    acc = acc + jnp.dot(
                        left, omegas[sa][first : first + chunk, :], preferred_element_type=jnp.float32
                    )
            outs[sb][pl.ds(start, TILE), :] = acc


def gram_kernel(own_ref, other_ref, out_ref):
    own = own_ref[...]
    half = own.shape[1]
    out_ref[:, :half] = dot_tn(own, own)
    panel = lax.axis_index("panel")

    @pl.when(panel == 0)
    def _():
        out_ref[:, half:] = dot_tn(own_ref[...], other_ref[:, : half // 2])

    @pl.when(panel == 1)
    def _():
        out_ref[:, half:] = dot_tn(other_ref[...], own_ref[:, half // 2 :])


def small_factor(block, base, size):
    cols = [jnp.broadcast_to(block[:, base + j : base + j + 1], (size, NB)) for j in range(size)]
    sub = lax.broadcasted_iota(jnp.int32, (size, NB), 0)
    scale = jnp.zeros((size, NB), jnp.float32)
    left, right = block[:, :NB], block[:, NB:]
    for j in range(size):
        pivot = jnp.broadcast_to(cols[j][j : j + 1, :], (size, NB))
        mult = jnp.where(sub > j, cols[j] * (1.0 / pivot), 0.0)
        for k in range(j + 1, size):
            cols[k] = cols[k] - mult * jnp.broadcast_to(cols[j][k : k + 1, :], (size, NB))
        scale = jnp.where(sub == j, pivot, scale)
        if j < size - 1:
            left = left - mult * jnp.broadcast_to(left[j : j + 1, :], (size, NB))
            right = right - mult * jnp.broadcast_to(right[j : j + 1, :], (size, NB))
    inv = lax.rsqrt(scale)
    return jnp.concatenate([left * inv, right * inv], 1)


def diag_factor(w):
    for kb in range(NB // IB):
        end = (kb + 1) * IB
        rows = small_factor(w[kb * IB : end, :], kb * IB, IB)
        w[kb * IB : end, :] = rows
        if end < NB:
            w[end:, :] = w[end:, :] - dot_tn(rows[:, end:NB], rows)


def factor_kernel(factor, gown, gother, sown, sother, basis_ref, tri_ref, a, w, r, v):
    half = gown.shape[0]
    n = 2 * half
    panel = lax.axis_index("panel")

    def place(first, second):
        a[:half, :half] = first[:, :half]
        a[:half, half : half + half // 2] = first[:, half:]
        a[half:, half:] = second[:, :half]
        a[:half, half + half // 2 :] = second[:, half:]

    @pl.when(panel == 0)
    def _():
        place(gown, gother)

    @pl.when(panel == 1)
    def _():
        place(gother, gown)

    r[...] = jnp.zeros_like(r)
    v[...] = jnp.zeros_like(v)
    ri = lax.broadcasted_iota(jnp.int32, (NB, NB), 0)
    ci = lax.broadcasted_iota(jnp.int32, (NB, NB), 1)
    eye = (ri == ci).astype(jnp.float32)
    for j in range(n // NB):
        js = slice(j * NB, (j + 1) * NB)
        w[:, :NB] = a[js, js]
        w[:, NB:] = eye
        diag_factor(w)
        wj = w[:, NB:]
        r[js, js] = jnp.where(ci >= ri, w[:, :NB], 0.0)
        v[js, js] = wj.T
        if (j + 1) * NB < n:
            rest = slice((j + 1) * NB, n)
            row = dot_nn(wj, a[js, rest])
            r[js, rest] = row
            for i in range(j + 1, n // NB):
                at = (i - j - 1) * NB
                a[i * NB : (i + 1) * NB, i * NB :] = a[i * NB : (i + 1) * NB, i * NB :] - dot_tn(
                    row[:, at : at + NB], row[:, at:]
                )
        if j > 0:
            top = slice(0, j * NB)
            v[top, js] = -dot_nt(dot_nn(v[top, top], r[top, js]), wj)

    @pl.when(panel == 0)
    def _():
        tri_ref[...] = r[:, :half] * (1.0 / factor)
        basis_ref[...] = dot_nn(sown[...], v[:half, :half]) * factor

    @pl.when(panel == 1)
    def _():
        tri_ref[...] = r[:, half:] * (1.0 / factor)
        basis_ref[...] = (dot_nn(sother[...], v[:half, half:]) + dot_nn(sown[...], v[half:, half:])) * factor


def vmem(count):
    return [pl.BlockSpec(memory_space=pltpu.VMEM)] * count


def per_device(series, test_matrix):
    n = lax.axis_size("tm")
    plan = Plan(n)
    rows, variables = series.shape
    depth, half = test_matrix.shape
    gathered = [test_matrix]
    for s in range(1, plan.na):
        gathered.append(lax.ppermute(test_matrix, BOTH, plan.pairs(s, 0)))
    pieces = [series]
    for s in range(1, plan.hi):
        pieces.append(lax.ppermute(series, "tm", plan.plain_pairs(s, 0)))
    stack = jnp.concatenate(pieces, 0)
    stacks = [stack]
    for s in range(1, plan.lo):
        stacks.append(lax.ppermute(stack, "tm", plan.plain_pairs(0, s)))
    span = WINDOW_LAGS * LAG_SPACING
    parts = pl.pallas_call(
        functools.partial(sketch_kernel, plan, rows, depth),
        out_shape=[jax.ShapeDtypeStruct((rows, half), jnp.float32)] * plan.nb,
        in_specs=vmem(plan.lo + plan.na),
        out_specs=vmem(plan.nb),
        scratch_shapes=[
            pltpu.VMEM((n * rows + span + 16, variables), jnp.bfloat16),
            pltpu.VMEM((n * rows + span, 2 * variables), jnp.bfloat16),
        ],
        name="sketch",
    )(*stacks, *gathered)
    own = parts[0]
    arrived = [lax.ppermute(parts[s], BOTH, plan.pairs(0, s)) for s in range(1, plan.nb)]
    for piece in arrived:
        own = own + piece
    other = lax.ppermute(own, "panel", [(0, 1), (1, 0)])
    gram = pl.pallas_call(
        gram_kernel,
        out_shape=jax.ShapeDtypeStruct((half, half + half // 2), jnp.float32),
        in_specs=vmem(2),
        out_specs=vmem(1)[0],
        name="gram",
    )(own, other)
    width = half + half // 2
    spread = lax.all_to_all(gram.reshape(n, half // n, width), "tm", 0, 0, tiled=True)
    summed = jnp.sum(spread, 0)
    wide = jnp.broadcast_to(summed[None], (n, half // n, width))
    gram = lax.all_to_all(wide, "tm", 0, 0, tiled=True).reshape(half, width)
    gram_other = lax.ppermute(gram, "panel", [(0, 1), (1, 0)])
    full = 2 * half
    return tuple(
        pl.pallas_call(
            functools.partial(factor_kernel, math.sqrt(n * rows)),
            out_shape=[
                jax.ShapeDtypeStruct((rows, half), jnp.float32),
                jax.ShapeDtypeStruct((full, half), jnp.float32),
            ],
            in_specs=vmem(4),
            out_specs=vmem(2),
            scratch_shapes=[
                pltpu.VMEM((full, full), jnp.float32),
                pltpu.VMEM((NB, 2 * NB), jnp.float32),
                pltpu.VMEM((full, full), jnp.float32),
                pltpu.VMEM((full, full), jnp.float32),
            ],
            name="factor",
        )(gram, gram_other, own, other)
    )


def solution(mesh):
    placed = (P(("grp", "tm"), None), P("tm", "panel"))
    return jax.shard_map(
        per_device,
        mesh=mesh,
        in_specs=placed,
        out_specs=(P(("grp", "tm"), "panel"), P("grp", "panel")),
        check_vma=False,
    )
```

time: 1780 us -> 167 us (0.09); the launches traced: 1750 us -> 167 us
  blocking collectives: 1020 us -> 36.9 us
  local copies, waits for them, and re-layouts: 479 us -> 5.08 us
  other arithmetic: 97.9 us -> 1.31 us
  waiting for transfers between devices: 116 us -> 60.7 us
  Pallas kernels: 0 us -> 40.7 us
  matrix products: 23.4 us -> 0 us
    psum x14 -> x0, blocking collectives: 1020 us -> none  [the longest x8 585 us: total_gram(): return lax.psum(inner(block, block), 'tm')]
    reshape x258 -> x0, local copies, waits for them, and re-layouts: 393 us -> none  [the longest x256 392 us: per_device(): window[:, step * variable_count:(step + rows_per_phase) * variable_count]]
    psum x1 -> x0, waiting for transfers between devices: 104 us -> none  [per_device(): coef = lax.psum(inner(partner, sketch), 'tm')]
    another operation x36 -> x0, other arithmetic: 93.9 us -> none  [the longest x24 52.2 us: factor_half(): lower = jnp.linalg.cholesky(gram_now)]
    concatenate x3 -> x0, local copies, waits for them, and re-layouts: 66 us -> none  [the longest x1 65.7 us: per_device(): lagged = jnp.concatenate(slices, 2)[:, :, :row_count]]
    ppermute x5 -> x14, waiting for transfers between devices: 11.4 us -> 60.7 us  [the longest x3 29.8 us: per_device(): stacks.append(lax.ppermute(stack, 'tm', plan.plain_pairs(0, s)))]
    pallas_call x0 -> x3, Pallas kernels: none -> 40.7 us  [the longest x1 24.1 us: per_device(): pl.pallas_call(functools.partial(factor_kernel, math.sqrt(n * rows)), out...]
    all_to_all x0 -> x2, blocking collectives: none -> 36.9 us  [the longest x1 21.4 us: per_device(): lax.all_to_all(gram.reshape(n, half // n, width), 'tm', 0, 0, tiled=True)]
  transfers between devices with their start and end apart: 7 -> 14, of which waited for: 6 -> 8; matrix products, arithmetic and copies ran while one was open for 27% -> 0% of each run, Pallas kernels for 0% -> 0%
where the time goes in v1:
time: 167 us
  waiting for transfers between devices  60.7 us (36%)
  Pallas kernels  40.7 us (24%)
  blocking collectives  36.9 us (22%)
  starting transfers between devices  21.3 us (13%)
  local copies, waits for them, and re-layouts  5.08 us (3%)
    ppermute x3, waiting for transfers between devices, per_device(): stacks.append(lax.ppermute(stack, 'tm', plan.plain_pairs(0, s)))  29.8 us
    pallas_call x1, Pallas kernels, per_device(): pl.pallas_call(functools.partial(factor_kernel, math.sqrt(n * rows)), out...  24.1 us
    all_to_all x1, blocking collectives, per_device(): lax.all_to_all(gram.reshape(n, half // n, width), 'tm', 0, 0, tiled=True)  21.4 us
    ppermute x3, waiting for transfers between devices, per_device(): lax.ppermute(parts[s], BOTH, plan.pairs(0, s))  17.1 us
    all_to_all x1, blocking collectives, per_device(): gram = lax.all_to_all(wide, 'tm', 0, 0, tiled=True).reshape(half, width)  15.5 us
    pallas_call x1, Pallas kernels, per_device(): pl.pallas_call(functools.partial(sketch_kernel, plan, rows, depth), out_s...  13.2 us
    ppermute x3, waiting for transfers between devices, per_device(): pieces.append(lax.ppermute(series, 'tm', plan.plain_pairs(s, 0)))  10.2 us
    ppermute x3, starting transfers between devices, per_device(): stacks.append(lax.ppermute(stack, 'tm', plan.plain_pairs(0, s)))  6.5 us
  transfers between devices with their start and end apart: 14, of which 8 were waited for; matrix products, arithmetic and copies ran while one was open for 0% of the time, Pallas kernels for 0%

profile of v1, /device:TPU:0, one launch (start us, length us, event | category | flops | bytes accessed | tf_op | source)
XLA Modules:
  0.0 166.8 jit_solution(172670726067391740)
XLA Ops:
  0.6 1.0 copy.7
  1.6 0.0 copy-start.4
  1.6 5.1 %collective-permute-start.2 = (bf16[512,64]{1,0:T(8,128)(2,1)S(1)}, bf16[512,64]{1,0:T(8,128)(2,1)S(1)}, u32[]{:S(2)}, u32[]{:S(2)}) collective-permute-start(bf16[512,64]{1,0:T(8,128)(2,1)S(1)} %copy.7), channel_id=1, source_target_pairs={{0,24},{2,26},{4,28},{6,30},{8,0},{10,2},{12,4},{14,6},{16,8},{18,... | collective-permute-start | bytes 196616 | tf_op jit(solution)/shard_map/ppermute | solution.py:243
  6.7 0.0 collective-permute-start.1
  6.7 1.0 collective-permute-start
  7.7 2.9 %collective-permute-done.2 = bf16[512,64]{1,0:T(8,128)(2,1)S(1)} collective-permute-done((bf16[512,64]{1,0:T(8,128)(2,1)S(1)}, bf16[512,64]{1,0:T(8,128)(2,1)S(1)}, u32[]{:S(2)}, u32[]{:S(2)}) %collective-permute-start.2) | collective-permute-done | bytes 65568 | tf_op jit(solution)/shard_map/ppermute | solution.py:243
  10.6 7.3 %collective-permute-done.1 = bf16[512,64]{1,0:T(8,128)(2,1)S(1)} collective-permute-done((bf16[512,64]{1,0:T(8,128)(2,1)S(1)}, bf16[512,64]{1,0:T(8,128)(2,1)S(1)}, u32[]{:S(2)}, u32[]{:S(2)}) %collective-permute-start.1) | collective-permute-done | bytes 65568 | tf_op jit(solution)/shard_map/ppermute | solution.py:243
  17.9 0.0 collective-permute-done
  18.0 0.1 pad_maximum_fusion.refs_0_
  18.1 0.0 copy-start.2
  18.1 2.5 %collective-permute-start.5 = (bf16[2048,64]{1,0:T(8,128)(2,1)S(1)}, bf16[2048,64]{1,0:T(8,128)(2,1)S(1)}, u32[]{:S(2)}, u32[]{:S(2)}) collective-permute-start(bf16[2048,64]{1,0:T(8,128)(2,1)S(1)} %pad_maximum_fusion.refs_0_), channel_id=1, source_target_pairs={{0,6},{2,0},{4,2},{6,4},{8,14},{10,8},{12,10},{14,12},{16,22},{18,... | collective-permute-start | bytes 786440 | tf_op jit(solution)/shard_map/ppermute | solution.py:247
  20.6 0.0 copy-done.4
  20.6 0.5 collective-permute-start.7
  21.1 0.6 collective-permute-start.6
  21.7 2.3 %collective-permute-start.8 = (bf16[1024,256]{1,0:T(8,128)(2,1)S(1)}, bf16[1024,256]{1,0:T(8,128)(2,1)S(1)}, u32[]{:S(2)}, u32[]{:S(2)}) collective-permute-start(bf16[1024,256]{1,0:T(8,128)(2,1)S(1)} %copy-done.4), channel_id=1, source_target_pairs={{0,6},{1,25},{2,0},{3,27},{4,2},{5,29},{6,4},{7,31},{8,14},{9,1},{... | collective-permute-start | bytes 1572872 | tf_op jit(solution)/shard_map/ppermute | solution.py:240
  24.0 1.5 collective-permute-start.4
  25.5 5.8 %collective-permute-done.5.refs_3_ = bf16[2048,64]{1,0:T(8,128)(2,1)S(1)} collective-permute-done((bf16[2048,64]{1,0:T(8,128)(2,1)S(1)}, bf16[2048,64]{1,0:T(8,128)(2,1)S(1)}, u32[]{:S(2)}, u32[]{:S(2)}) %collective-permute-start.5) | collective-permute-done | bytes 262176 | tf_op jit(solution)/shard_map/ppermute | solution.py:247
  31.4 2.5 %collective-permute-start.3 = (bf16[2048,64]{1,0:T(8,128)(2,1)S(1)}, bf16[2048,64]{1,0:T(8,128)(2,1)S(1)}, u32[]{:S(2)}, u32[]{:S(2)}) collective-permute-start(bf16[2048,64]{1,0:T(8,128)(2,1)S(1)} %pad_maximum_fusion.refs_0_), channel_id=1, source_target_pairs={{0,2},{2,4},{4,6},{6,0},{8,10},{10,12},{12,14},{14,8},{16,18},{18,... | collective-permute-start | bytes 786440 | tf_op jit(solution)/shard_map/ppermute | solution.py:247
  33.9 24.0 %collective-permute-done.4.refs_2_ = bf16[2048,64]{1,0:T(8,128)(2,1)S(1)} collective-permute-done((bf16[2048,64]{1,0:T(8,128)(2,1)S(1)}, bf16[2048,64]{1,0:T(8,128)(2,1)S(1)}, u32[]{:S(2)}, u32[]{:S(2)}) %collective-permute-start.4) | collective-permute-done | bytes 262176 | tf_op jit(solution)/shard_map/ppermute | solution.py:247
  57.8 0.0 collective-permute-done.3.refs_1_
  57.9 0.0 collective-permute-done.7.refs_6_
  57.9 0.0 copy-start.6
  57.9 0.0 collective-permute-done.6.refs_5_
  57.9 0.8 copy-done.9
  58.7 0.2 copy-done.10
  58.8 0.0 collective-permute-done.8.refs_7_
  58.8 0.2 copy-done.6
  59.0 0.6 copy-done.7
  59.6 0.8 copy-done.8
  60.4 13.2 %sketch.1 = (f32[512,256]{1,0:T(8,128)}, f32[512,256]{1,0:T(8,128)}, f32[512,256]{1,0:T(8,128)}, f32[512,256]{1,0:T(8,128)}) custom-call(bf16[2048,64]{1,0:T(8,128)(2,1)} %copy-done.2, bf16[2048,64]{1,0:T(8,128)(2,1)} %copy-done.10, bf16[2048,64]{1,0:T(8,128)(2,1)} %copy-done.9, bf16[2048,64]{1,0:T(8,128)(2,1)} %copy-done.5, bf16[1024,256]{1,0:T(8,128)(2,1)} %refs_4_.1, ...), custom_call_target="tpu_custom_call" | custom-call | tf_op jit(solution)/shard_map/sketch/pallas_call | solution.py:249
  73.6 0.7 collective-permute-start.9
  74.3 1.6 collective-permute-start.10
  75.9 2.9 %collective-permute-start.11 = (f32[512,256]{1,0:T(8,128)}, f32[512,256]{1,0:T(8,128)S(1)}, u32[]{:S(2)}, u32[]{:S(2)}) collective-permute-start(f32[512,256]{1,0:T(8,128)} %get-tuple-element.9), channel_id=1, source_target_pairs={{0,24},{1,7},{2,26},{3,1},{4,28},{5,3},{6,30},{7,5},{8,0},{9,15},{... | collective-permute-start | bytes 1572872 | tf_op jit(solution)/shard_map/ppermute | solution.py:261
  78.8 6.2 %collective-permute-done.9 = f32[512,256]{1,0:T(8,128)S(1)} collective-permute-done((f32[512,256]{1,0:T(8,128)}, f32[512,256]{1,0:T(8,128)S(1)}, u32[]{:S(2)}, u32[]{:S(2)}) %collective-permute-start.9) | collective-permute-done | bytes 524320 | tf_op jit(solution)/shard_map/ppermute | solution.py:261
  85.0 10.9 %collective-permute-done.10 = f32[512,256]{1,0:T(8,128)S(1)} collective-permute-done((f32[512,256]{1,0:T(8,128)}, f32[512,256]{1,0:T(8,128)S(1)}, u32[]{:S(2)}, u32[]{:S(2)}) %collective-permute-start.10) | collective-permute-done | bytes 524320 | tf_op jit(solution)/shard_map/ppermute | solution.py:261
  95.9 0.0 collective-permute-done.11
  95.9 1.2 add_add_fusion.own_ref.sown
  97.1 0.1 collective-permute-start.12
  97.1 1.9 %collective-permute-done.12.other_ref.sother = f32[512,256]{1,0:T(8,128)S(1)} collective-permute-done((f32[512,256]{1,0:T(8,128)S(1)}, f32[512,256]{1,0:T(8,128)S(1)}, u32[]{:S(2)}, u32[]{:S(2)}) %collective-permute-start.12) | collective-permute-done | bytes 524320 | tf_op jit(solution)/shard_map/ppermute | solution.py:264
  99.0 0.0 copy-done
  99.0 0.8 copy-done.1
  99.9 3.4 %gram.1 = f32[256,384]{1,0:T(8,128)} custom-call(f32[512,256]{1,0:T(8,128)} %copy-done, f32[512,256]{1,0:T(8,128)} %copy-done.1), custom_call_target="tpu_custom_call" | custom-call | tf_op jit(solution)/shard_map/gram/pallas_call | solution.py:265
  103.2 21.4 %all_to_all.10 = f32[16,16,384]{2,1,0:T(8,128)S(1)} all-to-all(f32[16,16,384]{2,1,0:T(8,128)} %bitcast.4), channel_id=1, replica_groups=mesh['grp'=1,'tm'=16,'panel'=2] {'tm'}, dimensions={0} | all-to-all | bytes 786432 | tf_op jit(solution)/shard_map/all_to_all | solution.py:273
  124.7 15.5 %all_to_all.11 = f32[16,16,384]{2,1,0:T(8,128)S(1)} all-to-all(f32[16,16,384]{2,1,0:T(8,128)S(1)} %broadcast_in_dim.2), channel_id=1, replica_groups=mesh['grp'=1,'tm'=16,'panel'=2] {'tm'}, dimensions={0} | all-to-all | bytes 786432 | tf_op jit(solution)/shard_map/all_to_all | solution.py:276
  140.2 0.0 collective-permute-start.13
  140.2 1.7 %collective-permute-done.13.gother = f32[256,384]{1,0:T(8,128)S(1)} collective-permute-done((f32[256,384]{1,0:T(8,128)S(1)}, f32[256,384]{1,0:T(8,128)S(1)}, u32[]{:S(2)}, u32[]{:S(2)}) %collective-permute-start.13) | collective-permute-done | bytes 393248 | tf_op jit(solution)/shard_map/ppermute | solution.py:277
  141.9 0.8 copy-done.11
  142.7 24.1 %factor.1 = (f32[512,256]{1,0:T(8,128)}, f32[512,256]{1,0:T(8,128)}) custom-call(f32[256,384]{1,0:T(8,128)} %bitcast.3, f32[256,384]{1,0:T(8,128)} %copy-done.11, f32[512,256]{1,0:T(8,128)} %copy-done, f32[512,256]{1,0:T(8,128)} %copy-done.1), custom_call_target="tpu_custom_call" | custom-call | tf_op jit(solution)/shard_map/factor/pallas_call | solution.py:280
  (14 shorter events, 0.1 us)
Async XLA Ops:
  1.6 19.0 %copy-start.4 = (bf16[1024,256]{1,0:T(8,128)(2,1)S(1)}, bf16[1024,256]{1,0:T(8,128)(2,1)}, u32[]{:S(2)}) copy-start(bf16[1024,256]{1,0:T(8,128)(2,1)} %refs_4_.1) | copy-start | bytes 1572868
  1.6 9.0 %collective-permute-start.2 = (bf16[512,64]{1,0:T(8,128)(2,1)S(1)}, bf16[512,64]{1,0:T(8,128)(2,1)S(1)}, u32[]{:S(2)}, u32[]{:S(2)}) collective-permute-start(bf16[512,64]{1,0:T(8,128)(2,1)S(1)} %copy.7), channel_id=1, source_target_pairs={{0,24},{2,26},{4,28},{6,30},{8,0},{10,2},{12,4},{14,6},{16,8},{18,... | collective-permute-start | bytes 196616 | tf_op jit(solution)/shard_map/ppermute | solution.py:243
  6.7 11.2 %collective-permute-start.1 = (bf16[512,64]{1,0:T(8,128)(2,1)S(1)}, bf16[512,64]{1,0:T(8,128)(2,1)S(1)}, u32[]{:S(2)}, u32[]{:S(2)}) collective-permute-start(bf16[512,64]{1,0:T(8,128)(2,1)S(1)} %copy.7), channel_id=1, source_target_pairs={{0,16},{2,18},{4,20},{6,22},{8,24},{10,26},{12,28},{14,30},{16,0},... | collective-permute-start | bytes 196616 | tf_op jit(solution)/shard_map/ppermute | solution.py:243
  6.7 11.2 %collective-permute-start = (bf16[512,64]{1,0:T(8,128)(2,1)S(1)}, bf16[512,64]{1,0:T(8,128)(2,1)S(1)}, u32[]{:S(2)}, u32[]{:S(2)}) collective-permute-start(bf16[512,64]{1,0:T(8,128)(2,1)S(1)} %copy.7), channel_id=1, source_target_pairs={{0,8},{2,10},{4,12},{6,14},{8,16},{10,18},{12,20},{14,22},{16,24},... | collective-permute-start | bytes 196616 | tf_op jit(solution)/shard_map/ppermute | solution.py:243
  18.1 40.8 %copy-start.2 = (bf16[2048,64]{1,0:T(8,128)(2,1)}, bf16[2048,64]{1,0:T(8,128)(2,1)S(1)}, u32[]{:S(2)}) copy-start(bf16[2048,64]{1,0:T(8,128)(2,1)S(1)} %pad_maximum_fusion.refs_0_) | copy-start | bytes 786436
  18.1 13.3 %collective-permute-start.5 = (bf16[2048,64]{1,0:T(8,128)(2,1)S(1)}, bf16[2048,64]{1,0:T(8,128)(2,1)S(1)}, u32[]{:S(2)}, u32[]{:S(2)}) collective-permute-start(bf16[2048,64]{1,0:T(8,128)(2,1)S(1)} %pad_maximum_fusion.refs_0_), channel_id=1, source_target_pairs={{0,6},{2,0},{4,2},{6,4},{8,14},{10,8},{12,10},{14,12},{16,22},{18,... | collective-permute-start | bytes 786440 | tf_op jit(solution)/shard_map/ppermute | solution.py:247
  20.6 37.3 %collective-permute-start.7 = (bf16[1024,256]{1,0:T(8,128)(2,1)S(1)}, bf16[1024,256]{1,0:T(8,128)(2,1)S(1)}, u32[]{:S(2)}, u32[]{:S(2)}) collective-permute-start(bf16[1024,256]{1,0:T(8,128)(2,1)S(1)} %copy-done.4), channel_id=1, source_target_pairs={{0,4},{1,17},{2,6},{3,19},{4,0},{5,21},{6,2},{7,23},{8,12},{9,25},... | collective-permute-start | bytes 1572872 | tf_op jit(solution)/shard_map/ppermute | solution.py:240
  21.1 36.8 %collective-permute-start.6 = (bf16[1024,256]{1,0:T(8,128)(2,1)S(1)}, bf16[1024,256]{1,0:T(8,128)(2,1)S(1)}, u32[]{:S(2)}, u32[]{:S(2)}) collective-permute-start(bf16[1024,256]{1,0:T(8,128)(2,1)S(1)} %copy-done.4), channel_id=1, source_target_pairs={{0,2},{1,9},{2,4},{3,11},{4,6},{5,13},{6,0},{7,15},{8,10},{9,17},{... | collective-permute-start | bytes 1572872 | tf_op jit(solution)/shard_map/ppermute | solution.py:240
  21.7 37.1 %collective-permute-start.8 = (bf16[1024,256]{1,0:T(8,128)(2,1)S(1)}, bf16[1024,256]{1,0:T(8,128)(2,1)S(1)}, u32[]{:S(2)}, u32[]{:S(2)}) collective-permute-start(bf16[1024,256]{1,0:T(8,128)(2,1)S(1)} %copy-done.4), channel_id=1, source_target_pairs={{0,6},{1,25},{2,0},{3,27},{4,2},{5,29},{6,4},{7,31},{8,14},{9,1},{... | collective-permute-start | bytes 1572872 | tf_op jit(solution)/shard_map/ppermute | solution.py:240
  24.0 33.8 %collective-permute-start.4 = (bf16[2048,64]{1,0:T(8,128)(2,1)S(1)}, bf16[2048,64]{1,0:T(8,128)(2,1)S(1)}, u32[]{:S(2)}, u32[]{:S(2)}) collective-permute-start(bf16[2048,64]{1,0:T(8,128)(2,1)S(1)} %pad_maximum_fusion.refs_0_), channel_id=1, source_target_pairs={{0,4},{2,6},{4,0},{6,2},{8,12},{10,14},{12,8},{14,10},{16,20},{18,... | collective-permute-start | bytes 786440 | tf_op jit(solution)/shard_map/ppermute | solution.py:247
  31.4 27.4 %copy-start.5 = (bf16[2048,64]{1,0:T(8,128)(2,1)}, bf16[2048,64]{1,0:T(8,128)(2,1)S(1)}, u32[]{:S(2)}) copy-start(bf16[2048,64]{1,0:T(8,128)(2,1)S(1)} %collective-permute-done.5.refs_3_) | copy-start | bytes 786436
  31.4 26.5 %collective-permute-start.3 = (bf16[2048,64]{1,0:T(8,128)(2,1)S(1)}, bf16[2048,64]{1,0:T(8,128)(2,1)S(1)}, u32[]{:S(2)}, u32[]{:S(2)}) collective-permute-start(bf16[2048,64]{1,0:T(8,128)(2,1)S(1)} %pad_maximum_fusion.refs_0_), channel_id=1, source_target_pairs={{0,2},{2,4},{4,6},{6,0},{8,10},{10,12},{12,14},{14,8},{16,18},{18,... | collective-permute-start | bytes 786440 | tf_op jit(solution)/shard_map/ppermute | solution.py:247
  57.8 0.8 copy-start.9
  57.9 1.0 copy-start.10
  57.9 1.1 copy-start.6
  58.8 0.8 copy-start.7
  59.6 0.8 copy-start.8
  73.6 11.4 %collective-permute-start.9 = (f32[512,256]{1,0:T(8,128)}, f32[512,256]{1,0:T(8,128)S(1)}, u32[]{:S(2)}, u32[]{:S(2)}) collective-permute-start(f32[512,256]{1,0:T(8,128)} %get-tuple-element.7), channel_id=1, source_target_pairs={{0,8},{1,3},{2,10},{3,5},{4,12},{5,7},{6,14},{7,1},{8,16},{9,11},{... | collective-permute-start | bytes 1572872 | tf_op jit(solution)/shard_map/ppermute | solution.py:261
  74.3 21.6 %collective-permute-start.10 = (f32[512,256]{1,0:T(8,128)}, f32[512,256]{1,0:T(8,128)S(1)}, u32[]{:S(2)}, u32[]{:S(2)}) collective-permute-start(f32[512,256]{1,0:T(8,128)} %get-tuple-element.8), channel_id=1, source_target_pairs={{0,16},{1,5},{2,18},{3,7},{4,20},{5,1},{6,22},{7,3},{8,24},{9,13},... | collective-permute-start | bytes 1572872 | tf_op jit(solution)/shard_map/ppermute | solution.py:261
  75.9 20.0 %collective-permute-start.11 = (f32[512,256]{1,0:T(8,128)}, f32[512,256]{1,0:T(8,128)S(1)}, u32[]{:S(2)}, u32[]{:S(2)}) collective-permute-start(f32[512,256]{1,0:T(8,128)} %get-tuple-element.9), channel_id=1, source_target_pairs={{0,24},{1,7},{2,26},{3,1},{4,28},{5,3},{6,30},{7,5},{8,0},{9,15},{... | collective-permute-start | bytes 1572872 | tf_op jit(solution)/shard_map/ppermute | solution.py:261
  97.1 2.0 %copy-start = (f32[512,256]{1,0:T(8,128)}, f32[512,256]{1,0:T(8,128)S(1)}, u32[]{:S(2)}) copy-start(f32[512,256]{1,0:T(8,128)S(1)} %add_add_fusion.own_ref.sown) | copy-start | bytes 1572868
  97.1 2.0 %collective-permute-start.12 = (f32[512,256]{1,0:T(8,128)S(1)}, f32[512,256]{1,0:T(8,128)S(1)}, u32[]{:S(2)}, u32[]{:S(2)}) collective-permute-start(f32[512,256]{1,0:T(8,128)S(1)} %add_add_fusion.own_ref.sown), channel_id=1, source_target_pairs={{0,1},{1,0},{2,3},{3,2},{4,5},{5,4},{6,7},{7,6},{8,9},{9,8},{10,11... | collective-permute-start | bytes 1572872 | tf_op jit(solution)/shard_map/ppermute | solution.py:264
  99.0 0.8 copy-start.1
  140.2 1.7 %copy-start.3 = (f32[16,16,384]{2,1,0:T(8,128)}, f32[16,16,384]{2,1,0:T(8,128)S(1)}, u32[]{:S(2)}) copy-start(f32[16,16,384]{2,1,0:T(8,128)S(1)} %all_to_all.11) | copy-start | bytes 1179652
  140.2 1.7 %collective-permute-start.13 = (f32[256,384]{1,0:T(8,128)S(1)}, f32[256,384]{1,0:T(8,128)S(1)}, u32[]{:S(2)}, u32[]{:S(2)}) collective-permute-start(f32[256,384]{1,0:T(8,128)S(1)} %bitcast.2), channel_id=1, source_target_pairs={{0,1},{1,0},{2,3},{3,2},{4,5},{5,4},{6,7},{7,6},{8,9},{9,8},{10,11... | collective-permute-start | bytes 1179656 | tf_op jit(solution)/shard_map/ppermute | solution.py:277
  141.9 0.8 copy-start.11

commit v2 on v1

--- a/solution.py
+++ b/solution.py
@@ -32,13 +32,10 @@
 
 class Plan:
     def __init__(self, n):
+        assert n & (n - 1) == 0
         lo = 1
-        while lo * lo < n:
+        while lo * lo * 4 <= n:
             lo *= 2
-        if n % lo or (n // lo) * lo != n:
-            lo = n
-        if lo * lo > n and n % (lo // 2) == 0:
-            lo //= 2
         self.n, self.lo, self.hi = n, lo, n // lo
         self.mixed = self.lo == self.hi
         self.na, self.nb = self.hi, self.lo
@@ -60,26 +57,41 @@
         for i in range(self.n):
             for panel in range(2):
                 a, b = self.coords(i, panel)
-                j = self.index((a + da) % self.na, (b + db) % self.nb, panel)
-                out.append((i * 2 + panel, j * 2 + panel))
+                out.append((i * 2 + panel, self.index(a ^ da, b ^ db, panel) * 2 + panel))
         return out
 
     def plain_pairs(self, dhi, dlo):
-        out = []
-        for i in range(self.n):
-            hi, lo = i // self.lo, i % self.lo
-            out.append((i, ((hi + dhi) % self.hi) * self.lo + (lo + dlo) % self.lo))
-        return out
-
-
-def sketch_kernel(plan, rows, depth, *refs):
-    na, nb = plan.na, plan.nb
+        return [(i, (i // self.lo ^ dhi) * self.lo + (i % self.lo ^ dlo)) for i in range(self.n)]
+
+
+def gather_blocks(plan, block):
+    depth = block.shape[0]
+
+    def sent(value, da):
+        return lax.ppermute(value, BOTH, plan.pairs(da, 0))
+
+    if plan.na != 4:
+        arrays = [block] + [sent(block, s) for s in range(1, plan.na)]
+        return arrays, [[(s, 0, depth)] for s in range(plan.na)]
+    cut = depth // 2
+    top, bottom = block[:cut], block[cut:]
+    top_one, bottom_two = sent(top, 1), sent(bottom, 2)
+    top_pair = sent(jnp.concatenate([top, top_one], 0), 2)
+    bottom_pair = sent(jnp.concatenate([bottom, bottom_two], 0), 1)
+    arrays = [block, top_one, bottom_two, top_pair, bottom_pair]
+    where = [
+        [(0, 0, depth)],
+        [(1, 0, cut), (4, 0, cut)],
+        [(3, 0, cut), (2, 0, cut)],
+        [(3, cut, cut), (4, cut, cut)],
+    ]
+    return arrays, where
+
+
+def widen_kernel(plan, rows, *refs):
     stacks = refs[: plan.lo]
-    omegas = refs[plan.lo : plan.lo + na]
-    outs = refs[plan.lo + na : plan.lo + na + nb]
-    flat, wide = refs[plan.lo + na + nb :]
+    wide, flat = refs[plan.lo :]
     i = lax.axis_index("tm")
-    panel = lax.axis_index("panel")
     hi, lo = i // plan.lo, i % plan.lo
     total = plan.n * rows
     variables = stacks[0].shape[1]
@@ -88,7 +100,7 @@
 
         @pl.loop(0, plan.hi)
         def _(shi):
-            slab = lax.rem(hi - shi + plan.hi, plan.hi) * plan.lo + lax.rem(lo - slo + plan.lo, plan.lo)
+            slab = (hi ^ shi) * plan.lo + (lo ^ slo)
             flat[pl.ds(pl.multiple_of(slab * rows, rows), rows), :] = stacks[slo][
                 pl.ds(pl.multiple_of(shi * rows, rows), rows), :
             ]
@@ -103,29 +115,35 @@
             [now[:step], now[LAG_SPACING : LAG_SPACING + step]], 1
         )
 
+
+def sketch_kernel(plan, rows, depth, variables, where, sb, wide, *refs):
+    blocks, out = refs[:-1], refs[-1]
+    i = lax.axis_index("tm")
+    panel = lax.axis_index("panel")
     a, b = plan.coords(i, panel)
     shift = depth // variables * LAG_SPACING
-    chunk = min(256, depth)
-    for sb in range(nb):
-        slab = plan.index(a, lax.rem(b + sb, nb), panel)
-
-        @pl.loop(0, rows // TILE)
-        def _(k):
-            start = pl.multiple_of(k * TILE, TILE)
-            acc = jnp.zeros((TILE, outs[0].shape[1]), jnp.float32)
-            for sa in range(na):
-                block = plan.index(lax.rem(a - sa + na, na), b, panel)
-                base = pl.multiple_of(slab * rows + block * shift + start, 16)
-                for first in range(0, depth, chunk):
+    slab = plan.index(a, b ^ sb, panel)
+
+    @pl.loop(0, rows // TILE)
+    def _(k):
+        start = pl.multiple_of(k * TILE, TILE)
+        acc = jnp.zeros((TILE, out.shape[1]), jnp.float32)
+        for sa in range(plan.na):
+            block = plan.index(a ^ sa, b, panel)
+            base = pl.multiple_of(slab * rows + block * shift + start, 16)
+            past = 0
+            for array, row, count in where[sa]:
+                chunk = min(256, count)
+                for first in range(0, count, chunk):
                     pieces = []
-                    for col in range(first, first + chunk, 2 * variables):
+                    for col in range(past + first, past + first + chunk, 2 * variables):
                         offset = col // variables * LAG_SPACING
                         pieces.append(wide[pl.ds(base + offset, TILE), :])
                     left = jnp.concatenate(pieces, 1) if len(pieces) > 1 else pieces[0]
-                    acc = acc + jnp.dot(
-                        left, omegas[sa][first : first + chunk, :], preferred_element_type=jnp.float32
-                    )
-            outs[sb][pl.ds(start, TILE), :] = acc
+                    right = blocks[array][row + first : row + first + chunk, :]
+                    acc = acc + jnp.dot(left, right, preferred_element_type=jnp.float32)
+                past += count
+        out[pl.ds(start, TILE), :] = acc
 
 
 def gram_kernel(own_ref, other_ref, out_ref):
@@ -235,9 +253,7 @@
     plan = Plan(n)
     rows, variables = series.shape
     depth, half = test_matrix.shape
-    gathered = [test_matrix]
-    for s in range(1, plan.na):
-        gathered.append(lax.ppermute(test_matrix, BOTH, plan.pairs(s, 0)))
+    arrays, where = gather_blocks(plan, test_matrix)
     pieces = [series]
     for s in range(1, plan.hi):
         pieces.append(lax.ppermute(series, "tm", plan.plain_pairs(s, 0)))
@@ -245,20 +261,27 @@
     stacks = [stack]
     for s in range(1, plan.lo):
         stacks.append(lax.ppermute(stack, "tm", plan.plain_pairs(0, s)))
-    span = WINDOW_LAGS * LAG_SPACING
-    parts = pl.pallas_call(
-        functools.partial(sketch_kernel, plan, rows, depth),
-        out_shape=[jax.ShapeDtypeStruct((rows, half), jnp.float32)] * plan.nb,
-        in_specs=vmem(plan.lo + plan.na),
-        out_specs=vmem(plan.nb),
-        scratch_shapes=[
-            pltpu.VMEM((n * rows + span + 16, variables), jnp.bfloat16),
-            pltpu.VMEM((n * rows + span, 2 * variables), jnp.bfloat16),
-        ],
-        name="sketch",
-    )(*stacks, *gathered)
-    own = parts[0]
-    arrived = [lax.ppermute(parts[s], BOTH, plan.pairs(0, s)) for s in range(1, plan.nb)]
+    length = n * rows + WINDOW_LAGS * LAG_SPACING
+    wide = pl.pallas_call(
+        functools.partial(widen_kernel, plan, rows),
+        out_shape=jax.ShapeDtypeStruct((length, 2 * variables), jnp.bfloat16),
+        in_specs=vmem(plan.lo),
+        out_specs=vmem(1)[0],
+        scratch_shapes=[pltpu.VMEM((length + 16, variables), jnp.bfloat16)],
+        name="widen",
+    )(*stacks)
+
+    def part(sb):
+        return pl.pallas_call(
+            functools.partial(sketch_kernel, plan, rows, depth, variables, where, sb),
+            out_shape=jax.ShapeDtypeStruct((rows, half), jnp.float32),
+            in_specs=vmem(1 + len(arrays)),
+            out_specs=vmem(1)[0],
+            name="sketch%d" % sb,
+        )(wide, *arrays)
+
+    arrived = [lax.ppermute(part(s), BOTH, plan.pairs(0, s)) for s in reversed(range(1, plan.nb))]
+    own = part(0)
     for piece in arrived:
         own = own + piece
     other = lax.ppermute(own, "panel", [(0, 1), (1, 0)])

time: 167 us -> 165 us (0.988)
  Pallas kernels: 40.7 us -> 52.7 us
  waiting for transfers between devices: 60.7 us -> 50.7 us
  blocking collectives: 36.9 us -> 33.3 us
  starting transfers between devices: 21.3 us -> 18 us
  other arithmetic: 1.31 us -> 3.14 us
    pallas_call x1 -> x5, Pallas kernels: 13.2 us -> 25.2 us  [the longest x4 18.2 us: part(): pl.pallas_call(functools.partial(sketch_kernel, plan, rows, depth, variab...]
    ppermute x6 -> x7, waiting for transfers between devices: 17.1 us -> 8.45 us  [the longest x3 8.44 us: per_device(): lax.ppermute(part(s), BOTH, plan.pairs(0, s))]
    ppermute x3, waiting for transfers between devices: 29.8 us -> 22.7 us  [per_device(): stacks.append(lax.ppermute(stack, 'tm', plan.plain_pairs(0, s)))]
    ppermute x3, waiting for transfers between devices: 10.2 us -> 15.9 us  [per_device(): pieces.append(lax.ppermute(series, 'tm', plan.plain_pairs(s, 0)))]
    all_to_all x1, blocking collectives: 21.4 us -> 17.8 us  [per_device(): lax.all_to_all(gram.reshape(n, half // n, width), 'tm', 0, 0, tiled=True)]
    ppermute x3, starting transfers between devices: 6.5 us -> 3.55 us  [per_device(): stacks.append(lax.ppermute(stack, 'tm', plan.plain_pairs(0, s)))]
    concatenate x0 -> x2, other arithmetic: none -> 1.83 us  [the longest x1 0.94 us: gather_blocks(): bottom_pair = sent(jnp.concatenate([bottom, bottom_two], 0), 1)]
    ppermute x3, starting transfers between devices: 6.14 us -> 4.45 us  [per_device(): pieces.append(lax.ppermute(series, 'tm', plan.plain_pairs(s, 0)))]
  transfers between devices with their start and end apart: 14 -> 15, of which waited for: 8 -> 9; matrix products, arithmetic and copies ran while one was open for 0% -> 2% of each run, Pallas kernels for 0% -> 13%
where the time goes in v2:
time: 165 us; the launch traced here: 164 us
  Pallas kernels  52.7 us (32%)
  waiting for transfers between devices  50.7 us (31%)
  blocking collectives  33.3 us (20%)
  starting transfers between devices  18 us (11%)
  local copies, waits for them, and re-layouts  5.83 us (4%)
  other arithmetic  3.14 us (2%)
    pallas_call x1, Pallas kernels, per_device(): pl.pallas_call(functools.partial(factor_kernel, math.sqrt(n * rows)), out...  24.1 us
    ppermute x3, waiting for transfers between devices, per_device(): stacks.append(lax.ppermute(stack, 'tm', plan.plain_pairs(0, s)))  22.7 us
    pallas_call x4, Pallas kernels, part(): pl.pallas_call(functools.partial(sketch_kernel, plan, rows, depth, variab...  18.2 us
    all_to_all x1, blocking collectives, per_device(): lax.all_to_all(gram.reshape(n, half // n, width), 'tm', 0, 0, tiled=True)  17.8 us
    ppermute x3, waiting for transfers between devices, per_device(): pieces.append(lax.ppermute(series, 'tm', plan.plain_pairs(s, 0)))  15.9 us
    all_to_all x1, blocking collectives, per_device(): gram = lax.all_to_all(wide, 'tm', 0, 0, tiled=True).reshape(half, width)  15.5 us
    ppermute x3, waiting for transfers between devices, per_device(): lax.ppermute(part(s), BOTH, plan.pairs(0, s))  8.44 us
    pallas_call x1, Pallas kernels, per_device(): pl.pallas_call(functools.partial(widen_kernel, plan, rows), out_shape=jax...  7.01 us
  transfers between devices with their start and end apart: 15, of which 9 were waited for; matrix products, arithmetic and copies ran while one was open for 2% of the time, Pallas kernels for 13%

profile of v2, /device:TPU:0, one launch (start us, length us, event | category | flops | bytes accessed | tf_op | source)
XLA Modules:
  0.0 164.4 jit_solution(10495276762207019197)
XLA Ops:
  0.6 1.1 fusion
  1.7 3.0 %collective-permute-start.6 = (bf16[512,256]{1,0:T(8,128)(2,1)S(1)}, bf16[512,256]{1,0:T(8,128)(2,1)S(1)}, u32[]{:S(2)}, u32[]{:S(2)}) collective-permute-start(bf16[512,256]{1,0:T(8,128)(2,1)S(1)} %get-tuple-element.3), channel_id=1, source_target_pairs={{0,2},{1,9},{2,0},{3,11},{4,6},{5,13},{6,4},{7,15},{8,10},{9,1},{1... | collective-permute-start | bytes 786440 | tf_op jit(solution)/shard_map/ppermute | solution.py:71
  4.7 1.5 collective-permute-start.7
  6.3 1.0 copy.7
  7.2 3.7 %collective-permute-start.2 = (bf16[512,64]{1,0:T(8,128)(2,1)S(1)}, bf16[512,64]{1,0:T(8,128)(2,1)S(1)}, u32[]{:S(2)}, u32[]{:S(2)}) collective-permute-start(bf16[512,64]{1,0:T(8,128)(2,1)S(1)} %copy.7), channel_id=1, source_target_pairs={{0,24},{2,26},{4,28},{6,30},{8,16},{10,18},{12,20},{14,22},{16,8},... | collective-permute-start | bytes 196616 | tf_op jit(solution)/shard_map/ppermute | solution.py:259
  10.9 0.8 collective-permute-start
  11.7 0.9 pad_maximum_fusion.1
  12.6 0.5 collective-permute-start.8
  13.1 0.0 collective-permute-done.7.refs_2_
  13.1 0.9 pad_maximum_fusion.2
  14.0 0.4 collective-permute-start.9
  14.5 1.1 collective-permute-done.2
  15.6 14.8 %collective-permute-done.1 = bf16[512,64]{1,0:T(8,128)(2,1)S(1)} collective-permute-done((bf16[512,64]{1,0:T(8,128)(2,1)S(1)}, bf16[512,64]{1,0:T(8,128)(2,1)S(1)}, u32[]{:S(2)}, u32[]{:S(2)}) %collective-permute-start.1) | collective-permute-done | bytes 65568 | tf_op jit(solution)/shard_map/ppermute | solution.py:259
  30.4 0.0 collective-permute-done
  30.4 0.1 pad_maximum_fusion.refs_0_
  30.5 0.0 copy-start.5
  30.5 1.7 %collective-permute-start.5 = (bf16[2048,64]{1,0:T(8,128)(2,1)S(1)}, bf16[2048,64]{1,0:T(8,128)(2,1)S(1)}, u32[]{:S(2)}, u32[]{:S(2)}) collective-permute-start(bf16[2048,64]{1,0:T(8,128)(2,1)S(1)} %pad_maximum_fusion.refs_0_), channel_id=1, source_target_pairs={{0,6},{2,4},{4,2},{6,0},{8,14},{10,12},{12,10},{14,8},{16,22},{18,... | collective-permute-start | bytes 786440 | tf_op jit(solution)/shard_map/ppermute | solution.py:263
  32.2 1.3 collective-permute-start.4
  33.5 0.6 collective-permute-start.3
  34.1 12.2 %collective-permute-done.5.refs_3_ = bf16[2048,64]{1,0:T(8,128)(2,1)S(1)} collective-permute-done((bf16[2048,64]{1,0:T(8,128)(2,1)S(1)}, bf16[2048,64]{1,0:T(8,128)(2,1)S(1)}, u32[]{:S(2)}, u32[]{:S(2)}) %collective-permute-start.5) | collective-permute-done | bytes 262176 | tf_op jit(solution)/shard_map/ppermute | solution.py:263
  46.3 10.3 %collective-permute-done.4.refs_2_ = bf16[2048,64]{1,0:T(8,128)(2,1)S(1)} collective-permute-done((bf16[2048,64]{1,0:T(8,128)(2,1)S(1)}, bf16[2048,64]{1,0:T(8,128)(2,1)S(1)}, u32[]{:S(2)}, u32[]{:S(2)}) %collective-permute-start.4) | collective-permute-done | bytes 262176 | tf_op jit(solution)/shard_map/ppermute | solution.py:263
  56.6 0.2 collective-permute-done.3.refs_1_
  56.8 0.6 copy-done.9
  57.4 7.0 %widen.1.wide = bf16[10240,128]{1,0:T(8,128)(2,1)} custom-call(bf16[2048,64]{1,0:T(8,128)(2,1)} %copy-done.5, bf16[2048,64]{1,0:T(8,128)(2,1)} %collective-permute-done.3.refs_1_, bf16[2048,64]{1,0:T(8,128)(2,1)} %copy-done.9, bf16[2048,64]{1,0:T(8,128)(2,1)} %copy-done.8), custom_call_target="tpu_custom_call" | custom-call | tf_op jit(solution)/shard_map/widen/pallas_call | solution.py:265
  64.4 0.0 collective-permute-done.8.refs_3_
  64.4 0.0 copy-start
  64.5 0.8 copy-done
  65.2 0.8 copy-done.1
  66.0 4.6 %sketch3.1 = f32[512,256]{1,0:T(8,128)} custom-call(bf16[10240,128]{1,0:T(8,128)(2,1)} %widen.1.wide, bf16[1024,256]{1,0:T(8,128)(2,1)} %refs_0_.7, bf16[512,256]{1,0:T(8,128)(2,1)} %copy-done.2, bf16[512,256]{1,0:T(8,128)(2,1)} %copy-done.3, bf16[1024,256]{1,0:T(8,128)(2,1)} %copy-done, bf16[1024,256]{1,0:T(8,128)(2,1)} %copy-done.1), custom_call_target="tpu_custom_call" | custom-call | tf_op jit(solution)/shard_map/sketch3/pallas_call | solution.py:275
  70.6 2.3 %collective-permute-start.10 = (f32[512,256]{1,0:T(8,128)}, f32[512,256]{1,0:T(8,128)S(1)}, u32[]{:S(2)}, u32[]{:S(2)}) collective-permute-start(f32[512,256]{1,0:T(8,128)} %sketch3.1), channel_id=1, source_target_pairs={{0,24},{1,7},{2,26},{3,5},{4,28},{5,3},{6,30},{7,1},{8,16},{9,15},... | collective-permute-start | bytes 1572872 | tf_op jit(solution)/shard_map/ppermute | solution.py:283
  72.8 4.6 %sketch2.1 = f32[512,256]{1,0:T(8,128)} custom-call(bf16[10240,128]{1,0:T(8,128)(2,1)} %widen.1.wide, bf16[1024,256]{1,0:T(8,128)(2,1)} %refs_0_.7, bf16[512,256]{1,0:T(8,128)(2,1)} %copy-done.2, bf16[512,256]{1,0:T(8,128)(2,1)} %copy-done.3, bf16[1024,256]{1,0:T(8,128)(2,1)} %copy-done, bf16[1024,256]{1,0:T(8,128)(2,1)} %copy-done.1), custom_call_target="tpu_custom_call" | custom-call | tf_op jit(solution)/shard_map/sketch2/pallas_call | solution.py:275
  77.4 0.0 collective-permute-start.11
  77.4 4.6 %sketch1.1 = f32[512,256]{1,0:T(8,128)} custom-call(bf16[10240,128]{1,0:T(8,128)(2,1)} %widen.1.wide, bf16[1024,256]{1,0:T(8,128)(2,1)} %refs_0_.7, bf16[512,256]{1,0:T(8,128)(2,1)} %copy-done.2, bf16[512,256]{1,0:T(8,128)(2,1)} %copy-done.3, bf16[1024,256]{1,0:T(8,128)(2,1)} %copy-done, bf16[1024,256]{1,0:T(8,128)(2,1)} %copy-done.1), custom_call_target="tpu_custom_call" | custom-call | tf_op jit(solution)/shard_map/sketch1/pallas_call | solution.py:275
  82.0 2.1 %collective-permute-start.12 = (f32[512,256]{1,0:T(8,128)}, f32[512,256]{1,0:T(8,128)S(1)}, u32[]{:S(2)}, u32[]{:S(2)}) collective-permute-start(f32[512,256]{1,0:T(8,128)} %sketch1.1), channel_id=1, source_target_pairs={{0,8},{1,3},{2,10},{3,1},{4,12},{5,7},{6,14},{7,5},{8,0},{9,11},{1... | collective-permute-start | bytes 1572872 | tf_op jit(solution)/shard_map/ppermute | solution.py:283
  84.1 4.5 %sketch0.1 = f32[512,256]{1,0:T(8,128)} custom-call(bf16[10240,128]{1,0:T(8,128)(2,1)} %widen.1.wide, bf16[1024,256]{1,0:T(8,128)(2,1)} %refs_0_.7, bf16[512,256]{1,0:T(8,128)(2,1)} %copy-done.2, bf16[512,256]{1,0:T(8,128)(2,1)} %copy-done.3, bf16[1024,256]{1,0:T(8,128)(2,1)} %copy-done, bf16[1024,256]{1,0:T(8,128)(2,1)} %copy-done.1), custom_call_target="tpu_custom_call" | custom-call | tf_op jit(solution)/shard_map/sketch0/pallas_call | solution.py:275
  88.6 7.1 %collective-permute-done.11 = f32[512,256]{1,0:T(8,128)S(1)} collective-permute-done((f32[512,256]{1,0:T(8,128)}, f32[512,256]{1,0:T(8,128)S(1)}, u32[]{:S(2)}, u32[]{:S(2)}) %collective-permute-start.11) | collective-permute-done | bytes 524320 | tf_op jit(solution)/shard_map/ppermute | solution.py:283
  95.7 1.4 collective-permute-done.12
  97.1 1.2 add_add_fusion.own_ref.sown
  98.3 0.1 collective-permute-start.13
  98.3 1.9 %collective-permute-done.13.other_ref.sother = f32[512,256]{1,0:T(8,128)S(1)} collective-permute-done((f32[512,256]{1,0:T(8,128)S(1)}, f32[512,256]{1,0:T(8,128)S(1)}, u32[]{:S(2)}, u32[]{:S(2)}) %collective-permute-start.13) | collective-permute-done | bytes 524320 | tf_op jit(solution)/shard_map/ppermute | solution.py:287
  100.2 0.8 copy-done.6
  101.0 3.4 %gram.1 = f32[256,384]{1,0:T(8,128)} custom-call(f32[512,256]{1,0:T(8,128)} %copy-done.4, f32[512,256]{1,0:T(8,128)} %copy-done.6), custom_call_target="tpu_custom_call" | custom-call | tf_op jit(solution)/shard_map/gram/pallas_call | solution.py:288
  104.4 17.8 %all_to_all.10 = f32[16,16,384]{2,1,0:T(8,128)S(1)} all-to-all(f32[16,16,384]{2,1,0:T(8,128)} %bitcast.4), channel_id=1, replica_groups=mesh['grp'=1,'tm'=16,'panel'=2] {'tm'}, dimensions={0} | all-to-all | bytes 786432 | tf_op jit(solution)/shard_map/all_to_all | solution.py:296
  122.3 15.5 %all_to_all.11 = f32[16,16,384]{2,1,0:T(8,128)S(1)} all-to-all(f32[16,16,384]{2,1,0:T(8,128)S(1)} %broadcast_in_dim.2), channel_id=1, replica_groups=mesh['grp'=1,'tm'=16,'panel'=2] {'tm'}, dimensions={0} | all-to-all | bytes 786432 | tf_op jit(solution)/shard_map/all_to_all | solution.py:299
  137.8 0.0 collective-permute-start.14
  137.8 1.7 %collective-permute-done.14.gother = f32[256,384]{1,0:T(8,128)S(1)} collective-permute-done((f32[256,384]{1,0:T(8,128)S(1)}, f32[256,384]{1,0:T(8,128)S(1)}, u32[]{:S(2)}, u32[]{:S(2)}) %collective-permute-start.14) | collective-permute-done | bytes 393248 | tf_op jit(solution)/shard_map/ppermute | solution.py:300
  139.5 0.8 copy-done.10
  140.3 24.1 %factor.1 = (f32[512,256]{1,0:T(8,128)}, f32[512,256]{1,0:T(8,128)}) custom-call(f32[256,384]{1,0:T(8,128)} %bitcast.3, f32[256,384]{1,0:T(8,128)} %copy-done.10, f32[512,256]{1,0:T(8,128)} %copy-done.4, f32[512,256]{1,0:T(8,128)} %copy-done.6), custom_call_target="tpu_custom_call" | custom-call | tf_op jit(solution)/shard_map/factor/pallas_call | solution.py:303
  (21 shorter events, 0.1 us)
Async XLA Ops:
  1.7 10.0 %collective-permute-start.6 = (bf16[512,256]{1,0:T(8,128)(2,1)S(1)}, bf16[512,256]{1,0:T(8,128)(2,1)S(1)}, u32[]{:S(2)}, u32[]{:S(2)}) collective-permute-start(bf16[512,256]{1,0:T(8,128)(2,1)S(1)} %get-tuple-element.3), channel_id=1, source_target_pairs={{0,2},{1,9},{2,0},{3,11},{4,6},{5,13},{6,4},{7,15},{8,10},{9,1},{1... | collective-permute-start | bytes 786440 | tf_op jit(solution)/shard_map/ppermute | solution.py:71
  4.7 8.3 %collective-permute-start.7 = (bf16[512,256]{1,0:T(8,128)(2,1)S(1)}, bf16[512,256]{1,0:T(8,128)(2,1)S(1)}, u32[]{:S(2)}, u32[]{:S(2)}) collective-permute-start(bf16[512,256]{1,0:T(8,128)(2,1)S(1)} %get-tuple-element.2), channel_id=1, source_target_pairs={{0,4},{1,17},{2,6},{3,19},{4,0},{5,21},{6,2},{7,23},{8,12},{9,25},... | collective-permute-start | bytes 786440 | tf_op jit(solution)/shard_map/ppermute | solution.py:71
  7.2 8.4 %collective-permute-start.2 = (bf16[512,64]{1,0:T(8,128)(2,1)S(1)}, bf16[512,64]{1,0:T(8,128)(2,1)S(1)}, u32[]{:S(2)}, u32[]{:S(2)}) collective-permute-start(bf16[512,64]{1,0:T(8,128)(2,1)S(1)} %copy.7), channel_id=1, source_target_pairs={{0,24},{2,26},{4,28},{6,30},{8,16},{10,18},{12,20},{14,22},{16,8},... | collective-permute-start | bytes 196616 | tf_op jit(solution)/shard_map/ppermute | solution.py:259
  10.9 19.5 %collective-permute-start.1 = (bf16[512,64]{1,0:T(8,128)(2,1)S(1)}, bf16[512,64]{1,0:T(8,128)(2,1)S(1)}, u32[]{:S(2)}, u32[]{:S(2)}) collective-permute-start(bf16[512,64]{1,0:T(8,128)(2,1)S(1)} %copy.7), channel_id=1, source_target_pairs={{0,16},{2,18},{4,20},{6,22},{8,24},{10,26},{12,28},{14,30},{16,0},... | collective-permute-start | bytes 196616 | tf_op jit(solution)/shard_map/ppermute | solution.py:259
  10.9 19.5 %collective-permute-start = (bf16[512,64]{1,0:T(8,128)(2,1)S(1)}, bf16[512,64]{1,0:T(8,128)(2,1)S(1)}, u32[]{:S(2)}, u32[]{:S(2)}) collective-permute-start(bf16[512,64]{1,0:T(8,128)(2,1)S(1)} %copy.7), channel_id=1, source_target_pairs={{0,8},{2,10},{4,12},{6,14},{8,0},{10,2},{12,4},{14,6},{16,24},{18,... | collective-permute-start | bytes 196616 | tf_op jit(solution)/shard_map/ppermute | solution.py:259
  11.7 52.8 %copy-start.2 = (bf16[512,256]{1,0:T(8,128)(2,1)}, bf16[512,256]{1,0:T(8,128)(2,1)S(1)}, u32[]{:S(2)}) copy-start(bf16[512,256]{1,0:T(8,128)(2,1)S(1)} %collective-permute-done.6.refs_1_) | copy-start | bytes 786436
  12.6 51.9 %collective-permute-start.8 = (bf16[1024,256]{1,0:T(8,128)(2,1)}, bf16[1024,256]{1,0:T(8,128)(2,1)S(1)}, u32[]{:S(2)}, u32[]{:S(2)}) collective-permute-start(bf16[1024,256]{1,0:T(8,128)(2,1)} %pad_maximum_fusion.1), channel_id=1, source_target_pairs={{0,4},{1,17},{2,6},{3,19},{4,0},{5,21},{6,2},{7,23},{8,12},{9,25},... | collective-permute-start | bytes 1572872 | tf_op jit(solution)/shard_map/ppermute | solution.py:71
  13.1 51.4 %copy-start.3 = (bf16[512,256]{1,0:T(8,128)(2,1)}, bf16[512,256]{1,0:T(8,128)(2,1)S(1)}, u32[]{:S(2)}) copy-start(bf16[512,256]{1,0:T(8,128)(2,1)S(1)} %collective-permute-done.7.refs_2_) | copy-start | bytes 786436
  14.0 50.4 %collective-permute-start.9 = (bf16[1024,256]{1,0:T(8,128)(2,1)}, bf16[1024,256]{1,0:T(8,128)(2,1)S(1)}, u32[]{:S(2)}, u32[]{:S(2)}) collective-permute-start(bf16[1024,256]{1,0:T(8,128)(2,1)} %pad_maximum_fusion.2), channel_id=1, source_target_pairs={{0,2},{1,9},{2,0},{3,11},{4,6},{5,13},{6,4},{7,15},{8,10},{9,1},{1... | collective-permute-start | bytes 1572872 | tf_op jit(solution)/shard_map/ppermute | solution.py:71
  30.5 26.3 %copy-start.5 = (bf16[2048,64]{1,0:T(8,128)(2,1)}, bf16[2048,64]{1,0:T(8,128)(2,1)S(1)}, u32[]{:S(2)}) copy-start(bf16[2048,64]{1,0:T(8,128)(2,1)S(1)} %pad_maximum_fusion.refs_0_) | copy-start | bytes 786436
  30.5 15.8 %collective-permute-start.5 = (bf16[2048,64]{1,0:T(8,128)(2,1)S(1)}, bf16[2048,64]{1,0:T(8,128)(2,1)S(1)}, u32[]{:S(2)}, u32[]{:S(2)}) collective-permute-start(bf16[2048,64]{1,0:T(8,128)(2,1)S(1)} %pad_maximum_fusion.refs_0_), channel_id=1, source_target_pairs={{0,6},{2,4},{4,2},{6,0},{8,14},{10,12},{12,10},{14,8},{16,22},{18,... | collective-permute-start | bytes 786440 | tf_op jit(solution)/shard_map/ppermute | solution.py:263
  32.2 24.4 %collective-permute-start.4 = (bf16[2048,64]{1,0:T(8,128)(2,1)S(1)}, bf16[2048,64]{1,0:T(8,128)(2,1)S(1)}, u32[]{:S(2)}, u32[]{:S(2)}) collective-permute-start(bf16[2048,64]{1,0:T(8,128)(2,1)S(1)} %pad_maximum_fusion.refs_0_), channel_id=1, source_target_pairs={{0,4},{2,6},{4,0},{6,2},{8,12},{10,14},{12,8},{14,10},{16,20},{18,... | collective-permute-start | bytes 786440 | tf_op jit(solution)/shard_map/ppermute | solution.py:263
  33.5 23.3 %collective-permute-start.3 = (bf16[2048,64]{1,0:T(8,128)(2,1)S(1)}, bf16[2048,64]{1,0:T(8,128)(2,1)}, u32[]{:S(2)}, u32[]{:S(2)}) collective-permute-start(bf16[2048,64]{1,0:T(8,128)(2,1)S(1)} %pad_maximum_fusion.refs_0_), channel_id=1, source_target_pairs={{0,2},{2,0},{4,6},{6,4},{8,10},{10,8},{12,14},{14,12},{16,18},{18,... | collective-permute-start | bytes 786440 | tf_op jit(solution)/shard_map/ppermute | solution.py:263
  46.3 10.5 %copy-start.8 = (bf16[2048,64]{1,0:T(8,128)(2,1)}, bf16[2048,64]{1,0:T(8,128)(2,1)S(1)}, u32[]{:S(2)}) copy-start(bf16[2048,64]{1,0:T(8,128)(2,1)S(1)} %collective-permute-done.5.refs_3_) | copy-start | bytes 786436
  56.6 0.8 copy-start.9
  64.4 0.8 copy-start
  65.2 0.8 copy-start.1
  70.6 18.0 %collective-permute-start.10 = (f32[512,256]{1,0:T(8,128)}, f32[512,256]{1,0:T(8,128)S(1)}, u32[]{:S(2)}, u32[]{:S(2)}) collective-permute-start(f32[512,256]{1,0:T(8,128)} %sketch3.1), channel_id=1, source_target_pairs={{0,24},{1,7},{2,26},{3,5},{4,28},{5,3},{6,30},{7,1},{8,16},{9,15},... | collective-permute-start | bytes 1572872 | tf_op jit(solution)/shard_map/ppermute | solution.py:283
  77.4 18.3 %collective-permute-start.11 = (f32[512,256]{1,0:T(8,128)}, f32[512,256]{1,0:T(8,128)S(1)}, u32[]{:S(2)}, u32[]{:S(2)}) collective-permute-start(f32[512,256]{1,0:T(8,128)} %sketch2.1), channel_id=1, source_target_pairs={{0,16},{1,5},{2,18},{3,7},{4,20},{5,1},{6,22},{7,3},{8,24},{9,13},... | collective-permute-start | bytes 1572872 | tf_op jit(solution)/shard_map/ppermute | solution.py:283
  82.0 15.1 %collective-permute-start.12 = (f32[512,256]{1,0:T(8,128)}, f32[512,256]{1,0:T(8,128)S(1)}, u32[]{:S(2)}, u32[]{:S(2)}) collective-permute-start(f32[512,256]{1,0:T(8,128)} %sketch1.1), channel_id=1, source_target_pairs={{0,8},{1,3},{2,10},{3,1},{4,12},{5,7},{6,14},{7,5},{8,0},{9,11},{1... | collective-permute-start | bytes 1572872 | tf_op jit(solution)/shard_map/ppermute | solution.py:283
  98.2 2.0 %copy-start.4 = (f32[512,256]{1,0:T(8,128)}, f32[512,256]{1,0:T(8,128)S(1)}, u32[]{:S(2)}) copy-start(f32[512,256]{1,0:T(8,128)S(1)} %add_add_fusion.own_ref.sown) | copy-start | bytes 1572868
  98.3 2.0 %collective-permute-start.13 = (f32[512,256]{1,0:T(8,128)S(1)}, f32[512,256]{1,0:T(8,128)S(1)}, u32[]{:S(2)}, u32[]{:S(2)}) collective-permute-start(f32[512,256]{1,0:T(8,128)S(1)} %add_add_fusion.own_ref.sown), channel_id=1, source_target_pairs={{0,1},{1,0},{2,3},{3,2},{4,5},{5,4},{6,7},{7,6},{8,9},{9,8},{10,11... | collective-permute-start | bytes 1572872 | tf_op jit(solution)/shard_map/ppermute | solution.py:287
  100.2 0.8 copy-start.6
  137.8 1.7 %copy-start.7 = (f32[16,16,384]{2,1,0:T(8,128)}, f32[16,16,384]{2,1,0:T(8,128)S(1)}, u32[]{:S(2)}) copy-start(f32[16,16,384]{2,1,0:T(8,128)S(1)} %all_to_all.11) | copy-start | bytes 1179652
  137.8 1.7 %collective-permute-start.14 = (f32[256,384]{1,0:T(8,128)S(1)}, f32[256,384]{1,0:T(8,128)S(1)}, u32[]{:S(2)}, u32[]{:S(2)}) collective-permute-start(f32[256,384]{1,0:T(8,128)S(1)} %bitcast.2), channel_id=1, source_target_pairs={{0,1},{1,0},{2,3},{3,2},{4,5},{5,4},{6,7},{7,6},{8,9},{9,8},{10,11... | collective-permute-start | bytes 1179656 | tf_op jit(solution)/shard_map/ppermute | solution.py:300
  139.5 0.8 copy-start.10

commit v3 on v2

--- a/solution.py
+++ b/solution.py
@@ -16,6 +16,7 @@
 TILE = 256
 HI = lax.Precision.HIGHEST
 BOTH = ("tm", "panel")
+SWAP = [(0, 1), (1, 0)]
 
 
 def dot_nn(a, b):
@@ -88,32 +89,45 @@
     return arrays, where
 
 
-def widen_kernel(plan, rows, *refs):
-    stacks = refs[: plan.lo]
-    wide, flat = refs[plan.lo :]
+def widen_kernel(series, out, flat):
+    rows, variables = series.shape
+    count = out.shape[0]
+    flat[:rows, :] = series[...]
+    flat[rows:, :] = jnp.zeros((flat.shape[0] - rows, variables), flat.dtype)
+    start = pl.multiple_of(lax.axis_index("panel") * count, count)
+    now = flat[pl.ds(start, count + 16), :]
+    out[...] = jnp.concatenate([now[:count], now[LAG_SPACING : LAG_SPACING + count]], 1)
+
+
+def place_kernel(plan, *refs):
+    wide = refs[-1]
     i = lax.axis_index("tm")
+    panel = lax.axis_index("panel")
     hi, lo = i // plan.lo, i % plan.lo
+    count = refs[0].shape[0] // plan.hi
+    rows = 2 * count
     total = plan.n * rows
-    variables = stacks[0].shape[1]
-    flat[total:, :] = jnp.zeros((flat.shape[0] - total, variables), flat.dtype)
-    for slo in range(plan.lo):
-
-        @pl.loop(0, plan.hi)
-        def _(shi):
-            slab = (hi ^ shi) * plan.lo + (lo ^ slo)
-            flat[pl.ds(pl.multiple_of(slab * rows, rows), rows), :] = stacks[slo][
-                pl.ds(pl.multiple_of(shi * rows, rows), rows), :
-            ]
-
-    step = 256
-
-    @pl.loop(0, wide.shape[0] // step)
+    variables = wide.shape[1] // 2
+    wide[total:, :] = jnp.zeros((wide.shape[0] - total, wide.shape[1]), wide.dtype)
+    for side in range(2):
+        for slo in range(plan.lo):
+            ref = refs[side * plan.lo + slo]
+
+            @pl.loop(0, plan.hi)
+            def _(shi):
+                slab = (hi ^ shi) * plan.lo + (lo ^ slo)
+                first = slab * rows + lax.rem(panel + side, 2) * count
+                wide[pl.ds(pl.multiple_of(first, count), count), :] = ref[
+                    pl.ds(pl.multiple_of(shi * count, count), count), :
+                ]
+
+    @pl.loop(1, plan.n + 1)
     def _(k):
-        start = pl.multiple_of(k * step, step)
-        now = flat[pl.ds(start, step + 16), :]
-        wide[pl.ds(start, step), :] = jnp.concatenate(
-            [now[:step], now[LAG_SPACING : LAG_SPACING + step]], 1
-        )
+        edge = pl.multiple_of(k * rows, rows)
+        after = wide[pl.ds(edge, 16), :]
+        before = wide[pl.ds(edge - 16, 16), :]
+        right = jnp.concatenate([before[:LAG_SPACING, variables:], after[:LAG_SPACING, :variables]], 0)
+        wide[pl.ds(edge - 16, 16), :] = jnp.concatenate([before[:, :variables], right], 1)
 
 
 def sketch_kernel(plan, rows, depth, variables, where, sb, wide, *refs):
@@ -147,18 +161,24 @@
 
 
 def gram_kernel(own_ref, other_ref, out_ref):
-    own = own_ref[...]
-    half = own.shape[1]
-    out_ref[:, :half] = dot_tn(own, own)
+    half = own_ref.shape[1]
+    first, last = own_ref[:, :NB], own_ref[:, NB:]
+    out_ref[:, :half] = dot_tn(first, own_ref[...])
+    out_ref[:, half : half + NB] = dot_tn(last, last)
     panel = lax.axis_index("panel")
 
+    def cross(left, right):
+        both = dot_tn(left, right)
+        out_ref[:, half + NB : half + 2 * NB] = both[:NB]
+        out_ref[:, half + 2 * NB :] = both[NB:]
+
     @pl.when(panel == 0)
     def _():
-        out_ref[:, half:] = dot_tn(own_ref[...], other_ref[:, : half // 2])
+        cross(own_ref[...], other_ref[:, :NB])
 
     @pl.when(panel == 1)
     def _():
-        out_ref[:, half:] = dot_tn(other_ref[...], own_ref[:, half // 2 :])
+        cross(other_ref[...], own_ref[:, NB:])
 
 
 def small_factor(block, base, size):
@@ -189,15 +209,17 @@
 
 
 def factor_kernel(factor, gown, gother, sown, sother, basis_ref, tri_ref, a, w, r, v):
-    half = gown.shape[0]
+    half = sown.shape[1]
     n = 2 * half
     panel = lax.axis_index("panel")
 
     def place(first, second):
-        a[:half, :half] = first[:, :half]
-        a[:half, half : half + half // 2] = first[:, half:]
-        a[half:, half:] = second[:, :half]
-        a[:half, half + half // 2 :] = second[:, half:]
+        for at, piece in ((0, first), (half, second)):
+            a[at : at + NB, at : at + half] = piece[:, :half]
+            a[at + NB : at + half, at + NB : at + half] = piece[:, half : half + NB]
+        for at, piece in ((half, first), (half + NB, second)):
+            a[:NB, at : at + NB] = piece[:, half + NB : half + 2 * NB]
+            a[NB:half, at : at + NB] = piece[:, half + 2 * NB :]
 
     @pl.when(panel == 0)
     def _():
@@ -254,21 +276,29 @@
     rows, variables = series.shape
     depth, half = test_matrix.shape
     arrays, where = gather_blocks(plan, test_matrix)
-    pieces = [series]
+    own_rows = pl.pallas_call(
+        widen_kernel,
+        out_shape=jax.ShapeDtypeStruct((rows // 2, 2 * variables), jnp.bfloat16),
+        in_specs=vmem(1),
+        out_specs=vmem(1)[0],
+        scratch_shapes=[pltpu.VMEM((rows + 16, variables), jnp.bfloat16)],
+        name="widen",
+    )(series)
+    pieces = [own_rows]
     for s in range(1, plan.hi):
-        pieces.append(lax.ppermute(series, "tm", plan.plain_pairs(s, 0)))
+        pieces.append(lax.ppermute(own_rows, "tm", plan.plain_pairs(s, 0)))
     stack = jnp.concatenate(pieces, 0)
     stacks = [stack]
     for s in range(1, plan.lo):
         stacks.append(lax.ppermute(stack, "tm", plan.plain_pairs(0, s)))
+    stacks = stacks + [lax.ppermute(value, "panel", SWAP) for value in stacks]
     length = n * rows + WINDOW_LAGS * LAG_SPACING
     wide = pl.pallas_call(
-        functools.partial(widen_kernel, plan, rows),
+        functools.partial(place_kernel, plan),
         out_shape=jax.ShapeDtypeStruct((length, 2 * variables), jnp.bfloat16),
-        in_specs=vmem(plan.lo),
+        in_specs=vmem(2 * plan.lo),
         out_specs=vmem(1)[0],
-        scratch_shapes=[pltpu.VMEM((length + 16, variables), jnp.bfloat16)],
-        name="widen",
+        name="place",
     )(*stacks)
 
     def part(sb):
@@ -284,20 +314,21 @@
     own = part(0)
     for piece in arrived:
         own = own + piece
-    other = lax.ppermute(own, "panel", [(0, 1), (1, 0)])
+    other = lax.ppermute(own, "panel", SWAP)
+    assert half == 2 * NB
+    width = 5 * NB
     gram = pl.pallas_call(
         gram_kernel,
-        out_shape=jax.ShapeDtypeStruct((half, half + half // 2), jnp.float32),
+        out_shape=jax.ShapeDtypeStruct((NB, width), jnp.float32),
         in_specs=vmem(2),
         out_specs=vmem(1)[0],
         name="gram",
     )(own, other)
-    width = half + half // 2
-    spread = lax.all_to_all(gram.reshape(n, half // n, width), "tm", 0, 0, tiled=True)
+    spread = lax.all_to_all(gram.reshape(n, NB // n, width), "tm", 0, 0, tiled=True)
     summed = jnp.sum(spread, 0)
-    wide = jnp.broadcast_to(summed[None], (n, half // n, width))
-    gram = lax.all_to_all(wide, "tm", 0, 0, tiled=True).reshape(half, width)
-    gram_other = lax.ppermute(gram, "panel", [(0, 1), (1, 0)])
+    alike = jnp.broadcast_to(summed[None], (n, NB // n, width))
+    gram = lax.all_to_all(alike, "tm", 0, 0, tiled=True).reshape(NB, width)
+    gram_other = lax.ppermute(gram, "panel", SWAP)
     full = 2 * half
     return tuple(
         pl.pallas_call(

time: 165 us -> 142 us (0.86)
  waiting for transfers between devices: 50.7 us -> 28.7 us
  blocking collectives: 33.3 us -> 30.7 us
  starting transfers between devices: 18 us -> 20.1 us
    ppermute x3, waiting for transfers between devices: 22.7 us -> 9.03 us  [per_device(): stacks.append(lax.ppermute(stack, 'tm', plan.plain_pairs(0, s)))]
    ppermute x5 -> x9, waiting for transfers between devices: 19.6 us -> 11.1 us  [the longest x3 6.73 us: per_device(): pieces.append(lax.ppermute(own_rows, 'tm', plan.plain_pairs(s, 0)))]
    all_to_all x2, blocking collectives: 33.3 us -> 30.7 us  [the longest x1 16.5 us: per_device(): lax.all_to_all(gram.reshape(n, NB // n, width), 'tm', 0, 0, tiled=True)]
    pallas_call x2 -> x3, Pallas kernels: 10.4 us -> 9.46 us  [the longest x1 4.52 us: per_device(): pl.pallas_call(functools.partial(place_kernel, plan), out_shape=jax.Shape...]
    unnamed x23 -> x31, local copies, waits for them, and re-layouts: 4.73 us -> 5.58 us
    ppermute x5 -> x9, starting transfers between devices: 4.53 us -> 5.05 us  [the longest x3 4.39 us: per_device(): pieces.append(lax.ppermute(own_rows, 'tm', plan.plain_pairs(s, 0)))]
  transfers between devices with their start and end apart: 15 -> 19, of which waited for: 9 -> 10; matrix products, arithmetic and copies ran while one was open for 2% -> 2% of each run, Pallas kernels for 13% -> 14%
where the time goes in v3:
time: 142 us; the launch traced here: 141 us
  Pallas kernels  51.8 us (36%)
  blocking collectives  30.7 us (22%)
  waiting for transfers between devices  28.7 us (20%)
  starting transfers between devices  20.1 us (14%)
  local copies, waits for them, and re-layouts  6.67 us (5%)
  other arithmetic  2.13 us (2%)
    pallas_call x1, Pallas kernels, per_device(): pl.pallas_call(functools.partial(factor_kernel, math.sqrt(n * rows)), out...  24.1 us
    pallas_call x4, Pallas kernels, part(): pl.pallas_call(functools.partial(sketch_kernel, plan, rows, depth, variab...  18.2 us
    all_to_all x1, blocking collectives, per_device(): lax.all_to_all(gram.reshape(n, NB // n, width), 'tm', 0, 0, tiled=True)  16.5 us
    all_to_all x1, blocking collectives, per_device(): gram = lax.all_to_all(alike, 'tm', 0, 0, tiled=True).reshape(NB, width)  14.2 us
    ppermute x3, waiting for transfers between devices, per_device(): stacks.append(lax.ppermute(stack, 'tm', plan.plain_pairs(0, s)))  9.03 us
    ppermute x3, waiting for transfers between devices, per_device(): lax.ppermute(part(s), BOTH, plan.pairs(0, s))  8.62 us
    ppermute x4, starting transfers between devices, sent(): return lax.ppermute(value, BOTH, plan.pairs(da, 0))  7.12 us
    ppermute x3, waiting for transfers between devices, per_device(): pieces.append(lax.ppermute(own_rows, 'tm', plan.plain_pairs(s, 0)))  6.73 us
  transfers between devices with their start and end apart: 19, of which 10 were waited for; matrix products, arithmetic and copies ran while one was open for 2% of the time, Pallas kernels for 14%

profile of v3, /device:TPU:0, one launch (start us, length us, event | category | flops | bytes accessed | tf_op | source)
XLA Modules:
  0.0 140.9 jit_solution(9445618216928193852)
XLA Ops:
  0.6 1.1 fusion
  1.7 3.0 %collective-permute-start.10 = (bf16[512,256]{1,0:T(8,128)(2,1)S(1)}, bf16[512,256]{1,0:T(8,128)(2,1)S(1)}, u32[]{:S(2)}, u32[]{:S(2)}) collective-permute-start(bf16[512,256]{1,0:T(8,128)(2,1)S(1)} %get-tuple-element.3), channel_id=1, source_target_pairs={{0,2},{1,9},{2,0},{3,11},{4,6},{5,13},{6,4},{7,15},{8,10},{9,1},{1... | collective-permute-start | bytes 786440 | tf_op jit(solution)/shard_map/ppermute | solution.py:72
  4.7 1.6 %copy.4.series = bf16[512,64]{1,0:T(8,128)(2,1)} copy(bf16[512,64]{0,1:T(8,128)(2,1)} %param.2) | data formatting | bytes 131072 | tf_op args[0]
  6.3 1.7 %widen.1 = bf16[256,128]{1,0:T(8,128)(2,1)} custom-call(bf16[512,64]{1,0:T(8,128)(2,1)} %copy.4.series), custom_call_target="tpu_custom_call" | custom-call | tf_op jit(solution)/shard_map/widen/pallas_call | solution.py:279
  8.0 3.6 %collective-permute-start.2 = (bf16[256,128]{1,0:T(8,128)(2,1)}, bf16[256,128]{1,0:T(8,128)(2,1)S(1)}, u32[]{:S(2)}, u32[]{:S(2)}) collective-permute-start(bf16[256,128]{1,0:T(8,128)(2,1)} %widen.1), channel_id=1, source_target_pairs={{0,24},{2,26},{4,28},{6,30},{8,16},{10,18},{12,20},{14,22},{16,8},... | collective-permute-start | bytes 196616 | tf_op jit(solution)/shard_map/ppermute | solution.py:289
  11.6 0.0 collective-permute-start.1
  11.6 0.8 collective-permute-start
  12.4 1.5 %collective-permute-start.11 = (bf16[512,256]{1,0:T(8,128)(2,1)S(1)}, bf16[512,256]{1,0:T(8,128)(2,1)S(1)}, u32[]{:S(2)}, u32[]{:S(2)}) collective-permute-start(bf16[512,256]{1,0:T(8,128)(2,1)S(1)} %get-tuple-element.2), channel_id=1, source_target_pairs={{0,4},{1,17},{2,6},{3,19},{4,0},{5,21},{6,2},{7,23},{8,12},{9,25},... | collective-permute-start | bytes 786440 | tf_op jit(solution)/shard_map/ppermute | solution.py:72
  13.9 1.1 collective-permute-done.2
  15.0 5.6 %collective-permute-done.1 = bf16[256,128]{1,0:T(8,128)(2,1)S(1)} collective-permute-done((bf16[256,128]{1,0:T(8,128)(2,1)}, bf16[256,128]{1,0:T(8,128)(2,1)S(1)}, u32[]{:S(2)}, u32[]{:S(2)}) %collective-permute-start.1) | collective-permute-done | bytes 65568 | tf_op jit(solution)/shard_map/ppermute | solution.py:289
  20.6 0.9 pad_maximum_fusion.2.refs_0_
  21.5 0.0 copy-start.7
  21.5 0.1 collective-permute-start.6
  21.6 1.9 %collective-permute-start.5 = (bf16[1024,128]{1,0:T(8,128)(2,1)S(1)}, bf16[1024,128]{1,0:T(8,128)(2,1)S(1)}, u32[]{:S(2)}, u32[]{:S(2)}) collective-permute-start(bf16[1024,128]{1,0:T(8,128)(2,1)S(1)} %pad_maximum_fusion.2.refs_0_), channel_id=1, source_target_pairs={{0,6},{2,4},{4,2},{6,0},{8,14},{10,12},{12,10},{14,8},{16,22},{18,... | collective-permute-start | bytes 786440 | tf_op jit(solution)/shard_map/ppermute | solution.py:293
  23.5 0.5 collective-permute-start.4
  24.0 1.1 collective-permute-start.3
  25.2 1.6 %collective-permute-start.12 = (bf16[1024,256]{1,0:T(8,128)(2,1)S(1)}, bf16[1024,256]{1,0:T(8,128)(2,1)S(1)}, u32[]{:S(2)}, u32[]{:S(2)}) collective-permute-start(bf16[1024,256]{1,0:T(8,128)(2,1)S(1)} %pad_maximum_fusion), channel_id=1, source_target_pairs={{0,4},{1,17},{2,6},{3,19},{4,0},{5,21},{6,2},{7,23},{8,12},{9,25},... | collective-permute-start | bytes 1572872 | tf_op jit(solution)/shard_map/ppermute | solution.py:72
  26.8 1.0 collective-permute-start.13
  27.8 3.9 %collective-permute-done.5.refs_3_ = bf16[1024,128]{1,0:T(8,128)(2,1)S(1)} collective-permute-done((bf16[1024,128]{1,0:T(8,128)(2,1)S(1)}, bf16[1024,128]{1,0:T(8,128)(2,1)S(1)}, u32[]{:S(2)}, u32[]{:S(2)}) %collective-permute-start.5) | collective-permute-done | bytes 262176 | tf_op jit(solution)/shard_map/ppermute | solution.py:293
  31.8 5.0 %collective-permute-done.4.refs_2_ = bf16[1024,128]{1,0:T(8,128)(2,1)S(1)} collective-permute-done((bf16[1024,128]{1,0:T(8,128)(2,1)S(1)}, bf16[1024,128]{1,0:T(8,128)(2,1)S(1)}, u32[]{:S(2)}, u32[]{:S(2)}) %collective-permute-start.4) | collective-permute-done | bytes 262176 | tf_op jit(solution)/shard_map/ppermute | solution.py:293
  36.8 0.0 collective-permute-start.8
  36.8 0.1 collective-permute-done.3.refs_1_
  36.9 0.5 collective-permute-start.7
  37.4 0.1 copy-done.11
  37.5 0.8 collective-permute-done.8.refs_6_
  38.3 0.7 copy-done.14
  39.1 4.5 %place.1.wide = bf16[10240,128]{1,0:T(8,128)(2,1)} custom-call(bf16[1024,128]{1,0:T(8,128)(2,1)} %copy-done.7, bf16[1024,128]{1,0:T(8,128)(2,1)} %copy-done.12, bf16[1024,128]{1,0:T(8,128)(2,1)} %copy-done.11, bf16[1024,128]{1,0:T(8,128)(2,1)} %copy-done.10, bf16[1024,128]{1,0:T(8,128)(2,1)} %copy-done.9, bf16[1024,128]{1,0:T(8,128)(2,1)} %collective-permute-done.7.refs_5_, ...), custom_call_target="tpu_custom_call" | custom-call | tf_op jit(solution)/shard_map/place/pallas_call | solution.py:296
  43.6 0.0 copy-start
  43.6 0.8 copy-done
  44.4 0.8 copy-done.1
  45.2 4.6 %sketch3.1 = f32[512,256]{1,0:T(8,128)} custom-call(bf16[10240,128]{1,0:T(8,128)(2,1)} %place.1.wide, bf16[1024,256]{1,0:T(8,128)(2,1)} %refs_0_.7, bf16[512,256]{1,0:T(8,128)(2,1)} %copy-done.2, bf16[512,256]{1,0:T(8,128)(2,1)} %copy-done.3, bf16[1024,256]{1,0:T(8,128)(2,1)} %copy-done, bf16[1024,256]{1,0:T(8,128)(2,1)} %copy-done.1), custom_call_target="tpu_custom_call" | custom-call | tf_op jit(solution)/shard_map/sketch3/pallas_call | solution.py:305
  49.7 2.5 %collective-permute-start.14 = (f32[512,256]{1,0:T(8,128)}, f32[512,256]{1,0:T(8,128)S(1)}, u32[]{:S(2)}, u32[]{:S(2)}) collective-permute-start(f32[512,256]{1,0:T(8,128)} %sketch3.1), channel_id=1, source_target_pairs={{0,24},{1,7},{2,26},{3,5},{4,28},{5,3},{6,30},{7,1},{8,16},{9,15},... | collective-permute-start | bytes 1572872 | tf_op jit(solution)/shard_map/ppermute | solution.py:313
  52.3 4.6 %sketch2.1 = f32[512,256]{1,0:T(8,128)} custom-call(bf16[10240,128]{1,0:T(8,128)(2,1)} %place.1.wide, bf16[1024,256]{1,0:T(8,128)(2,1)} %refs_0_.7, bf16[512,256]{1,0:T(8,128)(2,1)} %copy-done.2, bf16[512,256]{1,0:T(8,128)(2,1)} %copy-done.3, bf16[1024,256]{1,0:T(8,128)(2,1)} %copy-done, bf16[1024,256]{1,0:T(8,128)(2,1)} %copy-done.1), custom_call_target="tpu_custom_call" | custom-call | tf_op jit(solution)/shard_map/sketch2/pallas_call | solution.py:305
  56.9 4.5 %sketch1.1 = f32[512,256]{1,0:T(8,128)} custom-call(bf16[10240,128]{1,0:T(8,128)(2,1)} %place.1.wide, bf16[1024,256]{1,0:T(8,128)(2,1)} %refs_0_.7, bf16[512,256]{1,0:T(8,128)(2,1)} %copy-done.2, bf16[512,256]{1,0:T(8,128)(2,1)} %copy-done.3, bf16[1024,256]{1,0:T(8,128)(2,1)} %copy-done, bf16[1024,256]{1,0:T(8,128)(2,1)} %copy-done.1), custom_call_target="tpu_custom_call" | custom-call | tf_op jit(solution)/shard_map/sketch1/pallas_call | solution.py:305
  61.4 1.8 %collective-permute-start.16 = (f32[512,256]{1,0:T(8,128)}, f32[512,256]{1,0:T(8,128)S(1)}, u32[]{:S(2)}, u32[]{:S(2)}) collective-permute-start(f32[512,256]{1,0:T(8,128)} %sketch1.1), channel_id=1, source_target_pairs={{0,8},{1,3},{2,10},{3,1},{4,12},{5,7},{6,14},{7,5},{8,0},{9,11},{1... | collective-permute-start | bytes 1572872 | tf_op jit(solution)/shard_map/ppermute | solution.py:313
  63.2 4.5 %sketch0.1 = f32[512,256]{1,0:T(8,128)} custom-call(bf16[10240,128]{1,0:T(8,128)(2,1)} %place.1.wide, bf16[1024,256]{1,0:T(8,128)(2,1)} %refs_0_.7, bf16[512,256]{1,0:T(8,128)(2,1)} %copy-done.2, bf16[512,256]{1,0:T(8,128)(2,1)} %copy-done.3, bf16[1024,256]{1,0:T(8,128)(2,1)} %copy-done, bf16[1024,256]{1,0:T(8,128)(2,1)} %copy-done.1), custom_call_target="tpu_custom_call" | custom-call | tf_op jit(solution)/shard_map/sketch0/pallas_call | solution.py:305
  67.8 7.6 %collective-permute-done.15 = f32[512,256]{1,0:T(8,128)S(1)} collective-permute-done((f32[512,256]{1,0:T(8,128)}, f32[512,256]{1,0:T(8,128)S(1)}, u32[]{:S(2)}, u32[]{:S(2)}) %collective-permute-start.15) | collective-permute-done | bytes 524320 | tf_op jit(solution)/shard_map/ppermute | solution.py:313
  75.3 1.1 collective-permute-done.16
  76.4 1.2 add_add_fusion.own_ref.sown
  77.6 0.1 collective-permute-start.17
  77.7 1.9 %collective-permute-done.17.other_ref.sother = f32[512,256]{1,0:T(8,128)S(1)} collective-permute-done((f32[512,256]{1,0:T(8,128)S(1)}, f32[512,256]{1,0:T(8,128)S(1)}, u32[]{:S(2)}, u32[]{:S(2)}) %collective-permute-start.17) | collective-permute-done | bytes 524320 | tf_op jit(solution)/shard_map/ppermute | solution.py:317
  79.6 0.8 copy-done.5
  80.4 3.3 %gram.1 = f32[128,640]{1,0:T(8,128)} custom-call(f32[512,256]{1,0:T(8,128)} %copy-done.4, f32[512,256]{1,0:T(8,128)} %copy-done.5), custom_call_target="tpu_custom_call" | custom-call | tf_op jit(solution)/shard_map/gram/pallas_call | solution.py:320
  83.7 16.5 %all_to_all.10 = f32[16,8,640]{2,1,0:T(8,128)S(1)} all-to-all(f32[16,8,640]{2,1,0:T(8,128)} %bitcast.4), channel_id=1, replica_groups=mesh['grp'=1,'tm'=16,'panel'=2] {'tm'}, dimensions={0} | all-to-all | bytes 655360 | tf_op jit(solution)/shard_map/all_to_all | solution.py:327
  100.3 14.2 %all_to_all.11 = f32[16,8,640]{2,1,0:T(8,128)S(1)} all-to-all(f32[16,8,640]{2,1,0:T(8,128)S(1)} %broadcast_in_dim.2), channel_id=1, replica_groups=mesh['grp'=1,'tm'=16,'panel'=2] {'tm'}, dimensions={0} | all-to-all | bytes 655360 | tf_op jit(solution)/shard_map/all_to_all | solution.py:330
  114.4 1.6 %collective-permute-done.18.gother = f32[128,640]{1,0:T(8,128)S(1)} collective-permute-done((f32[128,640]{1,0:T(8,128)S(1)}, f32[128,640]{1,0:T(8,128)S(1)}, u32[]{:S(2)}, u32[]{:S(2)}) %collective-permute-start.18) | collective-permute-done | bytes 327712 | tf_op jit(solution)/shard_map/ppermute | solution.py:331
  116.1 0.7 copy-done.8
  116.8 24.1 %factor.1 = (f32[512,256]{1,0:T(8,128)}, f32[512,256]{1,0:T(8,128)}) custom-call(f32[128,640]{1,0:T(8,128)} %bitcast.3, f32[128,640]{1,0:T(8,128)} %copy-done.8, f32[512,256]{1,0:T(8,128)} %copy-done.4, f32[512,256]{1,0:T(8,128)} %copy-done.5), custom_call_target="tpu_custom_call" | custom-call | tf_op jit(solution)/shard_map/factor/pallas_call | solution.py:334
  (38 shorter events, 0.2 us)
Async XLA Ops:
  1.7 22.3 %collective-permute-start.10 = (bf16[512,256]{1,0:T(8,128)(2,1)S(1)}, bf16[512,256]{1,0:T(8,128)(2,1)S(1)}, u32[]{:S(2)}, u32[]{:S(2)}) collective-permute-start(bf16[512,256]{1,0:T(8,128)(2,1)S(1)} %get-tuple-element.3), channel_id=1, source_target_pairs={{0,2},{1,9},{2,0},{3,11},{4,6},{5,13},{6,4},{7,15},{8,10},{9,1},{1... | collective-permute-start | bytes 786440 | tf_op jit(solution)/shard_map/ppermute | solution.py:72
  8.0 7.0 %collective-permute-start.2 = (bf16[256,128]{1,0:T(8,128)(2,1)}, bf16[256,128]{1,0:T(8,128)(2,1)S(1)}, u32[]{:S(2)}, u32[]{:S(2)}) collective-permute-start(bf16[256,128]{1,0:T(8,128)(2,1)} %widen.1), channel_id=1, source_target_pairs={{0,24},{2,26},{4,28},{6,30},{8,16},{10,18},{12,20},{14,22},{16,8},... | collective-permute-start | bytes 196616 | tf_op jit(solution)/shard_map/ppermute | solution.py:289
  11.6 9.0 %collective-permute-start.1 = (bf16[256,128]{1,0:T(8,128)(2,1)}, bf16[256,128]{1,0:T(8,128)(2,1)S(1)}, u32[]{:S(2)}, u32[]{:S(2)}) collective-permute-start(bf16[256,128]{1,0:T(8,128)(2,1)} %widen.1), channel_id=1, source_target_pairs={{0,16},{2,18},{4,20},{6,22},{8,24},{10,26},{12,28},{14,30},{16,0},... | collective-permute-start | bytes 196616 | tf_op jit(solution)/shard_map/ppermute | solution.py:289
  11.6 9.0 %collective-permute-start = (bf16[256,128]{1,0:T(8,128)(2,1)}, bf16[256,128]{1,0:T(8,128)(2,1)S(1)}, u32[]{:S(2)}, u32[]{:S(2)}) collective-permute-start(bf16[256,128]{1,0:T(8,128)(2,1)} %widen.1), channel_id=1, source_target_pairs={{0,8},{2,10},{4,12},{6,14},{8,0},{10,2},{12,4},{14,6},{16,24},{18,... | collective-permute-start | bytes 196616 | tf_op jit(solution)/shard_map/ppermute | solution.py:289
  12.4 12.8 %collective-permute-start.11 = (bf16[512,256]{1,0:T(8,128)(2,1)S(1)}, bf16[512,256]{1,0:T(8,128)(2,1)S(1)}, u32[]{:S(2)}, u32[]{:S(2)}) collective-permute-start(bf16[512,256]{1,0:T(8,128)(2,1)S(1)} %get-tuple-element.2), channel_id=1, source_target_pairs={{0,4},{1,17},{2,6},{3,19},{4,0},{5,21},{6,2},{7,23},{8,12},{9,25},... | collective-permute-start | bytes 786440 | tf_op jit(solution)/shard_map/ppermute | solution.py:72
  21.5 17.6 %copy-start.7 = (bf16[1024,128]{1,0:T(8,128)(2,1)}, bf16[1024,128]{1,0:T(8,128)(2,1)S(1)}, u32[]{:S(2)}) copy-start(bf16[1024,128]{1,0:T(8,128)(2,1)S(1)} %pad_maximum_fusion.2.refs_0_) | copy-start | bytes 786436
  21.5 5.3 %collective-permute-start.6 = (bf16[1024,128]{1,0:T(8,128)(2,1)S(1)}, bf16[1024,128]{1,0:T(8,128)(2,1)S(1)}, u32[]{:S(2)}, u32[]{:S(2)}) collective-permute-start(bf16[1024,128]{1,0:T(8,128)(2,1)S(1)} %pad_maximum_fusion.2.refs_0_), channel_id=1, source_target_pairs={{0,1},{1,0},{2,3},{3,2},{4,5},{5,4},{6,7},{7,6},{8,9},{9,8},{10,11... | collective-permute-start | bytes 786440 | tf_op jit(solution)/shard_map/ppermute | solution.py:294
  21.6 10.2 %collective-permute-start.5 = (bf16[1024,128]{1,0:T(8,128)(2,1)S(1)}, bf16[1024,128]{1,0:T(8,128)(2,1)S(1)}, u32[]{:S(2)}, u32[]{:S(2)}) collective-permute-start(bf16[1024,128]{1,0:T(8,128)(2,1)S(1)} %pad_maximum_fusion.2.refs_0_), channel_id=1, source_target_pairs={{0,6},{2,4},{4,2},{6,0},{8,14},{10,12},{12,10},{14,8},{16,22},{18,... | collective-permute-start | bytes 786440 | tf_op jit(solution)/shard_map/ppermute | solution.py:293
  23.5 13.3 %collective-permute-start.4 = (bf16[1024,128]{1,0:T(8,128)(2,1)S(1)}, bf16[1024,128]{1,0:T(8,128)(2,1)S(1)}, u32[]{:S(2)}, u32[]{:S(2)}) collective-permute-start(bf16[1024,128]{1,0:T(8,128)(2,1)S(1)} %pad_maximum_fusion.2.refs_0_), channel_id=1, source_target_pairs={{0,4},{2,6},{4,0},{6,2},{8,12},{10,14},{12,8},{14,10},{16,20},{18,... | collective-permute-start | bytes 786440 | tf_op jit(solution)/shard_map/ppermute | solution.py:293
  24.0 19.5 %copy-start.2 = (bf16[512,256]{1,0:T(8,128)(2,1)}, bf16[512,256]{1,0:T(8,128)(2,1)S(1)}, u32[]{:S(2)}) copy-start(bf16[512,256]{1,0:T(8,128)(2,1)S(1)} %collective-permute-done.10.refs_1_) | copy-start | bytes 786436
  24.0 12.9 %collective-permute-start.3 = (bf16[1024,128]{1,0:T(8,128)(2,1)S(1)}, bf16[1024,128]{1,0:T(8,128)(2,1)S(1)}, u32[]{:S(2)}, u32[]{:S(2)}) collective-permute-start(bf16[1024,128]{1,0:T(8,128)(2,1)S(1)} %pad_maximum_fusion.2.refs_0_), channel_id=1, source_target_pairs={{0,2},{2,0},{4,6},{6,4},{8,10},{10,8},{12,14},{14,12},{16,18},{18,... | collective-permute-start | bytes 786440 | tf_op jit(solution)/shard_map/ppermute | solution.py:293
  25.2 18.4 %copy-start.3 = (bf16[512,256]{1,0:T(8,128)(2,1)}, bf16[512,256]{1,0:T(8,128)(2,1)S(1)}, u32[]{:S(2)}) copy-start(bf16[512,256]{1,0:T(8,128)(2,1)S(1)} %collective-permute-done.11.refs_2_) | copy-start | bytes 786436
  25.2 18.4 %collective-permute-start.12 = (bf16[1024,256]{1,0:T(8,128)(2,1)S(1)}, bf16[1024,256]{1,0:T(8,128)(2,1)S(1)}, u32[]{:S(2)}, u32[]{:S(2)}) collective-permute-start(bf16[1024,256]{1,0:T(8,128)(2,1)S(1)} %pad_maximum_fusion), channel_id=1, source_target_pairs={{0,4},{1,17},{2,6},{3,19},{4,0},{5,21},{6,2},{7,23},{8,12},{9,25},... | collective-permute-start | bytes 1572872 | tf_op jit(solution)/shard_map/ppermute | solution.py:72
  26.8 12.2 %copy-start.9 = (bf16[1024,128]{1,0:T(8,128)(2,1)}, bf16[1024,128]{1,0:T(8,128)(2,1)S(1)}, u32[]{:S(2)}) copy-start(bf16[1024,128]{1,0:T(8,128)(2,1)S(1)} %collective-permute-done.6.refs_4_) | copy-start | bytes 786436
  26.8 16.8 %collective-permute-start.13 = (bf16[1024,256]{1,0:T(8,128)(2,1)S(1)}, bf16[1024,256]{1,0:T(8,128)(2,1)S(1)}, u32[]{:S(2)}, u32[]{:S(2)}) collective-permute-start(bf16[1024,256]{1,0:T(8,128)(2,1)S(1)} %pad_maximum_fusion.1), channel_id=1, source_target_pairs={{0,2},{1,9},{2,0},{3,11},{4,6},{5,13},{6,4},{7,15},{8,10},{9,1},{1... | collective-permute-start | bytes 1572872 | tf_op jit(solution)/shard_map/ppermute | solution.py:72
  31.8 5.1 %copy-start.10 = (bf16[1024,128]{1,0:T(8,128)(2,1)}, bf16[1024,128]{1,0:T(8,128)(2,1)S(1)}, u32[]{:S(2)}) copy-start(bf16[1024,128]{1,0:T(8,128)(2,1)S(1)} %collective-permute-done.5.refs_3_) | copy-start | bytes 786436
  31.8 5.6 %collective-permute-start.9 = (bf16[1024,128]{1,0:T(8,128)(2,1)S(1)}, bf16[1024,128]{1,0:T(8,128)(2,1)S(1)}, u32[]{:S(2)}, u32[]{:S(2)}) collective-permute-start(bf16[1024,128]{1,0:T(8,128)(2,1)S(1)} %collective-permute-done.5.refs_3_), channel_id=1, source_target_pairs={{0,1},{1,0},{2,3},{3,2},{4,5},{5,4},{6,7},{7,6},{8,9},{9,8},{10,11... | collective-permute-start | bytes 786440 | tf_op jit(solution)/shard_map/ppermute | solution.py:294
  36.8 0.7 copy-start.11
  36.8 1.5 %collective-permute-start.8 = (bf16[1024,128]{1,0:T(8,128)(2,1)S(1)}, bf16[1024,128]{1,0:T(8,128)(2,1)S(1)}, u32[]{:S(2)}, u32[]{:S(2)}) collective-permute-start(bf16[1024,128]{1,0:T(8,128)(2,1)S(1)} %collective-permute-done.4.refs_2_), channel_id=1, source_target_pairs={{0,1},{1,0},{2,3},{3,2},{4,5},{5,4},{6,7},{7,6},{8,9},{9,8},{10,11... | collective-permute-start | bytes 786440 | tf_op jit(solution)/shard_map/ppermute | solution.py:294
  36.9 1.4 %copy-start.12 = (bf16[1024,128]{1,0:T(8,128)(2,1)}, bf16[1024,128]{1,0:T(8,128)(2,1)S(1)}, u32[]{:S(2)}) copy-start(bf16[1024,128]{1,0:T(8,128)(2,1)S(1)} %collective-permute-done.3.refs_1_) | copy-start | bytes 786436
  36.9 2.1 %collective-permute-start.7 = (bf16[1024,128]{1,0:T(8,128)(2,1)S(1)}, bf16[1024,128]{1,0:T(8,128)(2,1)}, u32[]{:S(2)}, u32[]{:S(2)}) collective-permute-start(bf16[1024,128]{1,0:T(8,128)(2,1)S(1)} %collective-permute-done.3.refs_1_), channel_id=1, source_target_pairs={{0,1},{1,0},{2,3},{3,2},{4,5},{5,4},{6,7},{7,6},{8,9},{9,8},{10,11... | collective-permute-start | bytes 786440 | tf_op jit(solution)/shard_map/ppermute | solution.py:294
  37.5 1.5 %copy-start.13 = (bf16[1024,128]{1,0:T(8,128)(2,1)}, bf16[1024,128]{1,0:T(8,128)(2,1)S(1)}, u32[]{:S(2)}) copy-start(bf16[1024,128]{1,0:T(8,128)(2,1)S(1)} %collective-permute-done.9.refs_7_) | copy-start | bytes 786436
  38.3 0.7 copy-start.14
  43.6 0.8 copy-start
  44.4 0.8 copy-start.1
  49.7 18.0 %collective-permute-start.14 = (f32[512,256]{1,0:T(8,128)}, f32[512,256]{1,0:T(8,128)S(1)}, u32[]{:S(2)}, u32[]{:S(2)}) collective-permute-start(f32[512,256]{1,0:T(8,128)} %sketch3.1), channel_id=1, source_target_pairs={{0,24},{1,7},{2,26},{3,5},{4,28},{5,3},{6,30},{7,1},{8,16},{9,15},... | collective-permute-start | bytes 1572872 | tf_op jit(solution)/shard_map/ppermute | solution.py:313
  56.8 18.5 %collective-permute-start.15 = (f32[512,256]{1,0:T(8,128)}, f32[512,256]{1,0:T(8,128)S(1)}, u32[]{:S(2)}, u32[]{:S(2)}) collective-permute-start(f32[512,256]{1,0:T(8,128)} %sketch2.1), channel_id=1, source_target_pairs={{0,16},{1,5},{2,18},{3,7},{4,20},{5,1},{6,22},{7,3},{8,24},{9,13},... | collective-permute-start | bytes 1572872 | tf_op jit(solution)/shard_map/ppermute | solution.py:313
  61.4 15.0 %collective-permute-start.16 = (f32[512,256]{1,0:T(8,128)}, f32[512,256]{1,0:T(8,128)S(1)}, u32[]{:S(2)}, u32[]{:S(2)}) collective-permute-start(f32[512,256]{1,0:T(8,128)} %sketch1.1), channel_id=1, source_target_pairs={{0,8},{1,3},{2,10},{3,1},{4,12},{5,7},{6,14},{7,5},{8,0},{9,11},{1... | collective-permute-start | bytes 1572872 | tf_op jit(solution)/shard_map/ppermute | solution.py:313
  77.6 2.0 %copy-start.4 = (f32[512,256]{1,0:T(8,128)}, f32[512,256]{1,0:T(8,128)S(1)}, u32[]{:S(2)}) copy-start(f32[512,256]{1,0:T(8,128)S(1)} %add_add_fusion.own_ref.sown) | copy-start | bytes 1572868
  77.6 2.0 %collective-permute-start.17 = (f32[512,256]{1,0:T(8,128)S(1)}, f32[512,256]{1,0:T(8,128)S(1)}, u32[]{:S(2)}, u32[]{:S(2)}) collective-permute-start(f32[512,256]{1,0:T(8,128)S(1)} %add_add_fusion.own_ref.sown), channel_id=1, source_target_pairs={{0,1},{1,0},{2,3},{3,2},{4,5},{5,4},{6,7},{7,6},{8,9},{9,8},{10,11... | collective-permute-start | bytes 1572872 | tf_op jit(solution)/shard_map/ppermute | solution.py:317
  79.6 0.8 copy-start.5
  114.4 1.6 %copy-start.6 = (f32[16,8,640]{2,1,0:T(8,128)}, f32[16,8,640]{2,1,0:T(8,128)S(1)}, u32[]{:S(2)}) copy-start(f32[16,8,640]{2,1,0:T(8,128)S(1)} %all_to_all.11) | copy-start | bytes 983044
  114.4 1.6 %collective-permute-start.18 = (f32[128,640]{1,0:T(8,128)S(1)}, f32[128,640]{1,0:T(8,128)S(1)}, u32[]{:S(2)}, u32[]{:S(2)}) collective-permute-start(f32[128,640]{1,0:T(8,128)S(1)} %bitcast.2), channel_id=1, source_target_pairs={{0,1},{1,0},{2,3},{3,2},{4,5},{5,4},{6,7},{7,6},{8,9},{9,8},{10,11... | collective-permute-start | bytes 983048 | tf_op jit(solution)/shard_map/ppermute | solution.py:331
  116.1 0.7 copy-start.8

commit v4 on v3

--- a/solution.py
+++ b/solution.py
@@ -99,27 +99,50 @@
     out[...] = jnp.concatenate([now[:count], now[LAG_SPACING : LAG_SPACING + count]], 1)
 
 
-def place_kernel(plan, *refs):
-    wide = refs[-1]
+def place_kernel(plan, moves, *refs):
+    stacks = refs[: 2 * plan.lo]
+    blocks = refs[2 * plan.lo : -4]
+    wide, matrix, record_sem, block_sem = refs[-4:]
     i = lax.axis_index("tm")
     panel = lax.axis_index("panel")
     hi, lo = i // plan.lo, i % plan.lo
-    count = refs[0].shape[0] // plan.hi
+    count = stacks[0].shape[0] // plan.hi
     rows = 2 * count
     total = plan.n * rows
     variables = wide.shape[1] // 2
+
+    def record_copy(side, slo, shi):
+        slab = (hi ^ shi) * plan.lo + (lo ^ slo)
+        first = slab * rows + lax.rem(panel + side, 2) * count
+        return pltpu.make_async_copy(
+            stacks[side * plan.lo + slo].at[pl.ds(pl.multiple_of(shi * count, count), count), :],
+            wide.at[pl.ds(pl.multiple_of(first, count), count), :],
+            record_sem.at[(side * plan.lo + slo) * plan.hi + shi],
+        )
+
+    copies = []
+    for at, (array, row, size, target) in enumerate(moves):
+        copies.append(
+            pltpu.make_async_copy(
+                blocks[array].at[row : row + size, :], matrix.at[target : target + size, :], block_sem.at[at]
+            )
+        )
+    for side in range(2):
+        for slo in range(plan.lo):
+
+            @pl.loop(0, plan.hi)
+            def _(shi):
+                record_copy(side, slo, shi).start()
+
+    for copy in copies:
+        copy.start()
     wide[total:, :] = jnp.zeros((wide.shape[0] - total, wide.shape[1]), wide.dtype)
     for side in range(2):
         for slo in range(plan.lo):
-            ref = refs[side * plan.lo + slo]
 
             @pl.loop(0, plan.hi)
             def _(shi):
-                slab = (hi ^ shi) * plan.lo + (lo ^ slo)
-                first = slab * rows + lax.rem(panel + side, 2) * count
-                wide[pl.ds(pl.multiple_of(first, count), count), :] = ref[
-                    pl.ds(pl.multiple_of(shi * count, count), count), :
-                ]
+                record_copy(side, slo, shi).wait()
 
     @pl.loop(1, plan.n + 1)
     def _(k):
@@ -129,14 +152,17 @@
         right = jnp.concatenate([before[:LAG_SPACING, variables:], after[:LAG_SPACING, :variables]], 0)
         wide[pl.ds(edge - 16, 16), :] = jnp.concatenate([before[:, :variables], right], 1)
 
-
-def sketch_kernel(plan, rows, depth, variables, where, sb, wide, *refs):
-    blocks, out = refs[:-1], refs[-1]
+    for copy in copies:
+        copy.wait()
+
+
+def sketch_kernel(plan, rows, depth, variables, sb, wide, matrix, out):
     i = lax.axis_index("tm")
     panel = lax.axis_index("panel")
     a, b = plan.coords(i, panel)
     shift = depth // variables * LAG_SPACING
     slab = plan.index(a, b ^ sb, panel)
+    chunk = min(256, depth)
 
     @pl.loop(0, rows // TILE)
     def _(k):
@@ -145,18 +171,14 @@
         for sa in range(plan.na):
             block = plan.index(a ^ sa, b, panel)
             base = pl.multiple_of(slab * rows + block * shift + start, 16)
-            past = 0
-            for array, row, count in where[sa]:
-                chunk = min(256, count)
-                for first in range(0, count, chunk):
-                    pieces = []
-                    for col in range(past + first, past + first + chunk, 2 * variables):
-                        offset = col // variables * LAG_SPACING
-                        pieces.append(wide[pl.ds(base + offset, TILE), :])
-                    left = jnp.concatenate(pieces, 1) if len(pieces) > 1 else pieces[0]
-                    right = blocks[array][row + first : row + first + chunk, :]
-                    acc = acc + jnp.dot(left, right, preferred_element_type=jnp.float32)
-                past += count
+            for first in range(0, depth, chunk):
+                pieces = []
+                for col in range(first, first + chunk, 2 * variables):
+                    offset = col // variables * LAG_SPACING
+                    pieces.append(wide[pl.ds(base + offset, TILE), :])
+                left = jnp.concatenate(pieces, 1) if len(pieces) > 1 else pieces[0]
+                right = matrix[sa * depth + first : sa * depth + first + chunk, :]
+                acc = acc + jnp.dot(left, right, preferred_element_type=jnp.float32)
         out[pl.ds(start, TILE), :] = acc
 
 
@@ -208,7 +230,12 @@
             w[end:, :] = w[end:, :] - dot_tn(rows[:, end:NB], rows)
 
 
-def factor_kernel(factor, gown, gother, sown, sother, basis_ref, tri_ref, a, w, r, v):
+def factor_kernel(factor, gown, gother, sown_hbm, sother_hbm, basis_hbm, tri_hbm, *scratch):
+    a, w, r, v, sown, sother, basis_ref, tri_ref, sem = scratch
+    own_in = pltpu.make_async_copy(sown_hbm, sown, sem.at[0])
+    other_in = pltpu.make_async_copy(sother_hbm, sother, sem.at[1])
+    own_in.start()
+    other_in.start()
     half = sown.shape[1]
     n = 2 * half
     panel = lax.axis_index("panel")
@@ -258,16 +285,51 @@
     @pl.when(panel == 0)
     def _():
         tri_ref[...] = r[:, :half] * (1.0 / factor)
-        basis_ref[...] = dot_nn(sown[...], v[:half, :half]) * factor
 
     @pl.when(panel == 1)
     def _():
         tri_ref[...] = r[:, half:] * (1.0 / factor)
-        basis_ref[...] = (dot_nn(sother[...], v[:half, half:]) + dot_nn(sown[...], v[half:, half:])) * factor
+
+    tri_out = pltpu.make_async_copy(tri_ref, tri_hbm, sem.at[2])
+    tri_out.start()
+    own_in.wait()
+    other_in.wait()
+    outs = []
+    piece = basis_ref.shape[0] // 2
+    for part in range(2):
+        at = slice(part * piece, (part + 1) * piece)
+
+        @pl.when(panel == 0)
+        def _():
+            basis_ref[at, :] = dot_nn(sown[at, :], v[:half, :half] * factor)
+
+        @pl.when(panel == 1)
+        def _():
+            basis_ref[at, :] = dot_nn(sother[at, :], v[:half, half:] * factor) + dot_nn(
+                sown[at, :], v[half:, half:] * factor
+            )
+
+        outs.append(pltpu.make_async_copy(basis_ref.at[at, :], basis_hbm.at[at, :], sem.at[3 + part]))
+        outs[-1].start()
+    tri_out.wait()
+    for out in outs:
+        out.wait()
 
 
 def vmem(count):
     return [pl.BlockSpec(memory_space=pltpu.VMEM)] * count
+
+
+def scoped(mebibytes):
+    return pltpu.CompilerParams(vmem_limit_bytes=mebibytes << 20)
+
+
+def anywhere(count):
+    return [pl.BlockSpec(memory_space=pl.ANY)] * count
+
+
+def in_vmem(value):
+    return pltpu.with_memory_space_constraint(value, pltpu.VMEM)
 
 
 def per_device(series, test_matrix):
@@ -283,6 +345,7 @@
         out_specs=vmem(1)[0],
         scratch_shapes=[pltpu.VMEM((rows + 16, variables), jnp.bfloat16)],
         name="widen",
+        compiler_params=scoped(8),
     )(series)
     pieces = [own_rows]
     for s in range(1, plan.hi):
@@ -293,22 +356,38 @@
         stacks.append(lax.ppermute(stack, "tm", plan.plain_pairs(0, s)))
     stacks = stacks + [lax.ppermute(value, "panel", SWAP) for value in stacks]
     length = n * rows + WINDOW_LAGS * LAG_SPACING
-    wide = pl.pallas_call(
-        functools.partial(place_kernel, plan),
-        out_shape=jax.ShapeDtypeStruct((length, 2 * variables), jnp.bfloat16),
-        in_specs=vmem(2 * plan.lo),
-        out_specs=vmem(1)[0],
+    moves = []
+    for s, parts in enumerate(where):
+        target = s * depth
+        for array, row, size in parts:
+            moves.append((array, row, size, target))
+            target += size
+    wide, matrix = pl.pallas_call(
+        functools.partial(place_kernel, plan, moves),
+        out_shape=[
+            pltpu.VMEM((length, 2 * variables), jnp.bfloat16),
+            pltpu.VMEM((plan.na * depth, half), jnp.bfloat16),
+        ],
+        in_specs=anywhere(len(stacks) + len(arrays)),
+        out_specs=vmem(2),
+        scratch_shapes=[pltpu.SemaphoreType.DMA((2 * n,)), pltpu.SemaphoreType.DMA((len(moves),))],
         name="place",
-    )(*stacks)
+        compiler_params=scoped(8),
+    )(*stacks, *arrays)
+    wide, matrix = in_vmem(wide), in_vmem(matrix)
 
     def part(sb):
         return pl.pallas_call(
-            functools.partial(sketch_kernel, plan, rows, depth, variables, where, sb),
+            functools.partial(sketch_kernel, plan, rows, depth, variables, sb),
             out_shape=jax.ShapeDtypeStruct((rows, half), jnp.float32),
-            in_specs=vmem(1 + len(arrays)),
+            in_specs=vmem(2),
             out_specs=vmem(1)[0],
             name="sketch%d" % sb,
-        )(wide, *arrays)
+            compiler_params=scoped(8),
+            cost_estimate=pl.CostEstimate(
+                flops=2 * rows * plan.na * depth * half, bytes_accessed=4 * rows * half, transcendentals=0
+            ),
+        )(wide, matrix)
 
     arrived = [lax.ppermute(part(s), BOTH, plan.pairs(0, s)) for s in reversed(range(1, plan.nb))]
     own = part(0)
@@ -323,7 +402,8 @@
         in_specs=vmem(2),
         out_specs=vmem(1)[0],
         name="gram",
-    )(own, other)
+        compiler_params=scoped(16),
+    )(in_vmem(own), in_vmem(other))
     spread = lax.all_to_all(gram.reshape(n, NB // n, width), "tm", 0, 0, tiled=True)
     summed = jnp.sum(spread, 0)
     alike = jnp.broadcast_to(summed[None], (n, NB // n, width))
@@ -337,15 +417,21 @@
                 jax.ShapeDtypeStruct((rows, half), jnp.float32),
                 jax.ShapeDtypeStruct((full, half), jnp.float32),
             ],
-            in_specs=vmem(4),
-            out_specs=vmem(2),
+            in_specs=vmem(2) + anywhere(2),
+            out_specs=anywhere(2),
             scratch_shapes=[
                 pltpu.VMEM((full, full), jnp.float32),
                 pltpu.VMEM((NB, 2 * NB), jnp.float32),
                 pltpu.VMEM((full, full), jnp.float32),
                 pltpu.VMEM((full, full), jnp.float32),
+                pltpu.VMEM((rows, half), jnp.float32),
+                pltpu.VMEM((rows, half), jnp.float32),
+                pltpu.VMEM((rows, half), jnp.float32),
+                pltpu.VMEM((full, half), jnp.float32),
+                pltpu.SemaphoreType.DMA((5,)),
             ],
             name="factor",
+            compiler_params=scoped(24),
         )(gram, gram_other, own, other)
     )
 

time: 142 us -> 132 us (0.930)
  Pallas kernels: 51.8 us -> 35 us
  waiting for transfers between devices: 28.7 us -> 44.2 us
  local copies, waits for them, and re-layouts: 6.67 us -> 2.1 us
  other arithmetic: 2.13 us -> 0.25 us
  blocking collectives: 30.7 us -> 28.9 us
    pallas_call x4, Pallas kernels: 18.2 us -> 5.87 us  [part(): pl.pallas_call(functools.partial(sketch_kernel, plan, rows, depth, variab...]
    ppermute x3, waiting for transfers between devices: 8.62 us -> 18.9 us  [per_device(): lax.ppermute(part(s), BOTH, plan.pairs(0, s))]
    unnamed x31 -> x3, local copies, waits for them, and re-layouts: 5.58 us -> 0.96 us
    ppermute x4, waiting for transfers between devices: 0.01 us -> 3.81 us  [sent(): return lax.ppermute(value, BOTH, plan.pairs(da, 0))]
    pallas_call x1, Pallas kernels: 3.28 us -> 1.36 us  [per_device(): pl.pallas_call(gram_kernel, out_shape=jax.ShapeDtypeStruct((NB, width), j...]
    all_to_all x1, blocking collectives: 16.5 us -> 14.8 us  [per_device(): lax.all_to_all(gram.reshape(n, NB // n, width), 'tm', 0, 0, tiled=True)]
    pallas_call x1, Pallas kernels: 1.65 us -> 0.12 us  [per_device(): pl.pallas_call(widen_kernel, out_shape=jax.ShapeDtypeStruct((rows // 2, 2...]
  transfers between devices with their start and end apart: 19 -> 19, of which waited for: 10 -> 13; matrix products, arithmetic and copies ran while one was open for 2% -> 1% of each run, Pallas kernels for 14% -> 1%
where the time goes in v4:
time: 132 us; the launch traced here: 131 us
  waiting for transfers between devices  44.2 us (33%)
  Pallas kernels  35 us (27%)
  blocking collectives  28.9 us (22%)
  starting transfers between devices  19.7 us (15%)
  local copies, waits for them, and re-layouts  2.1 us (2%)
    pallas_call x1, Pallas kernels, per_device(): pl.pallas_call(functools.partial(factor_kernel, math.sqrt(n * rows)), out...  22.7 us
    ppermute x3, waiting for transfers between devices, per_device(): lax.ppermute(part(s), BOTH, plan.pairs(0, s))  18.9 us
    all_to_all x1, blocking collectives, per_device(): lax.all_to_all(gram.reshape(n, NB // n, width), 'tm', 0, 0, tiled=True)  14.8 us
    all_to_all x1, blocking collectives, per_device(): gram = lax.all_to_all(alike, 'tm', 0, 0, tiled=True).reshape(NB, width)  14.2 us
    ppermute x3, waiting for transfers between devices, per_device(): stacks.append(lax.ppermute(stack, 'tm', plan.plain_pairs(0, s)))  9.56 us
    ppermute x3, waiting for transfers between devices, per_device(): pieces.append(lax.ppermute(own_rows, 'tm', plan.plain_pairs(s, 0)))  6.95 us
    ppermute x4, starting transfers between devices, sent(): return lax.ppermute(value, BOTH, plan.pairs(da, 0))  6.62 us
    pallas_call x4, Pallas kernels, part(): pl.pallas_call(functools.partial(sketch_kernel, plan, rows, depth, variab...  5.87 us
  transfers between devices with their start and end apart: 19, of which 13 were waited for; matrix products, arithmetic and copies ran while one was open for 1% of the time, Pallas kernels for 1%

profile of v4, /device:TPU:0, one launch (start us, length us, event | category | flops | bytes accessed | tf_op | source)
XLA Modules:
  0.0 131.0 jit_solution(1332858210273130154)
XLA Ops:
  0.6 1.1 fusion
  1.8 3.0 %collective-permute-start.10 = (bf16[512,256]{1,0:T(8,128)(2,1)S(1)}, bf16[512,256]{1,0:T(8,128)(2,1)S(1)}, u32[]{:S(2)}, u32[]{:S(2)}) collective-permute-start(bf16[512,256]{1,0:T(8,128)(2,1)S(1)} %get-tuple-element.7), channel_id=1, source_target_pairs={{0,2},{1,9},{2,0},{3,11},{4,6},{5,13},{6,4},{7,15},{8,10},{9,1},{1... | collective-permute-start | bytes 786440 | tf_op jit(solution)/shard_map/ppermute | solution.py:72
  4.8 1.0 copy.4.series
  5.8 0.1 widen.1
  5.9 3.7 %collective-permute-start.2 = (bf16[256,128]{1,0:T(8,128)(2,1)S(1)}, bf16[256,128]{1,0:T(8,128)(2,1)S(1)}, u32[]{:S(2)}, u32[]{:S(2)}) collective-permute-start(bf16[256,128]{1,0:T(8,128)(2,1)S(1)} %widen.1), channel_id=1, source_target_pairs={{0,24},{2,26},{4,28},{6,30},{8,16},{10,18},{12,20},{14,22},{16,8},... | collective-permute-start | bytes 196616 | tf_op jit(solution)/shard_map/ppermute | solution.py:352
  9.5 0.0 collective-permute-start.1
  9.5 0.8 collective-permute-start
  10.3 1.5 %collective-permute-start.11 = (bf16[512,256]{1,0:T(8,128)(2,1)S(1)}, bf16[512,256]{1,0:T(8,128)(2,1)S(1)}, u32[]{:S(2)}, u32[]{:S(2)}) collective-permute-start(bf16[512,256]{1,0:T(8,128)(2,1)S(1)} %get-tuple-element.6), channel_id=1, source_target_pairs={{0,4},{1,17},{2,6},{3,19},{4,0},{5,21},{6,2},{7,23},{8,12},{9,25},... | collective-permute-start | bytes 786440 | tf_op jit(solution)/shard_map/ppermute | solution.py:72
  11.9 0.8 collective-permute-done.2
  12.7 6.1 %collective-permute-done.1 = bf16[256,128]{1,0:T(8,128)(2,1)S(1)} collective-permute-done((bf16[256,128]{1,0:T(8,128)(2,1)S(1)}, bf16[256,128]{1,0:T(8,128)(2,1)S(1)}, u32[]{:S(2)}, u32[]{:S(2)}) %collective-permute-start.1) | collective-permute-done | bytes 65568 | tf_op jit(solution)/shard_map/ppermute | solution.py:352
  18.8 0.0 collective-permute-done
  18.8 0.1 collective-permute-start.6
  18.9 1.4 %collective-permute-start.5 = (bf16[1024,128]{1,0:T(8,128)(2,1)S(1)}, bf16[1024,128]{1,0:T(8,128)(2,1)S(1)}, u32[]{:S(2)}, u32[]{:S(2)}) collective-permute-start(bf16[1024,128]{1,0:T(8,128)(2,1)S(1)} %pad_maximum_fusion.2.refs_0_), channel_id=1, source_target_pairs={{0,6},{2,4},{4,2},{6,0},{8,14},{10,12},{12,10},{14,8},{16,22},{18,... | collective-permute-start | bytes 786440 | tf_op jit(solution)/shard_map/ppermute | solution.py:356
  20.3 0.5 collective-permute-start.4
  20.8 0.0 collective-permute-done.10.refs_9_
  20.8 1.6 %collective-permute-start.3 = (bf16[1024,128]{1,0:T(8,128)(2,1)S(1)}, bf16[1024,128]{1,0:T(8,128)(2,1)S(1)}, u32[]{:S(2)}, u32[]{:S(2)}) collective-permute-start(bf16[1024,128]{1,0:T(8,128)(2,1)S(1)} %pad_maximum_fusion.2.refs_0_), channel_id=1, source_target_pairs={{0,2},{2,0},{4,6},{6,4},{8,10},{10,8},{12,14},{14,12},{16,18},{18,... | collective-permute-start | bytes 786440 | tf_op jit(solution)/shard_map/ppermute | solution.py:356
  22.5 0.0 collective-permute-done.11.refs_10_
  22.5 1.6 %collective-permute-start.12 = (bf16[1024,256]{1,0:T(8,128)(2,1)S(1)}, bf16[1024,256]{1,0:T(8,128)(2,1)S(1)}, u32[]{:S(2)}, u32[]{:S(2)}) collective-permute-start(bf16[1024,256]{1,0:T(8,128)(2,1)S(1)} %pad_maximum_fusion), channel_id=1, source_target_pairs={{0,4},{1,17},{2,6},{3,19},{4,0},{5,21},{6,2},{7,23},{8,12},{9,25},... | collective-permute-start | bytes 1572872 | tf_op jit(solution)/shard_map/ppermute | solution.py:72
  24.1 0.0 collective-permute-done.6.refs_4_
  24.1 0.5 collective-permute-start.13
  24.6 4.5 %collective-permute-done.5.refs_3_ = bf16[1024,128]{1,0:T(8,128)(2,1)S(1)} collective-permute-done((bf16[1024,128]{1,0:T(8,128)(2,1)S(1)}, bf16[1024,128]{1,0:T(8,128)(2,1)S(1)}, u32[]{:S(2)}, u32[]{:S(2)}) %collective-permute-start.5) | collective-permute-done | bytes 262176 | tf_op jit(solution)/shard_map/ppermute | solution.py:356
  29.1 0.0 collective-permute-start.9
  29.1 5.0 %collective-permute-done.4.refs_2_ = bf16[1024,128]{1,0:T(8,128)(2,1)S(1)} collective-permute-done((bf16[1024,128]{1,0:T(8,128)(2,1)S(1)}, bf16[1024,128]{1,0:T(8,128)(2,1)S(1)}, u32[]{:S(2)}, u32[]{:S(2)}) %collective-permute-start.4) | collective-permute-done | bytes 262176 | tf_op jit(solution)/shard_map/ppermute | solution.py:356
  34.1 0.0 collective-permute-start.8
  34.2 0.1 collective-permute-done.3.refs_1_
  34.2 0.4 collective-permute-start.7
  34.6 1.0 collective-permute-done.8.refs_6_
  35.7 0.4 collective-permute-done.7.refs_5_
  36.0 3.7 %collective-permute-done.12.refs_11_ = bf16[1024,256]{1,0:T(8,128)(2,1)S(1)} collective-permute-done((bf16[1024,256]{1,0:T(8,128)(2,1)S(1)}, bf16[1024,256]{1,0:T(8,128)(2,1)S(1)}, u32[]{:S(2)}, u32[]{:S(2)}) %collective-permute-start.12) | collective-permute-done | bytes 524320 | tf_op jit(solution)/shard_map/ppermute | solution.py:72
  39.7 0.1 collective-permute-done.13.refs_12_
  39.9 4.9 %place.1 = (bf16[10240,128]{1,0:T(8,128)(2,1)S(1)}, bf16[4096,256]{1,0:T(8,128)(2,1)S(1)}) custom-call(bf16[1024,128]{1,0:T(8,128)(2,1)S(1)} %pad_maximum_fusion.2.refs_0_, bf16[1024,128]{1,0:T(8,128)(2,1)S(1)} %collective-permute-done.3.refs_1_, bf16[1024,128]{1,0:T(8,128)(2,1)S(1)} %collective-permute-done.4.refs_2_, ...), custom_call_target="tpu_custom_call" | custom-call | tf_op jit(solution)/shard_map/place/pallas_call | solution.py:365
  44.8 1.5 %sketch1.1 = f32[512,256]{1,0:T(8,128)S(1)} custom-call(bf16[10240,128]{1,0:T(8,128)(2,1)S(1)} %get-tuple-element.4.wide, bf16[4096,256]{1,0:T(8,128)(2,1)S(1)} %get-tuple-element.5.matrix), custom_call_target="tpu_custom_call" | custom-call | flops 1073741824 | bytes 524288 | tf_op jit(solution)/shard_map/sketch1/pallas_call | solution.py:380
  46.2 1.5 %sketch2.1 = f32[512,256]{1,0:T(8,128)S(1)} custom-call(bf16[10240,128]{1,0:T(8,128)(2,1)S(1)} %get-tuple-element.4.wide, bf16[4096,256]{1,0:T(8,128)(2,1)S(1)} %get-tuple-element.5.matrix), custom_call_target="tpu_custom_call" | custom-call | flops 1073741824 | bytes 524288 | tf_op jit(solution)/shard_map/sketch2/pallas_call | solution.py:380
  47.7 1.5 %sketch3.1 = f32[512,256]{1,0:T(8,128)S(1)} custom-call(bf16[10240,128]{1,0:T(8,128)(2,1)S(1)} %get-tuple-element.4.wide, bf16[4096,256]{1,0:T(8,128)(2,1)S(1)} %get-tuple-element.5.matrix), custom_call_target="tpu_custom_call" | custom-call | flops 1073741824 | bytes 524288 | tf_op jit(solution)/shard_map/sketch3/pallas_call | solution.py:380
  49.2 2.2 %collective-permute-start.14 = (f32[512,256]{1,0:T(8,128)S(1)}, f32[512,256]{1,0:T(8,128)S(1)}, u32[]{:S(2)}, u32[]{:S(2)}) collective-permute-start(f32[512,256]{1,0:T(8,128)S(1)} %sketch3.1), channel_id=1, source_target_pairs={{0,24},{1,7},{2,26},{3,5},{4,28},{5,3},{6,30},{7,1},{8,16},{9,15},... | collective-permute-start | bytes 1572872 | tf_op jit(solution)/shard_map/ppermute | solution.py:392
  51.4 2.3 %collective-permute-start.16 = (f32[512,256]{1,0:T(8,128)S(1)}, f32[512,256]{1,0:T(8,128)S(1)}, u32[]{:S(2)}, u32[]{:S(2)}) collective-permute-start(f32[512,256]{1,0:T(8,128)S(1)} %sketch1.1), channel_id=1, source_target_pairs={{0,8},{1,3},{2,10},{3,1},{4,12},{5,7},{6,14},{7,5},{8,0},{9,11},{1... | collective-permute-start | bytes 1572872 | tf_op jit(solution)/shard_map/ppermute | solution.py:392
  53.7 1.4 %sketch0.1 = f32[512,256]{1,0:T(8,128)S(1)} custom-call(bf16[10240,128]{1,0:T(8,128)(2,1)S(1)} %get-tuple-element.4.wide, bf16[4096,256]{1,0:T(8,128)(2,1)S(1)} %get-tuple-element.5.matrix), custom_call_target="tpu_custom_call" | custom-call | flops 1073741824 | bytes 524288 | tf_op jit(solution)/shard_map/sketch0/pallas_call | solution.py:380
  55.1 5.3 %collective-permute-done.14 = f32[512,256]{1,0:T(8,128)S(1)} collective-permute-done((f32[512,256]{1,0:T(8,128)S(1)}, f32[512,256]{1,0:T(8,128)S(1)}, u32[]{:S(2)}, u32[]{:S(2)}) %collective-permute-start.14) | collective-permute-done | bytes 524320 | tf_op jit(solution)/shard_map/ppermute | solution.py:392
  60.5 13.6 %collective-permute-done.15 = f32[512,256]{1,0:T(8,128)S(1)} collective-permute-done((f32[512,256]{1,0:T(8,128)S(1)}, f32[512,256]{1,0:T(8,128)S(1)}, u32[]{:S(2)}, u32[]{:S(2)}) %collective-permute-start.15) | collective-permute-done | bytes 524320 | tf_op jit(solution)/shard_map/ppermute | solution.py:392
  74.0 0.1 add_add_fusion.own_ref.sown_hbm
  74.2 0.1 collective-permute-start.17
  74.3 1.9 %collective-permute-done.17.other_ref.sother_hbm = f32[512,256]{1,0:T(8,128)S(1)} collective-permute-done((f32[512,256]{1,0:T(8,128)S(1)}, f32[512,256]{1,0:T(8,128)S(1)}, u32[]{:S(2)}, u32[]{:S(2)}) %collective-permute-start.17) | collective-permute-done | bytes 524320 | tf_op jit(solution)/shard_map/ppermute | solution.py:396
  76.2 1.4 %gram.1 = f32[128,640]{1,0:T(8,128)S(1)} custom-call(f32[512,256]{1,0:T(8,128)S(1)} %add_add_fusion.own_ref.sown_hbm, f32[512,256]{1,0:T(8,128)S(1)} %collective-permute-done.17.other_ref.sother_hbm), custom_call_target="tpu_custom_call" | custom-call | tf_op jit(solution)/shard_map/gram/pallas_call | solution.py:399
  77.5 14.8 %all_to_all.10 = f32[16,8,640]{2,1,0:T(8,128)S(1)} all-to-all(f32[16,8,640]{2,1,0:T(8,128)S(1)} %bitcast.4), channel_id=1, replica_groups=mesh['grp'=1,'tm'=16,'panel'=2] {'tm'}, dimensions={0} | all-to-all | bytes 655360 | tf_op jit(solution)/shard_map/all_to_all | solution.py:407
  92.4 14.2 %all_to_all.11 = f32[16,8,640]{2,1,0:T(8,128)S(1)} all-to-all(f32[16,8,640]{2,1,0:T(8,128)S(1)} %broadcast_in_dim.2), channel_id=1, replica_groups=mesh['grp'=1,'tm'=16,'panel'=2] {'tm'}, dimensions={0} | all-to-all | bytes 655360 | tf_op jit(solution)/shard_map/all_to_all | solution.py:410
  106.5 0.0 collective-permute-start.18
  106.5 1.6 %collective-permute-done.18.gother = f32[128,640]{1,0:T(8,128)S(1)} collective-permute-done((f32[128,640]{1,0:T(8,128)S(1)}, f32[128,640]{1,0:T(8,128)S(1)}, u32[]{:S(2)}, u32[]{:S(2)}) %collective-permute-start.18) | collective-permute-done | bytes 327712 | tf_op jit(solution)/shard_map/ppermute | solution.py:411
  108.2 22.7 %factor.1 = (f32[512,256]{1,0:T(8,128)}, f32[512,256]{1,0:T(8,128)}) custom-call(f32[128,640]{1,0:T(8,128)S(1)} %bitcast.3, f32[128,640]{1,0:T(8,128)S(1)} %collective-permute-done.18.gother, f32[512,256]{1,0:T(8,128)S(1)} %add_add_fusion.own_ref.sown_hbm, f32[512,256]{1,0:T(8,128)S(1)} %collective-permute-done.17.other_ref.sother_hbm), custom_call_target="tpu_custom_call" | custom-call | tf_op jit(solution)/shard_map/factor/pallas_call | solution.py:414
  (10 shorter events, 0.1 us)
Async XLA Ops:
  0.6 39.2 %copy-start = (bf16[1024,256]{1,0:T(8,128)(2,1)S(1)}, bf16[1024,256]{1,0:T(8,128)(2,1)}, u32[]{:S(2)}) copy-start(bf16[1024,256]{1,0:T(8,128)(2,1)} %refs_8_.1) | copy-start | bytes 1572868
  1.8 19.0 %collective-permute-start.10 = (bf16[512,256]{1,0:T(8,128)(2,1)S(1)}, bf16[512,256]{1,0:T(8,128)(2,1)S(1)}, u32[]{:S(2)}, u32[]{:S(2)}) collective-permute-start(bf16[512,256]{1,0:T(8,128)(2,1)S(1)} %get-tuple-element.7), channel_id=1, source_target_pairs={{0,2},{1,9},{2,0},{3,11},{4,6},{5,13},{6,4},{7,15},{8,10},{9,1},{1... | collective-permute-start | bytes 786440 | tf_op jit(solution)/shard_map/ppermute | solution.py:72
  5.9 6.8 %collective-permute-start.2 = (bf16[256,128]{1,0:T(8,128)(2,1)S(1)}, bf16[256,128]{1,0:T(8,128)(2,1)S(1)}, u32[]{:S(2)}, u32[]{:S(2)}) collective-permute-start(bf16[256,128]{1,0:T(8,128)(2,1)S(1)} %widen.1), channel_id=1, source_target_pairs={{0,24},{2,26},{4,28},{6,30},{8,16},{10,18},{12,20},{14,22},{16,8},... | collective-permute-start | bytes 196616 | tf_op jit(solution)/shard_map/ppermute | solution.py:352
  9.5 9.3 %collective-permute-start.1 = (bf16[256,128]{1,0:T(8,128)(2,1)S(1)}, bf16[256,128]{1,0:T(8,128)(2,1)S(1)}, u32[]{:S(2)}, u32[]{:S(2)}) collective-permute-start(bf16[256,128]{1,0:T(8,128)(2,1)S(1)} %widen.1), channel_id=1, source_target_pairs={{0,16},{2,18},{4,20},{6,22},{8,24},{10,26},{12,28},{14,30},{16,0},... | collective-permute-start | bytes 196616 | tf_op jit(solution)/shard_map/ppermute | solution.py:352
  9.5 9.3 %collective-permute-start = (bf16[256,128]{1,0:T(8,128)(2,1)S(1)}, bf16[256,128]{1,0:T(8,128)(2,1)S(1)}, u32[]{:S(2)}, u32[]{:S(2)}) collective-permute-start(bf16[256,128]{1,0:T(8,128)(2,1)S(1)} %widen.1), channel_id=1, source_target_pairs={{0,8},{2,10},{4,12},{6,14},{8,0},{10,2},{12,4},{14,6},{16,24},{18,... | collective-permute-start | bytes 196616 | tf_op jit(solution)/shard_map/ppermute | solution.py:352
  10.3 12.2 %collective-permute-start.11 = (bf16[512,256]{1,0:T(8,128)(2,1)S(1)}, bf16[512,256]{1,0:T(8,128)(2,1)S(1)}, u32[]{:S(2)}, u32[]{:S(2)}) collective-permute-start(bf16[512,256]{1,0:T(8,128)(2,1)S(1)} %get-tuple-element.6), channel_id=1, source_target_pairs={{0,4},{1,17},{2,6},{3,19},{4,0},{5,21},{6,2},{7,23},{8,12},{9,25},... | collective-permute-start | bytes 786440 | tf_op jit(solution)/shard_map/ppermute | solution.py:72
  18.8 5.3 %collective-permute-start.6 = (bf16[1024,128]{1,0:T(8,128)(2,1)S(1)}, bf16[1024,128]{1,0:T(8,128)(2,1)S(1)}, u32[]{:S(2)}, u32[]{:S(2)}) collective-permute-start(bf16[1024,128]{1,0:T(8,128)(2,1)S(1)} %pad_maximum_fusion.2.refs_0_), channel_id=1, source_target_pairs={{0,1},{1,0},{2,3},{3,2},{4,5},{5,4},{6,7},{7,6},{8,9},{9,8},{10,11... | collective-permute-start | bytes 786440 | tf_op jit(solution)/shard_map/ppermute | solution.py:357
  18.9 10.2 %collective-permute-start.5 = (bf16[1024,128]{1,0:T(8,128)(2,1)S(1)}, bf16[1024,128]{1,0:T(8,128)(2,1)S(1)}, u32[]{:S(2)}, u32[]{:S(2)}) collective-permute-start(bf16[1024,128]{1,0:T(8,128)(2,1)S(1)} %pad_maximum_fusion.2.refs_0_), channel_id=1, source_target_pairs={{0,6},{2,4},{4,2},{6,0},{8,14},{10,12},{12,10},{14,8},{16,22},{18,... | collective-permute-start | bytes 786440 | tf_op jit(solution)/shard_map/ppermute | solution.py:356
  20.3 13.8 %collective-permute-start.4 = (bf16[1024,128]{1,0:T(8,128)(2,1)S(1)}, bf16[1024,128]{1,0:T(8,128)(2,1)S(1)}, u32[]{:S(2)}, u32[]{:S(2)}) collective-permute-start(bf16[1024,128]{1,0:T(8,128)(2,1)S(1)} %pad_maximum_fusion.2.refs_0_), channel_id=1, source_target_pairs={{0,4},{2,6},{4,0},{6,2},{8,12},{10,14},{12,8},{14,10},{16,20},{18,... | collective-permute-start | bytes 786440 | tf_op jit(solution)/shard_map/ppermute | solution.py:356
  20.8 13.4 %collective-permute-start.3 = (bf16[1024,128]{1,0:T(8,128)(2,1)S(1)}, bf16[1024,128]{1,0:T(8,128)(2,1)S(1)}, u32[]{:S(2)}, u32[]{:S(2)}) collective-permute-start(bf16[1024,128]{1,0:T(8,128)(2,1)S(1)} %pad_maximum_fusion.2.refs_0_), channel_id=1, source_target_pairs={{0,2},{2,0},{4,6},{6,4},{8,10},{10,8},{12,14},{14,12},{16,18},{18,... | collective-permute-start | bytes 786440 | tf_op jit(solution)/shard_map/ppermute | solution.py:356
  22.5 17.2 %collective-permute-start.12 = (bf16[1024,256]{1,0:T(8,128)(2,1)S(1)}, bf16[1024,256]{1,0:T(8,128)(2,1)S(1)}, u32[]{:S(2)}, u32[]{:S(2)}) collective-permute-start(bf16[1024,256]{1,0:T(8,128)(2,1)S(1)} %pad_maximum_fusion), channel_id=1, source_target_pairs={{0,4},{1,17},{2,6},{3,19},{4,0},{5,21},{6,2},{7,23},{8,12},{9,25},... | collective-permute-start | bytes 1572872 | tf_op jit(solution)/shard_map/ppermute | solution.py:72
  24.1 15.7 %collective-permute-start.13 = (bf16[1024,256]{1,0:T(8,128)(2,1)S(1)}, bf16[1024,256]{1,0:T(8,128)(2,1)S(1)}, u32[]{:S(2)}, u32[]{:S(2)}) collective-permute-start(bf16[1024,256]{1,0:T(8,128)(2,1)S(1)} %pad_maximum_fusion.1), channel_id=1, source_target_pairs={{0,2},{1,9},{2,0},{3,11},{4,6},{5,13},{6,4},{7,15},{8,10},{9,1},{1... | collective-permute-start | bytes 1572872 | tf_op jit(solution)/shard_map/ppermute | solution.py:72
  29.1 5.6 %collective-permute-start.9 = (bf16[1024,128]{1,0:T(8,128)(2,1)S(1)}, bf16[1024,128]{1,0:T(8,128)(2,1)S(1)}, u32[]{:S(2)}, u32[]{:S(2)}) collective-permute-start(bf16[1024,128]{1,0:T(8,128)(2,1)S(1)} %collective-permute-done.5.refs_3_), channel_id=1, source_target_pairs={{0,1},{1,0},{2,3},{3,2},{4,5},{5,4},{6,7},{7,6},{8,9},{9,8},{10,11... | collective-permute-start | bytes 786440 | tf_op jit(solution)/shard_map/ppermute | solution.py:357
  34.1 1.5 %collective-permute-start.8 = (bf16[1024,128]{1,0:T(8,128)(2,1)S(1)}, bf16[1024,128]{1,0:T(8,128)(2,1)S(1)}, u32[]{:S(2)}, u32[]{:S(2)}) collective-permute-start(bf16[1024,128]{1,0:T(8,128)(2,1)S(1)} %collective-permute-done.4.refs_2_), channel_id=1, source_target_pairs={{0,1},{1,0},{2,3},{3,2},{4,5},{5,4},{6,7},{7,6},{8,9},{9,8},{10,11... | collective-permute-start | bytes 786440 | tf_op jit(solution)/shard_map/ppermute | solution.py:357
  34.2 1.8 %collective-permute-start.7 = (bf16[1024,128]{1,0:T(8,128)(2,1)S(1)}, bf16[1024,128]{1,0:T(8,128)(2,1)S(1)}, u32[]{:S(2)}, u32[]{:S(2)}) collective-permute-start(bf16[1024,128]{1,0:T(8,128)(2,1)S(1)} %collective-permute-done.3.refs_1_), channel_id=1, source_target_pairs={{0,1},{1,0},{2,3},{3,2},{4,5},{5,4},{6,7},{7,6},{8,9},{9,8},{10,11... | collective-permute-start | bytes 786440 | tf_op jit(solution)/shard_map/ppermute | solution.py:357
  49.2 11.2 %collective-permute-start.14 = (f32[512,256]{1,0:T(8,128)S(1)}, f32[512,256]{1,0:T(8,128)S(1)}, u32[]{:S(2)}, u32[]{:S(2)}) collective-permute-start(f32[512,256]{1,0:T(8,128)S(1)} %sketch3.1), channel_id=1, source_target_pairs={{0,24},{1,7},{2,26},{3,5},{4,28},{5,3},{6,30},{7,1},{8,16},{9,15},... | collective-permute-start | bytes 1572872 | tf_op jit(solution)/shard_map/ppermute | solution.py:392
  51.4 22.7 %collective-permute-start.15 = (f32[512,256]{1,0:T(8,128)S(1)}, f32[512,256]{1,0:T(8,128)S(1)}, u32[]{:S(2)}, u32[]{:S(2)}) collective-permute-start(f32[512,256]{1,0:T(8,128)S(1)} %sketch2.1), channel_id=1, source_target_pairs={{0,16},{1,5},{2,18},{3,7},{4,20},{5,1},{6,22},{7,3},{8,24},{9,13},... | collective-permute-start | bytes 1572872 | tf_op jit(solution)/shard_map/ppermute | solution.py:392
  51.4 22.7 %collective-permute-start.16 = (f32[512,256]{1,0:T(8,128)S(1)}, f32[512,256]{1,0:T(8,128)S(1)}, u32[]{:S(2)}, u32[]{:S(2)}) collective-permute-start(f32[512,256]{1,0:T(8,128)S(1)} %sketch1.1), channel_id=1, source_target_pairs={{0,8},{1,3},{2,10},{3,1},{4,12},{5,7},{6,14},{7,5},{8,0},{9,11},{1... | collective-permute-start | bytes 1572872 | tf_op jit(solution)/shard_map/ppermute | solution.py:392
  74.2 2.0 %collective-permute-start.17 = (f32[512,256]{1,0:T(8,128)S(1)}, f32[512,256]{1,0:T(8,128)S(1)}, u32[]{:S(2)}, u32[]{:S(2)}) collective-permute-start(f32[512,256]{1,0:T(8,128)S(1)} %add_add_fusion.own_ref.sown_hbm), channel_id=1, source_target_pairs={{0,1},{1,0},{2,3},{3,2},{4,5},{5,4},{6,7},{7,6},{8,9},{9,8},{10,11... | collective-permute-start | bytes 1572872 | tf_op jit(solution)/shard_map/ppermute | solution.py:396
  106.5 1.6 %collective-permute-start.18 = (f32[128,640]{1,0:T(8,128)S(1)}, f32[128,640]{1,0:T(8,128)S(1)}, u32[]{:S(2)}, u32[]{:S(2)}) collective-permute-start(f32[128,640]{1,0:T(8,128)S(1)} %bitcast.2), channel_id=1, source_target_pairs={{0,1},{1,0},{2,3},{3,2},{4,5},{5,4},{6,7},{7,6},{8,9},{9,8},{10,11... | collective-permute-start | bytes 983048 | tf_op jit(solution)/shard_map/ppermute | solution.py:411

commit v5 on v4

--- a/solution.py
+++ b/solution.py
@@ -75,18 +75,35 @@
         arrays = [block] + [sent(block, s) for s in range(1, plan.na)]
         return arrays, [[(s, 0, depth)] for s in range(plan.na)]
     cut = depth // 2
-    top, bottom = block[:cut], block[cut:]
-    top_one, bottom_two = sent(top, 1), sent(bottom, 2)
-    top_pair = sent(jnp.concatenate([top, top_one], 0), 2)
-    bottom_pair = sent(jnp.concatenate([bottom, bottom_two], 0), 1)
-    arrays = [block, top_one, bottom_two, top_pair, bottom_pair]
-    where = [
+    one, two = sent(block, 1), sent(block, 2)
+    top, bottom = sent(one[:cut], 2), sent(two[cut:], 1)
+    return [block, one, two, top, bottom], [
         [(0, 0, depth)],
-        [(1, 0, cut), (4, 0, cut)],
-        [(3, 0, cut), (2, 0, cut)],
-        [(3, cut, cut), (4, cut, cut)],
+        [(1, 0, depth)],
+        [(2, 0, depth)],
+        [(3, 0, cut), (4, 0, cut)],
     ]
-    return arrays, where
+
+
+def scatter_sums(plan, part):
+    def sent(value, db):
+        return lax.ppermute(value, BOTH, plan.pairs(0, db))
+
+    if plan.nb != 4:
+        arrived = [sent(part(s), s) for s in range(1, plan.nb)]
+        own = part(0)
+    else:
+        third = part(3)
+        cut = third.shape[0] // 2
+        top, bottom = sent(third[:cut], 1), sent(third[cut:], 2)
+        two, one = part(2), part(1)
+        two = jnp.concatenate([two[:cut] + top, two[cut:]], 0)
+        one = jnp.concatenate([one[:cut], one[cut:] + bottom], 0)
+        arrived = [sent(two, 2), sent(one, 1)]
+        own = part(0)
+    for piece in arrived:
+        own = own + piece
+    return own
 
 
 def widen_kernel(series, out, flat):
@@ -99,10 +116,9 @@
     out[...] = jnp.concatenate([now[:count], now[LAG_SPACING : LAG_SPACING + count]], 1)
 
 
-def place_kernel(plan, moves, *refs):
-    stacks = refs[: 2 * plan.lo]
-    blocks = refs[2 * plan.lo : -4]
-    wide, matrix, record_sem, block_sem = refs[-4:]
+def place_kernel(plan, *refs):
+    stacks = refs[:-2]
+    wide, record_sem = refs[-2:]
     i = lax.axis_index("tm")
     panel = lax.axis_index("panel")
     hi, lo = i // plan.lo, i % plan.lo
@@ -120,13 +136,6 @@
             record_sem.at[(side * plan.lo + slo) * plan.hi + shi],
         )
 
-    copies = []
-    for at, (array, row, size, target) in enumerate(moves):
-        copies.append(
-            pltpu.make_async_copy(
-                blocks[array].at[row : row + size, :], matrix.at[target : target + size, :], block_sem.at[at]
-            )
-        )
     for side in range(2):
         for slo in range(plan.lo):
 
@@ -134,8 +143,6 @@
             def _(shi):
                 record_copy(side, slo, shi).start()
 
-    for copy in copies:
-        copy.start()
     wide[total:, :] = jnp.zeros((wide.shape[0] - total, wide.shape[1]), wide.dtype)
     for side in range(2):
         for slo in range(plan.lo):
@@ -152,17 +159,14 @@
         right = jnp.concatenate([before[:LAG_SPACING, variables:], after[:LAG_SPACING, :variables]], 0)
         wide[pl.ds(edge - 16, 16), :] = jnp.concatenate([before[:, :variables], right], 1)
 
-    for copy in copies:
-        copy.wait()
-
-
-def sketch_kernel(plan, rows, depth, variables, sb, wide, matrix, out):
+
+def sketch_kernel(plan, rows, depth, variables, where, sb, wide, *refs):
+    blocks, out = refs[:-1], refs[-1]
     i = lax.axis_index("tm")
     panel = lax.axis_index("panel")
     a, b = plan.coords(i, panel)
     shift = depth // variables * LAG_SPACING
     slab = plan.index(a, b ^ sb, panel)
-    chunk = min(256, depth)
 
     @pl.loop(0, rows // TILE)
     def _(k):
@@ -171,14 +175,18 @@
         for sa in range(plan.na):
             block = plan.index(a ^ sa, b, panel)
             base = pl.multiple_of(slab * rows + block * shift + start, 16)
-            for first in range(0, depth, chunk):
-                pieces = []
-                for col in range(first, first + chunk, 2 * variables):
-                    offset = col // variables * LAG_SPACING
-                    pieces.append(wide[pl.ds(base + offset, TILE), :])
-                left = jnp.concatenate(pieces, 1) if len(pieces) > 1 else pieces[0]
-                right = matrix[sa * depth + first : sa * depth + first + chunk, :]
-                acc = acc + jnp.dot(left, right, preferred_element_type=jnp.float32)
+            past = 0
+            for array, row, count in where[sa]:
+                chunk = min(256, count)
+                for first in range(0, count, chunk):
+                    pieces = []
+                    for col in range(past + first, past + first + chunk, 2 * variables):
+                        offset = col // variables * LAG_SPACING
+                        pieces.append(wide[pl.ds(base + offset, TILE), :])
+                    left = jnp.concatenate(pieces, 1) if len(pieces) > 1 else pieces[0]
+                    right = blocks[array][row + first : row + first + chunk, :]
+                    acc = acc + jnp.dot(left, right, preferred_element_type=jnp.float32)
+                past += count
         out[pl.ds(start, TILE), :] = acc
 
 
@@ -354,45 +362,36 @@
     stacks = [stack]
     for s in range(1, plan.lo):
         stacks.append(lax.ppermute(stack, "tm", plan.plain_pairs(0, s)))
+    if plan.na == 4:
+        stacks = lax.optimization_barrier((stacks, arrays[1], arrays[2]))[0]
     stacks = stacks + [lax.ppermute(value, "panel", SWAP) for value in stacks]
     length = n * rows + WINDOW_LAGS * LAG_SPACING
-    moves = []
-    for s, parts in enumerate(where):
-        target = s * depth
-        for array, row, size in parts:
-            moves.append((array, row, size, target))
-            target += size
-    wide, matrix = pl.pallas_call(
-        functools.partial(place_kernel, plan, moves),
-        out_shape=[
-            pltpu.VMEM((length, 2 * variables), jnp.bfloat16),
-            pltpu.VMEM((plan.na * depth, half), jnp.bfloat16),
-        ],
-        in_specs=anywhere(len(stacks) + len(arrays)),
-        out_specs=vmem(2),
-        scratch_shapes=[pltpu.SemaphoreType.DMA((2 * n,)), pltpu.SemaphoreType.DMA((len(moves),))],
+    wide = pl.pallas_call(
+        functools.partial(place_kernel, plan),
+        out_shape=pltpu.VMEM((length, 2 * variables), jnp.bfloat16),
+        in_specs=anywhere(len(stacks)),
+        out_specs=vmem(1)[0],
+        scratch_shapes=[pltpu.SemaphoreType.DMA((2 * n,))],
         name="place",
         compiler_params=scoped(8),
-    )(*stacks, *arrays)
-    wide, matrix = in_vmem(wide), in_vmem(matrix)
+    )(*stacks)
+    wide = in_vmem(wide)
+    arrays = [in_vmem(value) for value in arrays]
 
     def part(sb):
         return pl.pallas_call(
-            functools.partial(sketch_kernel, plan, rows, depth, variables, sb),
+            functools.partial(sketch_kernel, plan, rows, depth, variables, where, sb),
             out_shape=jax.ShapeDtypeStruct((rows, half), jnp.float32),
-            in_specs=vmem(2),
+            in_specs=vmem(1 + len(arrays)),
             out_specs=vmem(1)[0],
             name="sketch%d" % sb,
             compiler_params=scoped(8),
             cost_estimate=pl.CostEstimate(
                 flops=2 * rows * plan.na * depth * half, bytes_accessed=4 * rows * half, transcendentals=0
             ),
-        )(wide, matrix)
-
-    arrived = [lax.ppermute(part(s), BOTH, plan.pairs(0, s)) for s in reversed(range(1, plan.nb))]
-    own = part(0)
-    for piece in arrived:
-        own = own + piece
+        )(wide, *arrays)
+
+    own = scatter_sums(plan, part)
     other = lax.ppermute(own, "panel", SWAP)
     assert half == 2 * NB
     width = 5 * NB

time: 132 us -> 132 us (level)
  blocking collectives: 28.9 us -> 30.6 us
    ppermute x3, waiting for transfers between devices: 6.95 us -> 11.7 us  [per_device(): pieces.append(lax.ppermute(own_rows, 'tm', plan.plain_pairs(s, 0)))]
    ppermute x4, waiting for transfers between devices: 3.81 us -> 0.12 us  [sent(): return lax.ppermute(value, BOTH, plan.pairs(da, 0))]
    ppermute x3 -> x4, waiting for transfers between devices: 18.9 us -> 16.2 us  [sent(): return lax.ppermute(value, BOTH, plan.pairs(0, db))]
    ppermute x3, waiting for transfers between devices: 9.56 us -> 12 us  [per_device(): stacks.append(lax.ppermute(stack, 'tm', plan.plain_pairs(0, s)))]
    all_to_all x1, blocking collectives: 14.8 us -> 16.4 us  [per_device(): lax.all_to_all(gram.reshape(n, NB // n, width), 'tm', 0, 0, tiled=True)]
    ppermute x3 -> x4, starting transfers between devices: 4.45 us -> 4.85 us  [sent(): return lax.ppermute(value, BOTH, plan.pairs(0, db))]
  transfers between devices with their start and end apart: 19 -> 20, of which waited for: 13 -> 12; matrix products, arithmetic and copies ran while one was open for 1% -> 1% of each run, Pallas kernels for 1% -> 7%
where the time goes in v5:
time: 132 us
  waiting for transfers between devices  43.7 us (33%)
  Pallas kernels  34.7 us (26%)
  blocking collectives  30.6 us (23%)
  starting transfers between devices  20.4 us (15%)
    pallas_call x1, Pallas kernels, per_device(): pl.pallas_call(functools.partial(factor_kernel, math.sqrt(n * rows)), out...  22.7 us
    all_to_all x1, blocking collectives, per_device(): lax.all_to_all(gram.reshape(n, NB // n, width), 'tm', 0, 0, tiled=True)  16.4 us
    ppermute x4, waiting for transfers between devices, sent(): return lax.ppermute(value, BOTH, plan.pairs(0, db))  16.2 us
    all_to_all x1, blocking collectives, per_device(): gram = lax.all_to_all(alike, 'tm', 0, 0, tiled=True).reshape(NB, width)  14.2 us
    ppermute x3, waiting for transfers between devices, per_device(): stacks.append(lax.ppermute(stack, 'tm', plan.plain_pairs(0, s)))  12 us
    ppermute x3, waiting for transfers between devices, per_device(): pieces.append(lax.ppermute(own_rows, 'tm', plan.plain_pairs(s, 0)))  11.7 us
    ppermute x4, starting transfers between devices, sent(): return lax.ppermute(value, BOTH, plan.pairs(da, 0))  6.39 us
    pallas_call x4, Pallas kernels, part(): pl.pallas_call(functools.partial(sketch_kernel, plan, rows, depth, variab...  5.82 us
  transfers between devices with their start and end apart: 20, of which 12 were waited for; matrix products, arithmetic and copies ran while one was open for 1% of the time, Pallas kernels for 7%

profile of v5, /device:TPU:0, one launch (start us, length us, event | category | flops | bytes accessed | tf_op | source)
XLA Modules:
  0.0 131.7 jit_solution(2418123620222369333)
XLA Ops:
  0.6 3.0 %collective-permute-start.6 = (bf16[1024,256]{1,0:T(8,128)(2,1)}, bf16[1024,256]{1,0:T(8,128)(2,1)S(1)}, u32[]{:S(2)}, u32[]{:S(2)}) collective-permute-start(bf16[1024,256]{1,0:T(8,128)(2,1)} %refs_0_.7), channel_id=1, source_target_pairs={{0,2},{1,9},{2,0},{3,11},{4,6},{5,13},{6,4},{7,15},{8,10},{9,1},{1... | collective-permute-start | bytes 1572872 | tf_op jit(solution)/shard_map/ppermute | solution.py:72
  3.7 1.5 %collective-permute-start.7 = (bf16[1024,256]{1,0:T(8,128)(2,1)}, bf16[1024,256]{1,0:T(8,128)(2,1)S(1)}, u32[]{:S(2)}, u32[]{:S(2)}) collective-permute-start(bf16[1024,256]{1,0:T(8,128)(2,1)} %refs_0_.7), channel_id=1, source_target_pairs={{0,4},{1,17},{2,6},{3,19},{4,0},{5,21},{6,2},{7,23},{8,12},{9,25},... | collective-permute-start | bytes 1572872 | tf_op jit(solution)/shard_map/ppermute | solution.py:72
  5.2 1.0 copy.4.series
  6.1 0.1 widen.1
  6.3 3.7 %collective-permute-start.2 = (bf16[256,128]{1,0:T(8,128)(2,1)S(1)}, bf16[256,128]{1,0:T(8,128)(2,1)S(1)}, u32[]{:S(2)}, u32[]{:S(2)}) collective-permute-start(bf16[256,128]{1,0:T(8,128)(2,1)S(1)} %widen.1), channel_id=1, source_target_pairs={{0,24},{2,26},{4,28},{6,30},{8,16},{10,18},{12,20},{14,22},{16,8},... | collective-permute-start | bytes 196616 | tf_op jit(solution)/shard_map/ppermute | solution.py:360
  9.9 0.0 collective-permute-start.1
  9.9 0.8 collective-permute-start
  10.7 2.4 %collective-permute-done.2 = bf16[256,128]{1,0:T(8,128)(2,1)S(1)} collective-permute-done((bf16[256,128]{1,0:T(8,128)(2,1)S(1)}, bf16[256,128]{1,0:T(8,128)(2,1)S(1)}, u32[]{:S(2)}, u32[]{:S(2)}) %collective-permute-start.2) | collective-permute-done | bytes 65568 | tf_op jit(solution)/shard_map/ppermute | solution.py:360
  13.1 9.3 %collective-permute-done.1 = bf16[256,128]{1,0:T(8,128)(2,1)S(1)} collective-permute-done((bf16[256,128]{1,0:T(8,128)(2,1)S(1)}, bf16[256,128]{1,0:T(8,128)(2,1)S(1)}, u32[]{:S(2)}, u32[]{:S(2)}) %collective-permute-start.1) | collective-permute-done | bytes 65568 | tf_op jit(solution)/shard_map/ppermute | solution.py:360
  22.4 1.2 collective-permute-start.3
  23.6 0.1 collective-permute-start.4
  23.7 2.3 %collective-permute-start.5 = (bf16[1024,128]{1,0:T(8,128)(2,1)S(1)}, bf16[1024,128]{1,0:T(8,128)(2,1)S(1)}, u32[]{:S(2)}, u32[]{:S(2)}) collective-permute-start(bf16[1024,128]{1,0:T(8,128)(2,1)S(1)} %pad_maximum_fusion.2.refs_0_), channel_id=1, source_target_pairs={{0,6},{2,4},{4,2},{6,0},{8,14},{10,12},{12,10},{14,8},{16,22},{18,... | collective-permute-start | bytes 786440 | tf_op jit(solution)/shard_map/ppermute | solution.py:364
  26.0 5.3 %collective-permute-done.3.refs_1_ = bf16[1024,128]{1,0:T(8,128)(2,1)S(1)} collective-permute-done((bf16[1024,128]{1,0:T(8,128)(2,1)S(1)}, bf16[1024,128]{1,0:T(8,128)(2,1)S(1)}, u32[]{:S(2)}, u32[]{:S(2)}) %collective-permute-start.3) | collective-permute-done | bytes 262176 | tf_op jit(solution)/shard_map/ppermute | solution.py:364
  31.3 6.7 %collective-permute-done.4.refs_2_ = bf16[1024,128]{1,0:T(8,128)(2,1)S(1)} collective-permute-done((bf16[1024,128]{1,0:T(8,128)(2,1)S(1)}, bf16[1024,128]{1,0:T(8,128)(2,1)S(1)}, u32[]{:S(2)}, u32[]{:S(2)}) %collective-permute-start.4) | collective-permute-done | bytes 262176 | tf_op jit(solution)/shard_map/ppermute | solution.py:364
  38.0 0.3 collective-permute-start.8
  38.3 0.3 collective-permute-start.9
  38.6 0.3 collective-permute-start.10
  38.8 0.3 collective-permute-start.11
  39.1 0.0 copy-start
  39.1 0.3 collective-permute-start.12
  39.5 0.1 collective-permute-done.8.refs_4_
  39.6 1.5 %collective-permute-start.13 = (bf16[512,256]{1,0:T(8,128)(2,1)S(1)}, bf16[512,256]{1,0:T(8,128)(2,1)S(1)}, u32[]{:S(2)}, u32[]{:S(2)}) collective-permute-start(bf16[512,256]{1,0:T(8,128)(2,1)S(1)} %slice.33), channel_id=1, source_target_pairs={{0,2},{1,9},{2,0},{3,11},{4,6},{5,13},{6,4},{7,15},{8,10},{9,1},{1... | collective-permute-start | bytes 786440 | tf_op jit(solution)/shard_map/ppermute | solution.py:72
  41.1 0.0 collective-permute-done.9.refs_5_
  41.1 0.0 collective-permute-done.10.refs_6_
  41.1 4.7 %place.1.wide = bf16[10240,128]{1,0:T(8,128)(2,1)S(1)} custom-call(bf16[1024,128]{1,0:T(8,128)(2,1)S(1)} %pad_maximum_fusion.2.refs_0_, bf16[1024,128]{1,0:T(8,128)(2,1)S(1)} %collective-permute-done.3.refs_1_, bf16[1024,128]{1,0:T(8,128)(2,1)S(1)} %collective-permute-done.4.refs_2_, bf16[1024,128]{1,0:T(8,128)(2,1)S(1)} %collective-permute-done.5.refs_3_, ...), custom_call_target="tpu_custom_call" | custom-call | tf_op jit(solution)/shard_map/place/pallas_call | solution.py:369
  45.9 0.1 collective-permute-done.13.refs_4_
  46.0 1.4 %sketch3.1 = f32[512,256]{1,0:T(8,128)S(1)} custom-call(bf16[10240,128]{1,0:T(8,128)(2,1)S(1)} %place.1.wide, bf16[1024,256]{1,0:T(8,128)(2,1)S(1)} %copy-done, bf16[1024,256]{1,0:T(8,128)(2,1)S(1)} %collective-permute-done.6.refs_1_, bf16[1024,256]{1,0:T(8,128)(2,1)S(1)} %collective-permute-done.7.refs_2_, ...), custom_call_target="tpu_custom_call" | custom-call | flops 1073741824 | bytes 524288 | tf_op jit(solution)/shard_map/sketch3/pallas_call | solution.py:382
  47.5 0.1 collective-permute-start.16
  47.6 2.5 %collective-permute-start.14 = (f32[256,256]{1,0:T(8,128)S(1)}, f32[256,256]{1,0:T(8,128)S(1)}, u32[]{:S(2)}, u32[]{:S(2)}) collective-permute-start(f32[256,256]{1,0:T(8,128)S(1)} %get-tuple-element.12), channel_id=1, source_target_pairs={{0,8},{1,3},{2,10},{3,1},{4,12},{5,7},{6,14},{7,5},{8,0},{9,11},{1... | collective-permute-start | bytes 786440 | tf_op jit(solution)/shard_map/ppermute | solution.py:90
  50.1 1.4 %sketch1.1 = f32[512,256]{1,0:T(8,128)S(1)} custom-call(bf16[10240,128]{1,0:T(8,128)(2,1)S(1)} %place.1.wide, bf16[1024,256]{1,0:T(8,128)(2,1)S(1)} %copy-done, bf16[1024,256]{1,0:T(8,128)(2,1)S(1)} %collective-permute-done.6.refs_1_, bf16[1024,256]{1,0:T(8,128)(2,1)S(1)} %collective-permute-done.7.refs_2_, ...), custom_call_target="tpu_custom_call" | custom-call | flops 1073741824 | bytes 524288 | tf_op jit(solution)/shard_map/sketch1/pallas_call | solution.py:382
  51.5 1.5 %sketch2.1 = f32[512,256]{1,0:T(8,128)S(1)} custom-call(bf16[10240,128]{1,0:T(8,128)(2,1)S(1)} %place.1.wide, bf16[1024,256]{1,0:T(8,128)(2,1)S(1)} %copy-done, bf16[1024,256]{1,0:T(8,128)(2,1)S(1)} %collective-permute-done.6.refs_1_, bf16[1024,256]{1,0:T(8,128)(2,1)S(1)} %collective-permute-done.7.refs_2_, ...), custom_call_target="tpu_custom_call" | custom-call | flops 1073741824 | bytes 524288 | tf_op jit(solution)/shard_map/sketch2/pallas_call | solution.py:382
  53.0 3.8 %collective-permute-done.16 = f32[256,256]{1,0:T(8,128)S(1)} collective-permute-done((f32[256,256]{1,0:T(8,128)S(1)}, f32[256,256]{1,0:T(8,128)S(1)}, u32[]{:S(2)}, u32[]{:S(2)}) %collective-permute-start.16) | collective-permute-done | bytes 262176 | tf_op jit(solution)/shard_map/ppermute | solution.py:90
  56.8 0.1 fusion.1
  56.9 0.1 collective-permute-start.17
  57.0 0.3 collective-permute-done.14
  57.2 0.1 slice_add_fusion.1
  57.3 2.2 %collective-permute-start.15 = (f32[512,256]{1,0:T(8,128)S(1)}, f32[512,256]{1,0:T(8,128)S(1)}, u32[]{:S(2)}, u32[]{:S(2)}) collective-permute-start(f32[512,256]{1,0:T(8,128)S(1)} %pad_maximum_fusion), channel_id=1, source_target_pairs={{0,16},{1,5},{2,18},{3,7},{4,20},{5,1},{6,22},{7,3},{8,24},{9,13},... | collective-permute-start | bytes 1572872 | tf_op jit(solution)/shard_map/ppermute | solution.py:90
  59.5 1.4 %sketch0.1 = f32[512,256]{1,0:T(8,128)S(1)} custom-call(bf16[10240,128]{1,0:T(8,128)(2,1)S(1)} %place.1.wide, bf16[1024,256]{1,0:T(8,128)(2,1)S(1)} %copy-done, bf16[1024,256]{1,0:T(8,128)(2,1)S(1)} %collective-permute-done.6.refs_1_, bf16[1024,256]{1,0:T(8,128)(2,1)S(1)} %collective-permute-done.7.refs_2_, ...), custom_call_target="tpu_custom_call" | custom-call | flops 1073741824 | bytes 524288 | tf_op jit(solution)/shard_map/sketch0/pallas_call | solution.py:382
  61.0 9.3 %collective-permute-done.17 = f32[512,256]{1,0:T(8,128)S(1)} collective-permute-done((f32[512,256]{1,0:T(8,128)S(1)}, f32[512,256]{1,0:T(8,128)S(1)}, u32[]{:S(2)}, u32[]{:S(2)}) %collective-permute-start.17) | collective-permute-done | bytes 524320 | tf_op jit(solution)/shard_map/ppermute | solution.py:90
  70.3 2.9 %collective-permute-done.15 = f32[512,256]{1,0:T(8,128)S(1)} collective-permute-done((f32[512,256]{1,0:T(8,128)S(1)}, f32[512,256]{1,0:T(8,128)S(1)}, u32[]{:S(2)}, u32[]{:S(2)}) %collective-permute-start.15) | collective-permute-done | bytes 524320 | tf_op jit(solution)/shard_map/ppermute | solution.py:90
  73.1 0.1 add_add_fusion.own_ref.sown_hbm
  73.2 0.1 collective-permute-start.18
  73.3 1.9 %collective-permute-done.18.other_ref.sother_hbm = f32[512,256]{1,0:T(8,128)S(1)} collective-permute-done((f32[512,256]{1,0:T(8,128)S(1)}, f32[512,256]{1,0:T(8,128)S(1)}, u32[]{:S(2)}, u32[]{:S(2)}) %collective-permute-start.18) | collective-permute-done | bytes 524320 | tf_op jit(solution)/shard_map/ppermute | solution.py:395
  75.2 1.4 %gram.1 = f32[128,640]{1,0:T(8,128)S(1)} custom-call(f32[512,256]{1,0:T(8,128)S(1)} %add_add_fusion.own_ref.sown_hbm, f32[512,256]{1,0:T(8,128)S(1)} %collective-permute-done.18.other_ref.sother_hbm), custom_call_target="tpu_custom_call" | custom-call | tf_op jit(solution)/shard_map/gram/pallas_call | solution.py:398
  76.6 16.4 %all_to_all.10 = f32[16,8,640]{2,1,0:T(8,128)S(1)} all-to-all(f32[16,8,640]{2,1,0:T(8,128)S(1)} %bitcast.4), channel_id=1, replica_groups=mesh['grp'=1,'tm'=16,'panel'=2] {'tm'}, dimensions={0} | all-to-all | bytes 655360 | tf_op jit(solution)/shard_map/all_to_all | solution.py:406
  93.1 14.2 %all_to_all.11 = f32[16,8,640]{2,1,0:T(8,128)S(1)} all-to-all(f32[16,8,640]{2,1,0:T(8,128)S(1)} %broadcast_in_dim.2), channel_id=1, replica_groups=mesh['grp'=1,'tm'=16,'panel'=2] {'tm'}, dimensions={0} | all-to-all | bytes 655360 | tf_op jit(solution)/shard_map/all_to_all | solution.py:409
  107.2 1.6 %collective-permute-done.19.gother = f32[128,640]{1,0:T(8,128)S(1)} collective-permute-done((f32[128,640]{1,0:T(8,128)S(1)}, f32[128,640]{1,0:T(8,128)S(1)}, u32[]{:S(2)}, u32[]{:S(2)}) %collective-permute-start.19) | collective-permute-done | bytes 327712 | tf_op jit(solution)/shard_map/ppermute | solution.py:410
  108.9 22.7 %factor.1 = (f32[512,256]{1,0:T(8,128)}, f32[512,256]{1,0:T(8,128)}) custom-call(f32[128,640]{1,0:T(8,128)S(1)} %bitcast.3, f32[128,640]{1,0:T(8,128)S(1)} %collective-permute-done.19.gother, f32[512,256]{1,0:T(8,128)S(1)} %add_add_fusion.own_ref.sown_hbm, f32[512,256]{1,0:T(8,128)S(1)} %collective-permute-done.18.other_ref.sother_hbm), custom_call_target="tpu_custom_call" | custom-call | tf_op jit(solution)/shard_map/factor/pallas_call | solution.py:413
  (16 shorter events, 0.2 us)
Async XLA Ops:
  0.6 37.4 %collective-permute-start.6 = (bf16[1024,256]{1,0:T(8,128)(2,1)}, bf16[1024,256]{1,0:T(8,128)(2,1)S(1)}, u32[]{:S(2)}, u32[]{:S(2)}) collective-permute-start(bf16[1024,256]{1,0:T(8,128)(2,1)} %refs_0_.7), channel_id=1, source_target_pairs={{0,2},{1,9},{2,0},{3,11},{4,6},{5,13},{6,4},{7,15},{8,10},{9,1},{1... | collective-permute-start | bytes 1572872 | tf_op jit(solution)/shard_map/ppermute | solution.py:72
  3.7 34.3 %collective-permute-start.7 = (bf16[1024,256]{1,0:T(8,128)(2,1)}, bf16[1024,256]{1,0:T(8,128)(2,1)S(1)}, u32[]{:S(2)}, u32[]{:S(2)}) collective-permute-start(bf16[1024,256]{1,0:T(8,128)(2,1)} %refs_0_.7), channel_id=1, source_target_pairs={{0,4},{1,17},{2,6},{3,19},{4,0},{5,21},{6,2},{7,23},{8,12},{9,25},... | collective-permute-start | bytes 1572872 | tf_op jit(solution)/shard_map/ppermute | solution.py:72
  6.3 6.8 %collective-permute-start.2 = (bf16[256,128]{1,0:T(8,128)(2,1)S(1)}, bf16[256,128]{1,0:T(8,128)(2,1)S(1)}, u32[]{:S(2)}, u32[]{:S(2)}) collective-permute-start(bf16[256,128]{1,0:T(8,128)(2,1)S(1)} %widen.1), channel_id=1, source_target_pairs={{0,24},{2,26},{4,28},{6,30},{8,16},{10,18},{12,20},{14,22},{16,8},... | collective-permute-start | bytes 196616 | tf_op jit(solution)/shard_map/ppermute | solution.py:360
  9.9 12.4 %collective-permute-start.1 = (bf16[256,128]{1,0:T(8,128)(2,1)S(1)}, bf16[256,128]{1,0:T(8,128)(2,1)S(1)}, u32[]{:S(2)}, u32[]{:S(2)}) collective-permute-start(bf16[256,128]{1,0:T(8,128)(2,1)S(1)} %widen.1), channel_id=1, source_target_pairs={{0,16},{2,18},{4,20},{6,22},{8,24},{10,26},{12,28},{14,30},{16,0},... | collective-permute-start | bytes 196616 | tf_op jit(solution)/shard_map/ppermute | solution.py:360
  9.9 12.4 %collective-permute-start = (bf16[256,128]{1,0:T(8,128)(2,1)S(1)}, bf16[256,128]{1,0:T(8,128)(2,1)S(1)}, u32[]{:S(2)}, u32[]{:S(2)}) collective-permute-start(bf16[256,128]{1,0:T(8,128)(2,1)S(1)} %widen.1), channel_id=1, source_target_pairs={{0,8},{2,10},{4,12},{6,14},{8,0},{10,2},{12,4},{14,6},{16,24},{18,... | collective-permute-start | bytes 196616 | tf_op jit(solution)/shard_map/ppermute | solution.py:360
  22.4 8.9 %collective-permute-start.3 = (bf16[1024,128]{1,0:T(8,128)(2,1)S(1)}, bf16[1024,128]{1,0:T(8,128)(2,1)S(1)}, u32[]{:S(2)}, u32[]{:S(2)}) collective-permute-start(bf16[1024,128]{1,0:T(8,128)(2,1)S(1)} %pad_maximum_fusion.2.refs_0_), channel_id=1, source_target_pairs={{0,2},{2,0},{4,6},{6,4},{8,10},{10,8},{12,14},{14,12},{16,18},{18,... | collective-permute-start | bytes 786440 | tf_op jit(solution)/shard_map/ppermute | solution.py:364
  23.6 14.4 %collective-permute-start.4 = (bf16[1024,128]{1,0:T(8,128)(2,1)S(1)}, bf16[1024,128]{1,0:T(8,128)(2,1)S(1)}, u32[]{:S(2)}, u32[]{:S(2)}) collective-permute-start(bf16[1024,128]{1,0:T(8,128)(2,1)S(1)} %pad_maximum_fusion.2.refs_0_), channel_id=1, source_target_pairs={{0,4},{2,6},{4,0},{6,2},{8,12},{10,14},{12,8},{14,10},{16,20},{18,... | collective-permute-start | bytes 786440 | tf_op jit(solution)/shard_map/ppermute | solution.py:364
  23.7 14.3 %collective-permute-start.5 = (bf16[1024,128]{1,0:T(8,128)(2,1)S(1)}, bf16[1024,128]{1,0:T(8,128)(2,1)S(1)}, u32[]{:S(2)}, u32[]{:S(2)}) collective-permute-start(bf16[1024,128]{1,0:T(8,128)(2,1)S(1)} %pad_maximum_fusion.2.refs_0_), channel_id=1, source_target_pairs={{0,6},{2,4},{4,2},{6,0},{8,14},{10,12},{12,10},{14,8},{16,22},{18,... | collective-permute-start | bytes 786440 | tf_op jit(solution)/shard_map/ppermute | solution.py:364
  38.0 1.6 %collective-permute-start.8 = (bf16[1024,128]{1,0:T(8,128)(2,1)S(1)}, bf16[1024,128]{1,0:T(8,128)(2,1)S(1)}, u32[]{:S(2)}, u32[]{:S(2)}) collective-permute-start(bf16[1024,128]{1,0:T(8,128)(2,1)S(1)} %pad_maximum_fusion.2.refs_0_), channel_id=1, source_target_pairs={{0,1},{1,0},{2,3},{3,2},{4,5},{5,4},{6,7},{7,6},{8,9},{9,8},{10,11... | collective-permute-start | bytes 786440 | tf_op jit(solution)/shard_map/ppermute | solution.py:367
  38.3 2.8 %collective-permute-start.9 = (bf16[1024,128]{1,0:T(8,128)(2,1)S(1)}, bf16[1024,128]{1,0:T(8,128)(2,1)S(1)}, u32[]{:S(2)}, u32[]{:S(2)}) collective-permute-start(bf16[1024,128]{1,0:T(8,128)(2,1)S(1)} %collective-permute-done.3.refs_1_), channel_id=1, source_target_pairs={{0,1},{1,0},{2,3},{3,2},{4,5},{5,4},{6,7},{7,6},{8,9},{9,8},{10,11... | collective-permute-start | bytes 786440 | tf_op jit(solution)/shard_map/ppermute | solution.py:367
  38.6 2.5 %collective-permute-start.10 = (bf16[1024,128]{1,0:T(8,128)(2,1)S(1)}, bf16[1024,128]{1,0:T(8,128)(2,1)S(1)}, u32[]{:S(2)}, u32[]{:S(2)}) collective-permute-start(bf16[1024,128]{1,0:T(8,128)(2,1)S(1)} %collective-permute-done.4.refs_2_), channel_id=1, source_target_pairs={{0,1},{1,0},{2,3},{3,2},{4,5},{5,4},{6,7},{7,6},{8,9},{9,8},{10,11... | collective-permute-start | bytes 786440 | tf_op jit(solution)/shard_map/ppermute | solution.py:367
  38.8 2.3 %collective-permute-start.11 = (bf16[1024,128]{1,0:T(8,128)(2,1)S(1)}, bf16[1024,128]{1,0:T(8,128)(2,1)S(1)}, u32[]{:S(2)}, u32[]{:S(2)}) collective-permute-start(bf16[1024,128]{1,0:T(8,128)(2,1)S(1)} %collective-permute-done.5.refs_3_), channel_id=1, source_target_pairs={{0,1},{1,0},{2,3},{3,2},{4,5},{5,4},{6,7},{7,6},{8,9},{9,8},{10,11... | collective-permute-start | bytes 786440 | tf_op jit(solution)/shard_map/ppermute | solution.py:367
  39.1 6.9 %copy-start = (bf16[1024,256]{1,0:T(8,128)(2,1)S(1)}, bf16[1024,256]{1,0:T(8,128)(2,1)}, u32[]{:S(2)}) copy-start(bf16[1024,256]{1,0:T(8,128)(2,1)} %refs_0_.7) | copy-start | bytes 1572868
  39.1 6.7 %collective-permute-start.12 = (bf16[512,256]{1,0:T(8,128)(2,1)S(1)}, bf16[512,256]{1,0:T(8,128)(2,1)S(1)}, u32[]{:S(2)}, u32[]{:S(2)}) collective-permute-start(bf16[512,256]{1,0:T(8,128)(2,1)S(1)} %slice.32), channel_id=1, source_target_pairs={{0,4},{1,17},{2,6},{3,19},{4,0},{5,21},{6,2},{7,23},{8,12},{9,25},... | collective-permute-start | bytes 786440 | tf_op jit(solution)/shard_map/ppermute | solution.py:72
  39.6 6.4 %collective-permute-start.13 = (bf16[512,256]{1,0:T(8,128)(2,1)S(1)}, bf16[512,256]{1,0:T(8,128)(2,1)S(1)}, u32[]{:S(2)}, u32[]{:S(2)}) collective-permute-start(bf16[512,256]{1,0:T(8,128)(2,1)S(1)} %slice.33), channel_id=1, source_target_pairs={{0,2},{1,9},{2,0},{3,11},{4,6},{5,13},{6,4},{7,15},{8,10},{9,1},{1... | collective-permute-start | bytes 786440 | tf_op jit(solution)/shard_map/ppermute | solution.py:72
  47.5 9.3 %collective-permute-start.16 = (f32[256,256]{1,0:T(8,128)S(1)}, f32[256,256]{1,0:T(8,128)S(1)}, u32[]{:S(2)}, u32[]{:S(2)}) collective-permute-start(f32[256,256]{1,0:T(8,128)S(1)} %get-tuple-element.13), channel_id=1, source_target_pairs={{0,16},{1,5},{2,18},{3,7},{4,20},{5,1},{6,22},{7,3},{8,24},{9,13},... | collective-permute-start | bytes 786440 | tf_op jit(solution)/shard_map/ppermute | solution.py:90
  47.6 9.7 %collective-permute-start.14 = (f32[256,256]{1,0:T(8,128)S(1)}, f32[256,256]{1,0:T(8,128)S(1)}, u32[]{:S(2)}, u32[]{:S(2)}) collective-permute-start(f32[256,256]{1,0:T(8,128)S(1)} %get-tuple-element.12), channel_id=1, source_target_pairs={{0,8},{1,3},{2,10},{3,1},{4,12},{5,7},{6,14},{7,5},{8,0},{9,11},{1... | collective-permute-start | bytes 786440 | tf_op jit(solution)/shard_map/ppermute | solution.py:90
  56.9 13.4 %collective-permute-start.17 = (f32[512,256]{1,0:T(8,128)S(1)}, f32[512,256]{1,0:T(8,128)S(1)}, u32[]{:S(2)}, u32[]{:S(2)}) collective-permute-start(f32[512,256]{1,0:T(8,128)S(1)} %pad_maximum_fusion.1), channel_id=1, source_target_pairs={{0,8},{1,3},{2,10},{3,1},{4,12},{5,7},{6,14},{7,5},{8,0},{9,11},{1... | collective-permute-start | bytes 1572872 | tf_op jit(solution)/shard_map/ppermute | solution.py:90
  57.3 15.8 %collective-permute-start.15 = (f32[512,256]{1,0:T(8,128)S(1)}, f32[512,256]{1,0:T(8,128)S(1)}, u32[]{:S(2)}, u32[]{:S(2)}) collective-permute-start(f32[512,256]{1,0:T(8,128)S(1)} %pad_maximum_fusion), channel_id=1, source_target_pairs={{0,16},{1,5},{2,18},{3,7},{4,20},{5,1},{6,22},{7,3},{8,24},{9,13},... | collective-permute-start | bytes 1572872 | tf_op jit(solution)/shard_map/ppermute | solution.py:90
  73.2 2.0 %collective-permute-start.18 = (f32[512,256]{1,0:T(8,128)S(1)}, f32[512,256]{1,0:T(8,128)S(1)}, u32[]{:S(2)}, u32[]{:S(2)}) collective-permute-start(f32[512,256]{1,0:T(8,128)S(1)} %add_add_fusion.own_ref.sown_hbm), channel_id=1, source_target_pairs={{0,1},{1,0},{2,3},{3,2},{4,5},{5,4},{6,7},{7,6},{8,9},{9,8},{10,11... | collective-permute-start | bytes 1572872 | tf_op jit(solution)/shard_map/ppermute | solution.py:395
  107.2 1.6 %collective-permute-start.19 = (f32[128,640]{1,0:T(8,128)S(1)}, f32[128,640]{1,0:T(8,128)S(1)}, u32[]{:S(2)}, u32[]{:S(2)}) collective-permute-start(f32[128,640]{1,0:T(8,128)S(1)} %bitcast.2), channel_id=1, source_target_pairs={{0,1},{1,0},{2,3},{3,2},{4,5},{5,4},{6,7},{7,6},{8,9},{9,8},{10,11... | collective-permute-start | bytes 983048 | tf_op jit(solution)/shard_map/ppermute | solution.py:410

commit v6 on v5

--- a/solution.py
+++ b/solution.py
@@ -106,33 +106,30 @@
     return own
 
 
-def widen_kernel(series, out, flat):
-    rows, variables = series.shape
-    count = out.shape[0]
-    flat[:rows, :] = series[...]
-    flat[rows:, :] = jnp.zeros((flat.shape[0] - rows, variables), flat.dtype)
+def pack_kernel(series, out):
+    count = 2 * out.shape[0]
+    variables = series.shape[1]
     start = pl.multiple_of(lax.axis_index("panel") * count, count)
-    now = flat[pl.ds(start, count + 16), :]
-    out[...] = jnp.concatenate([now[:count], now[LAG_SPACING : LAG_SPACING + count]], 1)
+    now = series[pl.ds(start, count), :].astype(jnp.float32)
+    now = now.reshape(count // 16, 2, 8, variables)
+    out[...] = jnp.concatenate([now[:, 0], now[:, 1]], 2).reshape(count // 2, 2 * variables).astype(out.dtype)
 
 
 def place_kernel(plan, *refs):
-    stacks = refs[:-2]
-    wide, record_sem = refs[-2:]
+    stacks = refs[:-3]
+    wide, packed, record_sem = refs[-3:]
     i = lax.axis_index("tm")
     panel = lax.axis_index("panel")
     hi, lo = i // plan.lo, i % plan.lo
     count = stacks[0].shape[0] // plan.hi
-    rows = 2 * count
-    total = plan.n * rows
-    variables = wide.shape[1] // 2
+    total = plan.n * 2 * count
 
     def record_copy(side, slo, shi):
         slab = (hi ^ shi) * plan.lo + (lo ^ slo)
-        first = slab * rows + lax.rem(panel + side, 2) * count
+        first = (slab * 2 + lax.rem(panel + side, 2)) * count
         return pltpu.make_async_copy(
             stacks[side * plan.lo + slo].at[pl.ds(pl.multiple_of(shi * count, count), count), :],
-            wide.at[pl.ds(pl.multiple_of(first, count), count), :],
+            packed.at[pl.ds(pl.multiple_of(first, count), count), :],
             record_sem.at[(side * plan.lo + slo) * plan.hi + shi],
         )
 
@@ -143,7 +140,7 @@
             def _(shi):
                 record_copy(side, slo, shi).start()
 
-    wide[total:, :] = jnp.zeros((wide.shape[0] - total, wide.shape[1]), wide.dtype)
+    packed[total:, :] = jnp.zeros((packed.shape[0] - total, packed.shape[1]), packed.dtype)
     for side in range(2):
         for slo in range(plan.lo):
 
@@ -151,13 +148,20 @@
             def _(shi):
                 record_copy(side, slo, shi).wait()
 
-    @pl.loop(1, plan.n + 1)
+    step = 128
+    lanes = packed.shape[1]
+    left = lax.broadcasted_iota(jnp.int32, (step, lanes), 1) < lanes // 2
+
+    @pl.loop(0, wide.shape[0] // (2 * step))
     def _(k):
-        edge = pl.multiple_of(k * rows, rows)
-        after = wide[pl.ds(edge, 16), :]
-        before = wide[pl.ds(edge - 16, 16), :]
-        right = jnp.concatenate([before[:LAG_SPACING, variables:], after[:LAG_SPACING, :variables]], 0)
-        wide[pl.ds(edge - 16, 16), :] = jnp.concatenate([before[:, :variables], right], 1)
+        start = pl.multiple_of(k * step, step)
+        now = packed[pl.ds(start, step + 16), :].astype(jnp.float32)
+        turned = pltpu.roll(now, lanes // 2, 1)
+        late = jnp.where(left, turned[:step], turned[8 : step + 8])
+        both = jnp.stack([now[:step].reshape(step // 8, 8, lanes), late.reshape(step // 8, 8, lanes)], 1)
+        wide[pl.ds(pl.multiple_of(k * 2 * step, 2 * step), 2 * step), :] = both.reshape(2 * step, lanes).astype(
+            wide.dtype
+        )
 
 
 def sketch_kernel(plan, rows, depth, variables, where, sb, wide, *refs):
@@ -345,16 +349,16 @@
     plan = Plan(n)
     rows, variables = series.shape
     depth, half = test_matrix.shape
-    arrays, where = gather_blocks(plan, test_matrix)
     own_rows = pl.pallas_call(
-        widen_kernel,
-        out_shape=jax.ShapeDtypeStruct((rows // 2, 2 * variables), jnp.bfloat16),
+        pack_kernel,
+        out_shape=jax.ShapeDtypeStruct((rows // 4, 2 * variables), jnp.bfloat16),
         in_specs=vmem(1),
         out_specs=vmem(1)[0],
-        scratch_shapes=[pltpu.VMEM((rows + 16, variables), jnp.bfloat16)],
-        name="widen",
+        name="pack",
         compiler_params=scoped(8),
     )(series)
+    test_matrix, own_rows = lax.optimization_barrier((test_matrix, own_rows))
+    arrays, where = gather_blocks(plan, test_matrix)
     pieces = [own_rows]
     for s in range(1, plan.hi):
         pieces.append(lax.ppermute(own_rows, "tm", plan.plain_pairs(s, 0)))
@@ -371,9 +375,12 @@
         out_shape=pltpu.VMEM((length, 2 * variables), jnp.bfloat16),
         in_specs=anywhere(len(stacks)),
         out_specs=vmem(1)[0],
-        scratch_shapes=[pltpu.SemaphoreType.DMA((2 * n,))],
+        scratch_shapes=[
+            pltpu.VMEM((length // 2 + 16, 2 * variables), jnp.bfloat16),
+            pltpu.SemaphoreType.DMA((2 * n,)),
+        ],
         name="place",
-        compiler_params=scoped(8),
+        compiler_params=scoped(8 + (length * variables * 2 >> 20)),
     )(*stacks)
     wide = in_vmem(wide)
     arrays = [in_vmem(value) for value in arrays]

time: 132 us -> 121 us (0.917)
  waiting for transfers between devices: 43.7 us -> 33.8 us
  starting transfers between devices: 20.4 us -> 18.4 us
    ppermute x3, waiting for transfers between devices: 12 us -> 4.43 us  [per_device(): stacks.append(lax.ppermute(stack, 'tm', plan.plain_pairs(0, s)))]
    ppermute x3, waiting for transfers between devices: 11.7 us -> 7.07 us  [per_device(): pieces.append(lax.ppermute(own_rows, 'tm', plan.plain_pairs(s, 0)))]
    ppermute x4, starting transfers between devices: 4.85 us -> 3.13 us  [sent(): return lax.ppermute(value, BOTH, plan.pairs(0, db))]
    ppermute x3, starting transfers between devices: 4.45 us -> 5.78 us  [per_device(): pieces.append(lax.ppermute(own_rows, 'tm', plan.plain_pairs(s, 0)))]
  transfers between devices with their start and end apart: 20 -> 20, of which waited for: 12 -> 14; matrix products, arithmetic and copies ran while one was open for 1% -> 0% of each run, Pallas kernels for 7% -> 8%
where the time goes in v6:
time: 121 us; the launch traced here: 120 us
  Pallas kernels  35.4 us (29%)
  waiting for transfers between devices  33.8 us (28%)
  blocking collectives  30 us (25%)
  starting transfers between devices  18.4 us (15%)
    pallas_call x1, Pallas kernels, per_device(): pl.pallas_call(functools.partial(factor_kernel, math.sqrt(n * rows)), out...  22.7 us
    ppermute x4, waiting for transfers between devices, sent(): return lax.ppermute(value, BOTH, plan.pairs(0, db))  17.5 us
    all_to_all x1, blocking collectives, per_device(): lax.all_to_all(gram.reshape(n, NB // n, width), 'tm', 0, 0, tiled=True)  15.8 us
    all_to_all x1, blocking collectives, per_device(): gram = lax.all_to_all(alike, 'tm', 0, 0, tiled=True).reshape(NB, width)  14.2 us
    ppermute x3, waiting for transfers between devices, per_device(): pieces.append(lax.ppermute(own_rows, 'tm', plan.plain_pairs(s, 0)))  7.07 us
    pallas_call x4, Pallas kernels, part(): pl.pallas_call(functools.partial(sketch_kernel, plan, rows, depth, variab...  5.84 us
    ppermute x3, starting transfers between devices, per_device(): pieces.append(lax.ppermute(own_rows, 'tm', plan.plain_pairs(s, 0)))  5.78 us
    pallas_call x1, Pallas kernels, per_device(): pl.pallas_call(functools.partial(place_kernel, plan), out_shape=pltpu.VME...  5.38 us
  transfers between devices with their start and end apart: 20, of which 14 were waited for; matrix products, arithmetic and copies ran while one was open for 0% of the time, Pallas kernels for 8%

profile of v6, /device:TPU:0, one launch (start us, length us, event | category | flops | bytes accessed | tf_op | source)
XLA Modules:
  0.0 120.1 jit_solution(15009438722794095078)
XLA Ops:
  0.6 0.0 copy-start
  0.6 1.0 copy.4.series
  1.7 0.1 pack.1
  1.8 5.1 %collective-permute-start.2 = (bf16[128,128]{1,0:T(8,128)(2,1)S(1)}, bf16[128,128]{1,0:T(8,128)(2,1)S(1)}, u32[]{:S(2)}, u32[]{:S(2)}) collective-permute-start(bf16[128,128]{1,0:T(8,128)(2,1)S(1)} %pack.1), channel_id=1, source_target_pairs={{0,24},{2,26},{4,28},{6,30},{8,16},{10,18},{12,20},{14,22},{16,8},... | collective-permute-start | bytes 98312 | tf_op jit(solution)/shard_map/ppermute | solution.py:364
  6.9 0.0 collective-permute-start.1
  6.9 0.6 collective-permute-start
  7.5 1.7 %collective-permute-start.7 = (bf16[1024,256]{1,0:T(8,128)(2,1)}, bf16[1024,256]{1,0:T(8,128)(2,1)S(1)}, u32[]{:S(2)}, u32[]{:S(2)}) collective-permute-start(bf16[1024,256]{1,0:T(8,128)(2,1)} %refs_0_.3), channel_id=1, source_target_pairs={{0,4},{1,17},{2,6},{3,19},{4,0},{5,21},{6,2},{7,23},{8,12},{9,25},... | collective-permute-start | bytes 1572872 | tf_op jit(solution)/shard_map/ppermute | solution.py:72
  9.2 1.5 %collective-permute-start.6 = (bf16[1024,256]{1,0:T(8,128)(2,1)}, bf16[1024,256]{1,0:T(8,128)(2,1)S(1)}, u32[]{:S(2)}, u32[]{:S(2)}) collective-permute-start(bf16[1024,256]{1,0:T(8,128)(2,1)} %refs_0_.3), channel_id=1, source_target_pairs={{0,2},{1,9},{2,0},{3,11},{4,6},{5,13},{6,4},{7,15},{8,10},{9,1},{1... | collective-permute-start | bytes 1572872 | tf_op jit(solution)/shard_map/ppermute | solution.py:72
  10.7 1.0 collective-permute-done
  11.7 6.1 %collective-permute-done.1 = bf16[128,128]{1,0:T(8,128)(2,1)S(1)} collective-permute-done((bf16[128,128]{1,0:T(8,128)(2,1)S(1)}, bf16[128,128]{1,0:T(8,128)(2,1)S(1)}, u32[]{:S(2)}, u32[]{:S(2)}) %collective-permute-start.1) | collective-permute-done | bytes 32800 | tf_op jit(solution)/shard_map/ppermute | solution.py:364
  17.8 2.5 %collective-permute-start.5 = (bf16[512,128]{1,0:T(8,128)(2,1)S(1)}, bf16[512,128]{1,0:T(8,128)(2,1)S(1)}, u32[]{:S(2)}, u32[]{:S(2)}) collective-permute-start(bf16[512,128]{1,0:T(8,128)(2,1)S(1)} %constant_dynamic-update-slice_fusion.refs_0_), channel_id=1, source_target_pairs={{0,6},{2,4},{4,2},{6,0},{8,14},{10,12},{12,10},{14,8},{16,22},{18,... | collective-permute-start | bytes 393224 | tf_op jit(solution)/shard_map/ppermute | solution.py:368
  20.3 0.5 collective-permute-start.4
  20.8 0.5 collective-permute-start.3
  21.4 2.4 %collective-permute-done.5.refs_3_ = bf16[512,128]{1,0:T(8,128)(2,1)S(1)} collective-permute-done((bf16[512,128]{1,0:T(8,128)(2,1)S(1)}, bf16[512,128]{1,0:T(8,128)(2,1)S(1)}, u32[]{:S(2)}, u32[]{:S(2)}) %collective-permute-start.5) | collective-permute-done | bytes 131104 | tf_op jit(solution)/shard_map/ppermute | solution.py:368
  23.7 1.5 %collective-permute-done.4.refs_2_ = bf16[512,128]{1,0:T(8,128)(2,1)S(1)} collective-permute-done((bf16[512,128]{1,0:T(8,128)(2,1)S(1)}, bf16[512,128]{1,0:T(8,128)(2,1)S(1)}, u32[]{:S(2)}, u32[]{:S(2)}) %collective-permute-start.4) | collective-permute-done | bytes 131104 | tf_op jit(solution)/shard_map/ppermute | solution.py:368
  25.3 0.5 collective-permute-done.3.refs_1_
  25.8 0.0 collective-permute-done.6.refs_1_
  25.8 0.0 collective-permute-start.8
  25.8 1.0 collective-permute-start.13
  26.9 1.2 collective-permute-start.12
  28.1 0.5 collective-permute-start.10
  28.6 0.0 collective-permute-start.11
  28.6 0.8 collective-permute-done.9.refs_5_
  29.4 0.2 collective-permute-done.10.refs_6_
  29.6 0.3 collective-permute-done.11.refs_7_
  29.9 5.4 %place.1.wide = bf16[10240,128]{1,0:T(8,128)(2,1)S(1)} custom-call(bf16[512,128]{1,0:T(8,128)(2,1)S(1)} %constant_dynamic-update-slice_fusion.refs_0_, bf16[512,128]{1,0:T(8,128)(2,1)S(1)} %collective-permute-done.3.refs_1_, bf16[512,128]{1,0:T(8,128)(2,1)S(1)} %collective-permute-done.4.refs_2_, bf16[512,128]{1,0:T(8,128)(2,1)S(1)} %collective-permute-done.5.refs_3_, ...), custom_call_target="tpu_custom_call" | custom-call | tf_op jit(solution)/shard_map/place/pallas_call | solution.py:373
  35.3 1.5 %sketch3.1 = f32[512,256]{1,0:T(8,128)S(1)} custom-call(bf16[10240,128]{1,0:T(8,128)(2,1)S(1)} %place.1.wide, bf16[1024,256]{1,0:T(8,128)(2,1)S(1)} %copy-done, bf16[1024,256]{1,0:T(8,128)(2,1)S(1)} %collective-permute-done.6.refs_1_, bf16[1024,256]{1,0:T(8,128)(2,1)S(1)} %collective-permute-done.7.refs_2_, ...), custom_call_target="tpu_custom_call" | custom-call | flops 1073741824 | bytes 524288 | tf_op jit(solution)/shard_map/sketch3/pallas_call | solution.py:389
  36.9 0.2 collective-permute-start.14
  37.1 2.4 %collective-permute-start.16 = (f32[256,256]{1,0:T(8,128)S(1)}, f32[256,256]{1,0:T(8,128)S(1)}, u32[]{:S(2)}, u32[]{:S(2)}) collective-permute-start(f32[256,256]{1,0:T(8,128)S(1)} %get-tuple-element.17), channel_id=1, source_target_pairs={{0,16},{1,5},{2,18},{3,7},{4,20},{5,1},{6,22},{7,3},{8,24},{9,13},... | collective-permute-start | bytes 786440 | tf_op jit(solution)/shard_map/ppermute | solution.py:90
  39.4 1.4 %sketch1.1 = f32[512,256]{1,0:T(8,128)S(1)} custom-call(bf16[10240,128]{1,0:T(8,128)(2,1)S(1)} %place.1.wide, bf16[1024,256]{1,0:T(8,128)(2,1)S(1)} %copy-done, bf16[1024,256]{1,0:T(8,128)(2,1)S(1)} %collective-permute-done.6.refs_1_, bf16[1024,256]{1,0:T(8,128)(2,1)S(1)} %collective-permute-done.7.refs_2_, ...), custom_call_target="tpu_custom_call" | custom-call | flops 1073741824 | bytes 524288 | tf_op jit(solution)/shard_map/sketch1/pallas_call | solution.py:389
  40.9 1.5 %sketch2.1 = f32[512,256]{1,0:T(8,128)S(1)} custom-call(bf16[10240,128]{1,0:T(8,128)(2,1)S(1)} %place.1.wide, bf16[1024,256]{1,0:T(8,128)(2,1)S(1)} %copy-done, bf16[1024,256]{1,0:T(8,128)(2,1)S(1)} %collective-permute-done.6.refs_1_, bf16[1024,256]{1,0:T(8,128)(2,1)S(1)} %collective-permute-done.7.refs_2_, ...), custom_call_target="tpu_custom_call" | custom-call | flops 1073741824 | bytes 524288 | tf_op jit(solution)/shard_map/sketch2/pallas_call | solution.py:389
  42.4 3.0 %collective-permute-done.14 = f32[256,256]{1,0:T(8,128)S(1)} collective-permute-done((f32[256,256]{1,0:T(8,128)S(1)}, f32[256,256]{1,0:T(8,128)S(1)}, u32[]{:S(2)}, u32[]{:S(2)}) %collective-permute-start.14) | collective-permute-done | bytes 262176 | tf_op jit(solution)/shard_map/ppermute | solution.py:90
  45.3 0.1 slice_add_fusion.1
  45.4 0.1 collective-permute-start.15
  45.5 1.7 %collective-permute-done.16 = f32[256,256]{1,0:T(8,128)S(1)} collective-permute-done((f32[256,256]{1,0:T(8,128)S(1)}, f32[256,256]{1,0:T(8,128)S(1)}, u32[]{:S(2)}, u32[]{:S(2)}) %collective-permute-start.16) | collective-permute-done | bytes 262176 | tf_op jit(solution)/shard_map/ppermute | solution.py:90
  47.2 0.1 fusion.1
  47.3 0.5 collective-permute-start.17
  47.8 1.4 %sketch0.1 = f32[512,256]{1,0:T(8,128)S(1)} custom-call(bf16[10240,128]{1,0:T(8,128)(2,1)S(1)} %place.1.wide, bf16[1024,256]{1,0:T(8,128)(2,1)S(1)} %copy-done, bf16[1024,256]{1,0:T(8,128)(2,1)S(1)} %collective-permute-done.6.refs_1_, bf16[1024,256]{1,0:T(8,128)(2,1)S(1)} %collective-permute-done.7.refs_2_, ...), custom_call_target="tpu_custom_call" | custom-call | flops 1073741824 | bytes 524288 | tf_op jit(solution)/shard_map/sketch0/pallas_call | solution.py:389
  49.2 11.0 %collective-permute-done.15 = f32[512,256]{1,0:T(8,128)S(1)} collective-permute-done((f32[512,256]{1,0:T(8,128)S(1)}, f32[512,256]{1,0:T(8,128)S(1)}, u32[]{:S(2)}, u32[]{:S(2)}) %collective-permute-start.15) | collective-permute-done | bytes 524320 | tf_op jit(solution)/shard_map/ppermute | solution.py:90
  60.3 1.8 %collective-permute-done.17 = f32[512,256]{1,0:T(8,128)S(1)} collective-permute-done((f32[512,256]{1,0:T(8,128)S(1)}, f32[512,256]{1,0:T(8,128)S(1)}, u32[]{:S(2)}, u32[]{:S(2)}) %collective-permute-start.17) | collective-permute-done | bytes 524320 | tf_op jit(solution)/shard_map/ppermute | solution.py:90
  62.1 0.1 add_add_fusion.own_ref.sown_hbm
  62.2 0.1 collective-permute-start.18
  62.2 1.9 %collective-permute-done.18.other_ref.sother_hbm = f32[512,256]{1,0:T(8,128)S(1)} collective-permute-done((f32[512,256]{1,0:T(8,128)S(1)}, f32[512,256]{1,0:T(8,128)S(1)}, u32[]{:S(2)}, u32[]{:S(2)}) %collective-permute-start.18) | collective-permute-done | bytes 524320 | tf_op jit(solution)/shard_map/ppermute | solution.py:402
  64.1 1.4 %gram.1 = f32[128,640]{1,0:T(8,128)S(1)} custom-call(f32[512,256]{1,0:T(8,128)S(1)} %add_add_fusion.own_ref.sown_hbm, f32[512,256]{1,0:T(8,128)S(1)} %collective-permute-done.18.other_ref.sother_hbm), custom_call_target="tpu_custom_call" | custom-call | tf_op jit(solution)/shard_map/gram/pallas_call | solution.py:405
  65.5 15.8 %all_to_all.10 = f32[16,8,640]{2,1,0:T(8,128)S(1)} all-to-all(f32[16,8,640]{2,1,0:T(8,128)S(1)} %bitcast.4), channel_id=1, replica_groups=mesh['grp'=1,'tm'=16,'panel'=2] {'tm'}, dimensions={0} | all-to-all | bytes 655360 | tf_op jit(solution)/shard_map/all_to_all | solution.py:413
  81.4 14.2 %all_to_all.11 = f32[16,8,640]{2,1,0:T(8,128)S(1)} all-to-all(f32[16,8,640]{2,1,0:T(8,128)S(1)} %broadcast_in_dim.2), channel_id=1, replica_groups=mesh['grp'=1,'tm'=16,'panel'=2] {'tm'}, dimensions={0} | all-to-all | bytes 655360 | tf_op jit(solution)/shard_map/all_to_all | solution.py:416
  95.6 1.6 %collective-permute-done.19.gother = f32[128,640]{1,0:T(8,128)S(1)} collective-permute-done((f32[128,640]{1,0:T(8,128)S(1)}, f32[128,640]{1,0:T(8,128)S(1)}, u32[]{:S(2)}, u32[]{:S(2)}) %collective-permute-start.19) | collective-permute-done | bytes 327712 | tf_op jit(solution)/shard_map/ppermute | solution.py:417
  97.2 22.7 %factor.1 = (f32[512,256]{1,0:T(8,128)}, f32[512,256]{1,0:T(8,128)}) custom-call(f32[128,640]{1,0:T(8,128)S(1)} %bitcast.3, f32[128,640]{1,0:T(8,128)S(1)} %collective-permute-done.19.gother, f32[512,256]{1,0:T(8,128)S(1)} %add_add_fusion.own_ref.sown_hbm, f32[512,256]{1,0:T(8,128)S(1)} %collective-permute-done.18.other_ref.sother_hbm), custom_call_target="tpu_custom_call" | custom-call | tf_op jit(solution)/shard_map/factor/pallas_call | solution.py:420
  (19 shorter events, 0.2 us)
Async XLA Ops:
  0.6 34.7 %copy-start = (bf16[1024,256]{1,0:T(8,128)(2,1)S(1)}, bf16[1024,256]{1,0:T(8,128)(2,1)}, u32[]{:S(2)}) copy-start(bf16[1024,256]{1,0:T(8,128)(2,1)} %refs_0_.3) | copy-start | bytes 1572868
  1.8 16.0 %collective-permute-start.2 = (bf16[128,128]{1,0:T(8,128)(2,1)S(1)}, bf16[128,128]{1,0:T(8,128)(2,1)S(1)}, u32[]{:S(2)}, u32[]{:S(2)}) collective-permute-start(bf16[128,128]{1,0:T(8,128)(2,1)S(1)} %pack.1), channel_id=1, source_target_pairs={{0,24},{2,26},{4,28},{6,30},{8,16},{10,18},{12,20},{14,22},{16,8},... | collective-permute-start | bytes 98312 | tf_op jit(solution)/shard_map/ppermute | solution.py:364
  6.9 10.9 %collective-permute-start.1 = (bf16[128,128]{1,0:T(8,128)(2,1)S(1)}, bf16[128,128]{1,0:T(8,128)(2,1)S(1)}, u32[]{:S(2)}, u32[]{:S(2)}) collective-permute-start(bf16[128,128]{1,0:T(8,128)(2,1)S(1)} %pack.1), channel_id=1, source_target_pairs={{0,16},{2,18},{4,20},{6,22},{8,24},{10,26},{12,28},{14,30},{16,0},... | collective-permute-start | bytes 98312 | tf_op jit(solution)/shard_map/ppermute | solution.py:364
  6.9 4.8 %collective-permute-start = (bf16[128,128]{1,0:T(8,128)(2,1)S(1)}, bf16[128,128]{1,0:T(8,128)(2,1)S(1)}, u32[]{:S(2)}, u32[]{:S(2)}) collective-permute-start(bf16[128,128]{1,0:T(8,128)(2,1)S(1)} %pack.1), channel_id=1, source_target_pairs={{0,8},{2,10},{4,12},{6,14},{8,0},{10,2},{12,4},{14,6},{16,24},{18,... | collective-permute-start | bytes 98312 | tf_op jit(solution)/shard_map/ppermute | solution.py:364
  7.5 18.3 %collective-permute-start.7 = (bf16[1024,256]{1,0:T(8,128)(2,1)}, bf16[1024,256]{1,0:T(8,128)(2,1)S(1)}, u32[]{:S(2)}, u32[]{:S(2)}) collective-permute-start(bf16[1024,256]{1,0:T(8,128)(2,1)} %refs_0_.3), channel_id=1, source_target_pairs={{0,4},{1,17},{2,6},{3,19},{4,0},{5,21},{6,2},{7,23},{8,12},{9,25},... | collective-permute-start | bytes 1572872 | tf_op jit(solution)/shard_map/ppermute | solution.py:72
  9.2 16.6 %collective-permute-start.6 = (bf16[1024,256]{1,0:T(8,128)(2,1)}, bf16[1024,256]{1,0:T(8,128)(2,1)S(1)}, u32[]{:S(2)}, u32[]{:S(2)}) collective-permute-start(bf16[1024,256]{1,0:T(8,128)(2,1)} %refs_0_.3), channel_id=1, source_target_pairs={{0,2},{1,9},{2,0},{3,11},{4,6},{5,13},{6,4},{7,15},{8,10},{9,1},{1... | collective-permute-start | bytes 1572872 | tf_op jit(solution)/shard_map/ppermute | solution.py:72
  17.8 5.9 %collective-permute-start.5 = (bf16[512,128]{1,0:T(8,128)(2,1)S(1)}, bf16[512,128]{1,0:T(8,128)(2,1)S(1)}, u32[]{:S(2)}, u32[]{:S(2)}) collective-permute-start(bf16[512,128]{1,0:T(8,128)(2,1)S(1)} %constant_dynamic-update-slice_fusion.refs_0_), channel_id=1, source_target_pairs={{0,6},{2,4},{4,2},{6,0},{8,14},{10,12},{12,10},{14,8},{16,22},{18,... | collective-permute-start | bytes 393224 | tf_op jit(solution)/shard_map/ppermute | solution.py:368
  20.3 5.0 %collective-permute-start.4 = (bf16[512,128]{1,0:T(8,128)(2,1)S(1)}, bf16[512,128]{1,0:T(8,128)(2,1)S(1)}, u32[]{:S(2)}, u32[]{:S(2)}) collective-permute-start(bf16[512,128]{1,0:T(8,128)(2,1)S(1)} %constant_dynamic-update-slice_fusion.refs_0_), channel_id=1, source_target_pairs={{0,4},{2,6},{4,0},{6,2},{8,12},{10,14},{12,8},{14,10},{16,20},{18,... | collective-permute-start | bytes 393224 | tf_op jit(solution)/shard_map/ppermute | solution.py:368
  20.8 5.0 %collective-permute-start.3 = (bf16[512,128]{1,0:T(8,128)(2,1)S(1)}, bf16[512,128]{1,0:T(8,128)(2,1)S(1)}, u32[]{:S(2)}, u32[]{:S(2)}) collective-permute-start(bf16[512,128]{1,0:T(8,128)(2,1)S(1)} %constant_dynamic-update-slice_fusion.refs_0_), channel_id=1, source_target_pairs={{0,2},{2,0},{4,6},{6,4},{8,10},{10,8},{12,14},{14,12},{16,18},{18,... | collective-permute-start | bytes 393224 | tf_op jit(solution)/shard_map/ppermute | solution.py:368
  25.8 2.8 %collective-permute-start.8 = (bf16[512,128]{1,0:T(8,128)(2,1)S(1)}, bf16[512,128]{1,0:T(8,128)(2,1)S(1)}, u32[]{:S(2)}, u32[]{:S(2)}) collective-permute-start(bf16[512,128]{1,0:T(8,128)(2,1)S(1)} %constant_dynamic-update-slice_fusion.refs_0_), channel_id=1, source_target_pairs={{0,1},{1,0},{2,3},{3,2},{4,5},{5,4},{6,7},{7,6},{8,9},{9,8},{10,11... | collective-permute-start | bytes 393224 | tf_op jit(solution)/shard_map/ppermute | solution.py:371
  25.8 9.5 %collective-permute-start.13 = (bf16[512,256]{1,0:T(8,128)(2,1)S(1)}, bf16[512,256]{1,0:T(8,128)(2,1)S(1)}, u32[]{:S(2)}, u32[]{:S(2)}) collective-permute-start(bf16[512,256]{1,0:T(8,128)(2,1)S(1)} %slice.33), channel_id=1, source_target_pairs={{0,2},{1,9},{2,0},{3,11},{4,6},{5,13},{6,4},{7,15},{8,10},{9,1},{1... | collective-permute-start | bytes 786440 | tf_op jit(solution)/shard_map/ppermute | solution.py:72
  26.9 8.4 %collective-permute-start.12 = (bf16[512,256]{1,0:T(8,128)(2,1)S(1)}, bf16[512,256]{1,0:T(8,128)(2,1)S(1)}, u32[]{:S(2)}, u32[]{:S(2)}) collective-permute-start(bf16[512,256]{1,0:T(8,128)(2,1)S(1)} %slice.32), channel_id=1, source_target_pairs={{0,4},{1,17},{2,6},{3,19},{4,0},{5,21},{6,2},{7,23},{8,12},{9,25},... | collective-permute-start | bytes 786440 | tf_op jit(solution)/shard_map/ppermute | solution.py:72
  28.1 1.3 %collective-permute-start.9 = (bf16[512,128]{1,0:T(8,128)(2,1)S(1)}, bf16[512,128]{1,0:T(8,128)(2,1)S(1)}, u32[]{:S(2)}, u32[]{:S(2)}) collective-permute-start(bf16[512,128]{1,0:T(8,128)(2,1)S(1)} %collective-permute-done.3.refs_1_), channel_id=1, source_target_pairs={{0,1},{1,0},{2,3},{3,2},{4,5},{5,4},{6,7},{7,6},{8,9},{9,8},{10,11... | collective-permute-start | bytes 393224 | tf_op jit(solution)/shard_map/ppermute | solution.py:371
  28.1 1.5 %collective-permute-start.10 = (bf16[512,128]{1,0:T(8,128)(2,1)S(1)}, bf16[512,128]{1,0:T(8,128)(2,1)S(1)}, u32[]{:S(2)}, u32[]{:S(2)}) collective-permute-start(bf16[512,128]{1,0:T(8,128)(2,1)S(1)} %collective-permute-done.4.refs_2_), channel_id=1, source_target_pairs={{0,1},{1,0},{2,3},{3,2},{4,5},{5,4},{6,7},{7,6},{8,9},{9,8},{10,11... | collective-permute-start | bytes 393224 | tf_op jit(solution)/shard_map/ppermute | solution.py:371
  28.6 1.3 %collective-permute-start.11 = (bf16[512,128]{1,0:T(8,128)(2,1)S(1)}, bf16[512,128]{1,0:T(8,128)(2,1)S(1)}, u32[]{:S(2)}, u32[]{:S(2)}) collective-permute-start(bf16[512,128]{1,0:T(8,128)(2,1)S(1)} %collective-permute-done.5.refs_3_), channel_id=1, source_target_pairs={{0,1},{1,0},{2,3},{3,2},{4,5},{5,4},{6,7},{7,6},{8,9},{9,8},{10,11... | collective-permute-start | bytes 393224 | tf_op jit(solution)/shard_map/ppermute | solution.py:371
  36.9 8.5 %collective-permute-start.14 = (f32[256,256]{1,0:T(8,128)S(1)}, f32[256,256]{1,0:T(8,128)S(1)}, u32[]{:S(2)}, u32[]{:S(2)}) collective-permute-start(f32[256,256]{1,0:T(8,128)S(1)} %get-tuple-element.16), channel_id=1, source_target_pairs={{0,8},{1,3},{2,10},{3,1},{4,12},{5,7},{6,14},{7,5},{8,0},{9,11},{1... | collective-permute-start | bytes 786440 | tf_op jit(solution)/shard_map/ppermute | solution.py:90
  37.1 10.1 %collective-permute-start.16 = (f32[256,256]{1,0:T(8,128)S(1)}, f32[256,256]{1,0:T(8,128)S(1)}, u32[]{:S(2)}, u32[]{:S(2)}) collective-permute-start(f32[256,256]{1,0:T(8,128)S(1)} %get-tuple-element.17), channel_id=1, source_target_pairs={{0,16},{1,5},{2,18},{3,7},{4,20},{5,1},{6,22},{7,3},{8,24},{9,13},... | collective-permute-start | bytes 786440 | tf_op jit(solution)/shard_map/ppermute | solution.py:90
  45.4 14.8 %collective-permute-start.15 = (f32[512,256]{1,0:T(8,128)S(1)}, f32[512,256]{1,0:T(8,128)S(1)}, u32[]{:S(2)}, u32[]{:S(2)}) collective-permute-start(f32[512,256]{1,0:T(8,128)S(1)} %pad_maximum_fusion), channel_id=1, source_target_pairs={{0,16},{1,5},{2,18},{3,7},{4,20},{5,1},{6,22},{7,3},{8,24},{9,13},... | collective-permute-start | bytes 1572872 | tf_op jit(solution)/shard_map/ppermute | solution.py:90
  47.3 14.8 %collective-permute-start.17 = (f32[512,256]{1,0:T(8,128)S(1)}, f32[512,256]{1,0:T(8,128)S(1)}, u32[]{:S(2)}, u32[]{:S(2)}) collective-permute-start(f32[512,256]{1,0:T(8,128)S(1)} %pad_maximum_fusion.1), channel_id=1, source_target_pairs={{0,8},{1,3},{2,10},{3,1},{4,12},{5,7},{6,14},{7,5},{8,0},{9,11},{1... | collective-permute-start | bytes 1572872 | tf_op jit(solution)/shard_map/ppermute | solution.py:90
  62.2 2.0 %collective-permute-start.18 = (f32[512,256]{1,0:T(8,128)S(1)}, f32[512,256]{1,0:T(8,128)S(1)}, u32[]{:S(2)}, u32[]{:S(2)}) collective-permute-start(f32[512,256]{1,0:T(8,128)S(1)} %add_add_fusion.own_ref.sown_hbm), channel_id=1, source_target_pairs={{0,1},{1,0},{2,3},{3,2},{4,5},{5,4},{6,7},{7,6},{8,9},{9,8},{10,11... | collective-permute-start | bytes 1572872 | tf_op jit(solution)/shard_map/ppermute | solution.py:402
  95.6 1.6 %collective-permute-start.19 = (f32[128,640]{1,0:T(8,128)S(1)}, f32[128,640]{1,0:T(8,128)S(1)}, u32[]{:S(2)}, u32[]{:S(2)}) collective-permute-start(f32[128,640]{1,0:T(8,128)S(1)} %bitcast.2), channel_id=1, source_target_pairs={{0,1},{1,0},{2,3},{3,2},{4,5},{5,4},{6,7},{7,6},{8,9},{9,8},{10,11... | collective-permute-start | bytes 983048 | tf_op jit(solution)/shard_map/ppermute | solution.py:417

commit v7 on v6

--- a/solution.py
+++ b/solution.py
@@ -29,6 +29,30 @@
 
 def dot_nt(a, b):
     return lax.dot_general(a, b, (((1,), (1,)), ((), ())), precision=HI, preferred_element_type=jnp.float32)
+
+
+def split_stack(value, axis, left):
+    high = value.astype(jnp.bfloat16)
+    rest = value - high.astype(jnp.float32)
+    mid = rest.astype(jnp.bfloat16)
+    low = (rest - mid.astype(jnp.float32)).astype(jnp.bfloat16)
+    order = [high, high, mid, high, low, mid] if left else [high, mid, high, low, high, mid]
+    return jnp.concatenate(order, axis)
+
+
+def stacked(a_axis, b_axis):
+    def product(a, b):
+        return lax.dot_general(
+            split_stack(a, a_axis, True),
+            split_stack(b, b_axis, False),
+            (((a_axis,), (b_axis,)), ((), ())),
+            preferred_element_type=jnp.float32,
+        )
+
+    return product
+
+
+stack_nn, stack_tn, stack_nt = stacked(1, 0), stacked(0, 0), stacked(1, 1)
 
 
 class Plan:
@@ -148,7 +172,7 @@
             def _(shi):
                 record_copy(side, slo, shi).wait()
 
-    step = 128
+    step = 512
     lanes = packed.shape[1]
     left = lax.broadcasted_iota(jnp.int32, (step, lanes), 1) < lanes // 2
 
@@ -239,7 +263,7 @@
         rows = small_factor(w[kb * IB : end, :], kb * IB, IB)
         w[kb * IB : end, :] = rows
         if end < NB:
-            w[end:, :] = w[end:, :] - dot_tn(rows[:, end:NB], rows)
+            w[end:, :] = w[end:, :] - stack_tn(rows[:, :NB], rows)[end:, :]
 
 
 def factor_kernel(factor, gown, gother, sown_hbm, sother_hbm, basis_hbm, tri_hbm, *scratch):
@@ -283,16 +307,16 @@
         v[js, js] = wj.T
         if (j + 1) * NB < n:
             rest = slice((j + 1) * NB, n)
-            row = dot_nn(wj, a[js, rest])
+            row = stack_nn(wj, a[js, rest])
             r[js, rest] = row
             for i in range(j + 1, n // NB):
                 at = (i - j - 1) * NB
-                a[i * NB : (i + 1) * NB, i * NB :] = a[i * NB : (i + 1) * NB, i * NB :] - dot_tn(
+                a[i * NB : (i + 1) * NB, i * NB :] = a[i * NB : (i + 1) * NB, i * NB :] - stack_tn(
                     row[:, at : at + NB], row[:, at:]
                 )
         if j > 0:
             top = slice(0, j * NB)
-            v[top, js] = -dot_nt(dot_nn(v[top, top], r[top, js]), wj)
+            v[top, js] = -stack_nt(stack_nn(v[top, top], r[top, js]), wj)
 
     @pl.when(panel == 0)
     def _():

time: 121 us -> 113 us (0.934)
  Pallas kernels: 35.4 us -> 28.1 us
    pallas_call x1, Pallas kernels: 22.7 us -> 17.6 us  [per_device(): pl.pallas_call(functools.partial(factor_kernel, math.sqrt(n * rows)), out...]
    pallas_call x1, Pallas kernels: 5.38 us -> 3.21 us  [per_device(): pl.pallas_call(functools.partial(place_kernel, plan), out_shape=pltpu.VME...]
  transfers between devices with their start and end apart: 20 -> 20, of which waited for: 14 -> 15; matrix products, arithmetic and copies ran while one was open for 0% -> 0% of each run, Pallas kernels for 8% -> 7%
where the time goes in v7:
time: 113 us
  waiting for transfers between devices  34.6 us (31%)
  blocking collectives  29.8 us (26%)
  Pallas kernels  28.1 us (25%)
  starting transfers between devices  17.9 us (16%)
  local copies, waits for them, and re-layouts  1.15 us (1%)
    ppermute x4, waiting for transfers between devices, sent(): return lax.ppermute(value, BOTH, plan.pairs(0, db))  18.1 us
    pallas_call x1, Pallas kernels, per_device(): pl.pallas_call(functools.partial(factor_kernel, math.sqrt(n * rows)), out...  17.6 us
    all_to_all x1, blocking collectives, per_device(): lax.all_to_all(gram.reshape(n, NB // n, width), 'tm', 0, 0, tiled=True)  15.6 us
    all_to_all x1, blocking collectives, per_device(): gram = lax.all_to_all(alike, 'tm', 0, 0, tiled=True).reshape(NB, width)  14.2 us
    ppermute x3, waiting for transfers between devices, per_device(): pieces.append(lax.ppermute(own_rows, 'tm', plan.plain_pairs(s, 0)))  7.07 us
    pallas_call x4, Pallas kernels, part(): pl.pallas_call(functools.partial(sketch_kernel, plan, rows, depth, variab...  5.81 us
    ppermute x3, starting transfers between devices, per_device(): pieces.append(lax.ppermute(own_rows, 'tm', plan.plain_pairs(s, 0)))  5.78 us
    ppermute x4, starting transfers between devices, sent(): return lax.ppermute(value, BOTH, plan.pairs(da, 0))  5.35 us
  transfers between devices with their start and end apart: 20, of which 15 were waited for; matrix products, arithmetic and copies ran while one was open for 0% of the time, Pallas kernels for 7%

profile of v7, /device:TPU:0, one launch (start us, length us, event | category | flops | bytes accessed | tf_op | source)
XLA Modules:
  0.0 112.8 jit_solution(7747116308021698131)
XLA Ops:
  0.6 0.0 copy-start
  0.6 1.0 copy.4.series
  1.7 0.1 pack.1
  1.8 5.1 %collective-permute-start.2 = (bf16[128,128]{1,0:T(8,128)(2,1)S(1)}, bf16[128,128]{1,0:T(8,128)(2,1)S(1)}, u32[]{:S(2)}, u32[]{:S(2)}) collective-permute-start(bf16[128,128]{1,0:T(8,128)(2,1)S(1)} %pack.1), channel_id=1, source_target_pairs={{0,24},{2,26},{4,28},{6,30},{8,16},{10,18},{12,20},{14,22},{16,8},... | collective-permute-start | bytes 98312 | tf_op jit(solution)/shard_map/ppermute | solution.py:388
  6.9 0.0 collective-permute-start.1
  6.9 0.6 collective-permute-start
  7.5 1.7 %collective-permute-start.7 = (bf16[1024,256]{1,0:T(8,128)(2,1)}, bf16[1024,256]{1,0:T(8,128)(2,1)S(1)}, u32[]{:S(2)}, u32[]{:S(2)}) collective-permute-start(bf16[1024,256]{1,0:T(8,128)(2,1)} %refs_0_.3), channel_id=1, source_target_pairs={{0,4},{1,17},{2,6},{3,19},{4,0},{5,21},{6,2},{7,23},{8,12},{9,25},... | collective-permute-start | bytes 1572872 | tf_op jit(solution)/shard_map/ppermute | solution.py:96
  9.2 1.5 %collective-permute-start.6 = (bf16[1024,256]{1,0:T(8,128)(2,1)}, bf16[1024,256]{1,0:T(8,128)(2,1)S(1)}, u32[]{:S(2)}, u32[]{:S(2)}) collective-permute-start(bf16[1024,256]{1,0:T(8,128)(2,1)} %refs_0_.3), channel_id=1, source_target_pairs={{0,2},{1,9},{2,0},{3,11},{4,6},{5,13},{6,4},{7,15},{8,10},{9,1},{1... | collective-permute-start | bytes 1572872 | tf_op jit(solution)/shard_map/ppermute | solution.py:96
  10.7 1.0 collective-permute-done
  11.7 6.1 %collective-permute-done.1 = bf16[128,128]{1,0:T(8,128)(2,1)S(1)} collective-permute-done((bf16[128,128]{1,0:T(8,128)(2,1)S(1)}, bf16[128,128]{1,0:T(8,128)(2,1)S(1)}, u32[]{:S(2)}, u32[]{:S(2)}) %collective-permute-start.1) | collective-permute-done | bytes 32800 | tf_op jit(solution)/shard_map/ppermute | solution.py:388
  17.8 2.5 %collective-permute-start.5 = (bf16[512,128]{1,0:T(8,128)(2,1)S(1)}, bf16[512,128]{1,0:T(8,128)(2,1)S(1)}, u32[]{:S(2)}, u32[]{:S(2)}) collective-permute-start(bf16[512,128]{1,0:T(8,128)(2,1)S(1)} %constant_dynamic-update-slice_fusion.refs_0_), channel_id=1, source_target_pairs={{0,6},{2,4},{4,2},{6,0},{8,14},{10,12},{12,10},{14,8},{16,22},{18,... | collective-permute-start | bytes 393224 | tf_op jit(solution)/shard_map/ppermute | solution.py:392
  20.3 0.5 collective-permute-start.4
  20.8 0.5 collective-permute-start.3
  21.4 2.4 %collective-permute-done.5.refs_3_ = bf16[512,128]{1,0:T(8,128)(2,1)S(1)} collective-permute-done((bf16[512,128]{1,0:T(8,128)(2,1)S(1)}, bf16[512,128]{1,0:T(8,128)(2,1)S(1)}, u32[]{:S(2)}, u32[]{:S(2)}) %collective-permute-start.5) | collective-permute-done | bytes 131104 | tf_op jit(solution)/shard_map/ppermute | solution.py:392
  23.7 1.5 %collective-permute-done.4.refs_2_ = bf16[512,128]{1,0:T(8,128)(2,1)S(1)} collective-permute-done((bf16[512,128]{1,0:T(8,128)(2,1)S(1)}, bf16[512,128]{1,0:T(8,128)(2,1)S(1)}, u32[]{:S(2)}, u32[]{:S(2)}) %collective-permute-start.4) | collective-permute-done | bytes 131104 | tf_op jit(solution)/shard_map/ppermute | solution.py:392
  25.3 0.5 collective-permute-done.3.refs_1_
  25.8 0.0 collective-permute-done.7.refs_2_
  25.8 1.0 collective-permute-start.13
  26.9 1.2 %collective-permute-start.12 = (bf16[512,256]{1,0:T(8,128)(2,1)S(1)}, bf16[512,256]{1,0:T(8,128)(2,1)S(1)}, u32[]{:S(2)}, u32[]{:S(2)}) collective-permute-start(bf16[512,256]{1,0:T(8,128)(2,1)S(1)} %slice.32), channel_id=1, source_target_pairs={{0,4},{1,17},{2,6},{3,19},{4,0},{5,21},{6,2},{7,23},{8,12},{9,25},... | collective-permute-start | bytes 786440 | tf_op jit(solution)/shard_map/ppermute | solution.py:96
  28.1 0.5 collective-permute-start.10
  28.6 0.0 collective-permute-start.11
  28.6 0.8 collective-permute-done.9.refs_5_
  29.4 0.2 collective-permute-done.10.refs_6_
  29.6 0.3 collective-permute-done.11.refs_7_
  29.9 3.2 %place.1.wide = bf16[10240,128]{1,0:T(8,128)(2,1)S(1)} custom-call(bf16[512,128]{1,0:T(8,128)(2,1)S(1)} %constant_dynamic-update-slice_fusion.refs_0_, bf16[512,128]{1,0:T(8,128)(2,1)S(1)} %collective-permute-done.3.refs_1_, bf16[512,128]{1,0:T(8,128)(2,1)S(1)} %collective-permute-done.4.refs_2_, bf16[512,128]{1,0:T(8,128)(2,1)S(1)} %collective-permute-done.5.refs_3_, ...), custom_call_target="tpu_custom_call" | custom-call | tf_op jit(solution)/shard_map/place/pallas_call | solution.py:397
  33.1 0.2 collective-permute-done.12.refs_3_
  33.3 1.4 %sketch3.1 = f32[512,256]{1,0:T(8,128)S(1)} custom-call(bf16[10240,128]{1,0:T(8,128)(2,1)S(1)} %place.1.wide, bf16[1024,256]{1,0:T(8,128)(2,1)S(1)} %copy-done, bf16[1024,256]{1,0:T(8,128)(2,1)S(1)} %collective-permute-done.6.refs_1_, bf16[1024,256]{1,0:T(8,128)(2,1)S(1)} %collective-permute-done.7.refs_2_, ...), custom_call_target="tpu_custom_call" | custom-call | flops 1073741824 | bytes 524288 | tf_op jit(solution)/shard_map/sketch3/pallas_call | solution.py:413
  34.8 0.3 collective-permute-start.14
  35.1 2.2 %collective-permute-start.16 = (f32[256,256]{1,0:T(8,128)S(1)}, f32[256,256]{1,0:T(8,128)S(1)}, u32[]{:S(2)}, u32[]{:S(2)}) collective-permute-start(f32[256,256]{1,0:T(8,128)S(1)} %get-tuple-element.17), channel_id=1, source_target_pairs={{0,16},{1,5},{2,18},{3,7},{4,20},{5,1},{6,22},{7,3},{8,24},{9,13},... | collective-permute-start | bytes 786440 | tf_op jit(solution)/shard_map/ppermute | solution.py:114
  37.2 1.5 %sketch1.1 = f32[512,256]{1,0:T(8,128)S(1)} custom-call(bf16[10240,128]{1,0:T(8,128)(2,1)S(1)} %place.1.wide, bf16[1024,256]{1,0:T(8,128)(2,1)S(1)} %copy-done, bf16[1024,256]{1,0:T(8,128)(2,1)S(1)} %collective-permute-done.6.refs_1_, bf16[1024,256]{1,0:T(8,128)(2,1)S(1)} %collective-permute-done.7.refs_2_, ...), custom_call_target="tpu_custom_call" | custom-call | flops 1073741824 | bytes 524288 | tf_op jit(solution)/shard_map/sketch1/pallas_call | solution.py:413
  38.7 1.5 %sketch2.1 = f32[512,256]{1,0:T(8,128)S(1)} custom-call(bf16[10240,128]{1,0:T(8,128)(2,1)S(1)} %place.1.wide, bf16[1024,256]{1,0:T(8,128)(2,1)S(1)} %copy-done, bf16[1024,256]{1,0:T(8,128)(2,1)S(1)} %collective-permute-done.6.refs_1_, bf16[1024,256]{1,0:T(8,128)(2,1)S(1)} %collective-permute-done.7.refs_2_, ...), custom_call_target="tpu_custom_call" | custom-call | flops 1073741824 | bytes 524288 | tf_op jit(solution)/shard_map/sketch2/pallas_call | solution.py:413
  40.2 3.4 %collective-permute-done.14 = f32[256,256]{1,0:T(8,128)S(1)} collective-permute-done((f32[256,256]{1,0:T(8,128)S(1)}, f32[256,256]{1,0:T(8,128)S(1)}, u32[]{:S(2)}, u32[]{:S(2)}) %collective-permute-start.14) | collective-permute-done | bytes 262176 | tf_op jit(solution)/shard_map/ppermute | solution.py:114
  43.6 0.1 slice_add_fusion.1
  43.7 0.1 collective-permute-start.15
  43.7 1.5 %collective-permute-done.16 = f32[256,256]{1,0:T(8,128)S(1)} collective-permute-done((f32[256,256]{1,0:T(8,128)S(1)}, f32[256,256]{1,0:T(8,128)S(1)}, u32[]{:S(2)}, u32[]{:S(2)}) %collective-permute-start.16) | collective-permute-done | bytes 262176 | tf_op jit(solution)/shard_map/ppermute | solution.py:114
  45.2 0.1 fusion.1
  45.3 0.1 collective-permute-start.17
  45.4 1.4 %sketch0.1 = f32[512,256]{1,0:T(8,128)S(1)} custom-call(bf16[10240,128]{1,0:T(8,128)(2,1)S(1)} %place.1.wide, bf16[1024,256]{1,0:T(8,128)(2,1)S(1)} %copy-done, bf16[1024,256]{1,0:T(8,128)(2,1)S(1)} %collective-permute-done.6.refs_1_, bf16[1024,256]{1,0:T(8,128)(2,1)S(1)} %collective-permute-done.7.refs_2_, ...), custom_call_target="tpu_custom_call" | custom-call | flops 1073741824 | bytes 524288 | tf_op jit(solution)/shard_map/sketch0/pallas_call | solution.py:413
  46.9 11.6 %collective-permute-done.15 = f32[512,256]{1,0:T(8,128)S(1)} collective-permute-done((f32[512,256]{1,0:T(8,128)S(1)}, f32[512,256]{1,0:T(8,128)S(1)}, u32[]{:S(2)}, u32[]{:S(2)}) %collective-permute-start.15) | collective-permute-done | bytes 524320 | tf_op jit(solution)/shard_map/ppermute | solution.py:114
  58.5 1.6 %collective-permute-done.17 = f32[512,256]{1,0:T(8,128)S(1)} collective-permute-done((f32[512,256]{1,0:T(8,128)S(1)}, f32[512,256]{1,0:T(8,128)S(1)}, u32[]{:S(2)}, u32[]{:S(2)}) %collective-permute-start.17) | collective-permute-done | bytes 524320 | tf_op jit(solution)/shard_map/ppermute | solution.py:114
  60.1 0.1 add_add_fusion.own_ref.sown_hbm
  60.2 0.1 collective-permute-start.18
  60.3 1.9 %collective-permute-done.18.other_ref.sother_hbm = f32[512,256]{1,0:T(8,128)S(1)} collective-permute-done((f32[512,256]{1,0:T(8,128)S(1)}, f32[512,256]{1,0:T(8,128)S(1)}, u32[]{:S(2)}, u32[]{:S(2)}) %collective-permute-start.18) | collective-permute-done | bytes 524320 | tf_op jit(solution)/shard_map/ppermute | solution.py:426
  62.2 1.4 %gram.1 = f32[128,640]{1,0:T(8,128)S(1)} custom-call(f32[512,256]{1,0:T(8,128)S(1)} %add_add_fusion.own_ref.sown_hbm, f32[512,256]{1,0:T(8,128)S(1)} %collective-permute-done.18.other_ref.sother_hbm), custom_call_target="tpu_custom_call" | custom-call | tf_op jit(solution)/shard_map/gram/pallas_call | solution.py:429
  63.6 15.6 %all_to_all.10 = f32[16,8,640]{2,1,0:T(8,128)S(1)} all-to-all(f32[16,8,640]{2,1,0:T(8,128)S(1)} %bitcast.4), channel_id=1, replica_groups=mesh['grp'=1,'tm'=16,'panel'=2] {'tm'}, dimensions={0} | all-to-all | bytes 655360 | tf_op jit(solution)/shard_map/all_to_all | solution.py:437
  79.2 14.2 %all_to_all.11 = f32[16,8,640]{2,1,0:T(8,128)S(1)} all-to-all(f32[16,8,640]{2,1,0:T(8,128)S(1)} %broadcast_in_dim.2), channel_id=1, replica_groups=mesh['grp'=1,'tm'=16,'panel'=2] {'tm'}, dimensions={0} | all-to-all | bytes 655360 | tf_op jit(solution)/shard_map/all_to_all | solution.py:440
  93.4 1.6 %collective-permute-done.19.gother = f32[128,640]{1,0:T(8,128)S(1)} collective-permute-done((f32[128,640]{1,0:T(8,128)S(1)}, f32[128,640]{1,0:T(8,128)S(1)}, u32[]{:S(2)}, u32[]{:S(2)}) %collective-permute-start.19) | collective-permute-done | bytes 327712 | tf_op jit(solution)/shard_map/ppermute | solution.py:441
  95.0 17.6 %factor.1 = (f32[512,256]{1,0:T(8,128)}, f32[512,256]{1,0:T(8,128)}) custom-call(f32[128,640]{1,0:T(8,128)S(1)} %bitcast.3, f32[128,640]{1,0:T(8,128)S(1)} %collective-permute-done.19.gother, f32[512,256]{1,0:T(8,128)S(1)} %add_add_fusion.own_ref.sown_hbm, f32[512,256]{1,0:T(8,128)S(1)} %collective-permute-done.18.other_ref.sother_hbm), custom_call_target="tpu_custom_call" | custom-call | tf_op jit(solution)/shard_map/factor/pallas_call | solution.py:444
  (19 shorter events, 0.2 us)
Async XLA Ops:
  0.6 32.7 %copy-start = (bf16[1024,256]{1,0:T(8,128)(2,1)S(1)}, bf16[1024,256]{1,0:T(8,128)(2,1)}, u32[]{:S(2)}) copy-start(bf16[1024,256]{1,0:T(8,128)(2,1)} %refs_0_.3) | copy-start | bytes 1572868
  1.8 16.0 %collective-permute-start.2 = (bf16[128,128]{1,0:T(8,128)(2,1)S(1)}, bf16[128,128]{1,0:T(8,128)(2,1)S(1)}, u32[]{:S(2)}, u32[]{:S(2)}) collective-permute-start(bf16[128,128]{1,0:T(8,128)(2,1)S(1)} %pack.1), channel_id=1, source_target_pairs={{0,24},{2,26},{4,28},{6,30},{8,16},{10,18},{12,20},{14,22},{16,8},... | collective-permute-start | bytes 98312 | tf_op jit(solution)/shard_map/ppermute | solution.py:388
  6.9 10.9 %collective-permute-start.1 = (bf16[128,128]{1,0:T(8,128)(2,1)S(1)}, bf16[128,128]{1,0:T(8,128)(2,1)S(1)}, u32[]{:S(2)}, u32[]{:S(2)}) collective-permute-start(bf16[128,128]{1,0:T(8,128)(2,1)S(1)} %pack.1), channel_id=1, source_target_pairs={{0,16},{2,18},{4,20},{6,22},{8,24},{10,26},{12,28},{14,30},{16,0},... | collective-permute-start | bytes 98312 | tf_op jit(solution)/shard_map/ppermute | solution.py:388
  6.9 4.8 %collective-permute-start = (bf16[128,128]{1,0:T(8,128)(2,1)S(1)}, bf16[128,128]{1,0:T(8,128)(2,1)S(1)}, u32[]{:S(2)}, u32[]{:S(2)}) collective-permute-start(bf16[128,128]{1,0:T(8,128)(2,1)S(1)} %pack.1), channel_id=1, source_target_pairs={{0,8},{2,10},{4,12},{6,14},{8,0},{10,2},{12,4},{14,6},{16,24},{18,... | collective-permute-start | bytes 98312 | tf_op jit(solution)/shard_map/ppermute | solution.py:388
  7.5 18.3 %collective-permute-start.7 = (bf16[1024,256]{1,0:T(8,128)(2,1)}, bf16[1024,256]{1,0:T(8,128)(2,1)S(1)}, u32[]{:S(2)}, u32[]{:S(2)}) collective-permute-start(bf16[1024,256]{1,0:T(8,128)(2,1)} %refs_0_.3), channel_id=1, source_target_pairs={{0,4},{1,17},{2,6},{3,19},{4,0},{5,21},{6,2},{7,23},{8,12},{9,25},... | collective-permute-start | bytes 1572872 | tf_op jit(solution)/shard_map/ppermute | solution.py:96
  9.2 16.6 %collective-permute-start.6 = (bf16[1024,256]{1,0:T(8,128)(2,1)}, bf16[1024,256]{1,0:T(8,128)(2,1)S(1)}, u32[]{:S(2)}, u32[]{:S(2)}) collective-permute-start(bf16[1024,256]{1,0:T(8,128)(2,1)} %refs_0_.3), channel_id=1, source_target_pairs={{0,2},{1,9},{2,0},{3,11},{4,6},{5,13},{6,4},{7,15},{8,10},{9,1},{1... | collective-permute-start | bytes 1572872 | tf_op jit(solution)/shard_map/ppermute | solution.py:96
  17.8 5.9 %collective-permute-start.5 = (bf16[512,128]{1,0:T(8,128)(2,1)S(1)}, bf16[512,128]{1,0:T(8,128)(2,1)S(1)}, u32[]{:S(2)}, u32[]{:S(2)}) collective-permute-start(bf16[512,128]{1,0:T(8,128)(2,1)S(1)} %constant_dynamic-update-slice_fusion.refs_0_), channel_id=1, source_target_pairs={{0,6},{2,4},{4,2},{6,0},{8,14},{10,12},{12,10},{14,8},{16,22},{18,... | collective-permute-start | bytes 393224 | tf_op jit(solution)/shard_map/ppermute | solution.py:392
  20.3 5.0 %collective-permute-start.4 = (bf16[512,128]{1,0:T(8,128)(2,1)S(1)}, bf16[512,128]{1,0:T(8,128)(2,1)S(1)}, u32[]{:S(2)}, u32[]{:S(2)}) collective-permute-start(bf16[512,128]{1,0:T(8,128)(2,1)S(1)} %constant_dynamic-update-slice_fusion.refs_0_), channel_id=1, source_target_pairs={{0,4},{2,6},{4,0},{6,2},{8,12},{10,14},{12,8},{14,10},{16,20},{18,... | collective-permute-start | bytes 393224 | tf_op jit(solution)/shard_map/ppermute | solution.py:392
  20.8 5.0 %collective-permute-start.3 = (bf16[512,128]{1,0:T(8,128)(2,1)S(1)}, bf16[512,128]{1,0:T(8,128)(2,1)S(1)}, u32[]{:S(2)}, u32[]{:S(2)}) collective-permute-start(bf16[512,128]{1,0:T(8,128)(2,1)S(1)} %constant_dynamic-update-slice_fusion.refs_0_), channel_id=1, source_target_pairs={{0,2},{2,0},{4,6},{6,4},{8,10},{10,8},{12,14},{14,12},{16,18},{18,... | collective-permute-start | bytes 393224 | tf_op jit(solution)/shard_map/ppermute | solution.py:392
  25.8 2.8 %collective-permute-start.8 = (bf16[512,128]{1,0:T(8,128)(2,1)S(1)}, bf16[512,128]{1,0:T(8,128)(2,1)S(1)}, u32[]{:S(2)}, u32[]{:S(2)}) collective-permute-start(bf16[512,128]{1,0:T(8,128)(2,1)S(1)} %constant_dynamic-update-slice_fusion.refs_0_), channel_id=1, source_target_pairs={{0,1},{1,0},{2,3},{3,2},{4,5},{5,4},{6,7},{7,6},{8,9},{9,8},{10,11... | collective-permute-start | bytes 393224 | tf_op jit(solution)/shard_map/ppermute | solution.py:395
  25.8 7.3 %collective-permute-start.13 = (bf16[512,256]{1,0:T(8,128)(2,1)S(1)}, bf16[512,256]{1,0:T(8,128)(2,1)S(1)}, u32[]{:S(2)}, u32[]{:S(2)}) collective-permute-start(bf16[512,256]{1,0:T(8,128)(2,1)S(1)} %slice.33), channel_id=1, source_target_pairs={{0,2},{1,9},{2,0},{3,11},{4,6},{5,13},{6,4},{7,15},{8,10},{9,1},{1... | collective-permute-start | bytes 786440 | tf_op jit(solution)/shard_map/ppermute | solution.py:96
  26.9 6.4 %collective-permute-start.12 = (bf16[512,256]{1,0:T(8,128)(2,1)S(1)}, bf16[512,256]{1,0:T(8,128)(2,1)S(1)}, u32[]{:S(2)}, u32[]{:S(2)}) collective-permute-start(bf16[512,256]{1,0:T(8,128)(2,1)S(1)} %slice.32), channel_id=1, source_target_pairs={{0,4},{1,17},{2,6},{3,19},{4,0},{5,21},{6,2},{7,23},{8,12},{9,25},... | collective-permute-start | bytes 786440 | tf_op jit(solution)/shard_map/ppermute | solution.py:96
  28.1 1.3 %collective-permute-start.9 = (bf16[512,128]{1,0:T(8,128)(2,1)S(1)}, bf16[512,128]{1,0:T(8,128)(2,1)S(1)}, u32[]{:S(2)}, u32[]{:S(2)}) collective-permute-start(bf16[512,128]{1,0:T(8,128)(2,1)S(1)} %collective-permute-done.3.refs_1_), channel_id=1, source_target_pairs={{0,1},{1,0},{2,3},{3,2},{4,5},{5,4},{6,7},{7,6},{8,9},{9,8},{10,11... | collective-permute-start | bytes 393224 | tf_op jit(solution)/shard_map/ppermute | solution.py:395
  28.1 1.5 %collective-permute-start.10 = (bf16[512,128]{1,0:T(8,128)(2,1)S(1)}, bf16[512,128]{1,0:T(8,128)(2,1)S(1)}, u32[]{:S(2)}, u32[]{:S(2)}) collective-permute-start(bf16[512,128]{1,0:T(8,128)(2,1)S(1)} %collective-permute-done.4.refs_2_), channel_id=1, source_target_pairs={{0,1},{1,0},{2,3},{3,2},{4,5},{5,4},{6,7},{7,6},{8,9},{9,8},{10,11... | collective-permute-start | bytes 393224 | tf_op jit(solution)/shard_map/ppermute | solution.py:395
  28.6 1.3 %collective-permute-start.11 = (bf16[512,128]{1,0:T(8,128)(2,1)S(1)}, bf16[512,128]{1,0:T(8,128)(2,1)S(1)}, u32[]{:S(2)}, u32[]{:S(2)}) collective-permute-start(bf16[512,128]{1,0:T(8,128)(2,1)S(1)} %collective-permute-done.5.refs_3_), channel_id=1, source_target_pairs={{0,1},{1,0},{2,3},{3,2},{4,5},{5,4},{6,7},{7,6},{8,9},{9,8},{10,11... | collective-permute-start | bytes 393224 | tf_op jit(solution)/shard_map/ppermute | solution.py:395
  34.8 8.7 %collective-permute-start.14 = (f32[256,256]{1,0:T(8,128)S(1)}, f32[256,256]{1,0:T(8,128)S(1)}, u32[]{:S(2)}, u32[]{:S(2)}) collective-permute-start(f32[256,256]{1,0:T(8,128)S(1)} %get-tuple-element.16), channel_id=1, source_target_pairs={{0,8},{1,3},{2,10},{3,1},{4,12},{5,7},{6,14},{7,5},{8,0},{9,11},{1... | collective-permute-start | bytes 786440 | tf_op jit(solution)/shard_map/ppermute | solution.py:114
  35.1 10.1 %collective-permute-start.16 = (f32[256,256]{1,0:T(8,128)S(1)}, f32[256,256]{1,0:T(8,128)S(1)}, u32[]{:S(2)}, u32[]{:S(2)}) collective-permute-start(f32[256,256]{1,0:T(8,128)S(1)} %get-tuple-element.17), channel_id=1, source_target_pairs={{0,16},{1,5},{2,18},{3,7},{4,20},{5,1},{6,22},{7,3},{8,24},{9,13},... | collective-permute-start | bytes 786440 | tf_op jit(solution)/shard_map/ppermute | solution.py:114
  43.7 14.8 %collective-permute-start.15 = (f32[512,256]{1,0:T(8,128)S(1)}, f32[512,256]{1,0:T(8,128)S(1)}, u32[]{:S(2)}, u32[]{:S(2)}) collective-permute-start(f32[512,256]{1,0:T(8,128)S(1)} %pad_maximum_fusion), channel_id=1, source_target_pairs={{0,16},{1,5},{2,18},{3,7},{4,20},{5,1},{6,22},{7,3},{8,24},{9,13},... | collective-permute-start | bytes 1572872 | tf_op jit(solution)/shard_map/ppermute | solution.py:114
  45.3 14.8 %collective-permute-start.17 = (f32[512,256]{1,0:T(8,128)S(1)}, f32[512,256]{1,0:T(8,128)S(1)}, u32[]{:S(2)}, u32[]{:S(2)}) collective-permute-start(f32[512,256]{1,0:T(8,128)S(1)} %pad_maximum_fusion.1), channel_id=1, source_target_pairs={{0,8},{1,3},{2,10},{3,1},{4,12},{5,7},{6,14},{7,5},{8,0},{9,11},{1... | collective-permute-start | bytes 1572872 | tf_op jit(solution)/shard_map/ppermute | solution.py:114
  60.2 2.0 %collective-permute-start.18 = (f32[512,256]{1,0:T(8,128)S(1)}, f32[512,256]{1,0:T(8,128)S(1)}, u32[]{:S(2)}, u32[]{:S(2)}) collective-permute-start(f32[512,256]{1,0:T(8,128)S(1)} %add_add_fusion.own_ref.sown_hbm), channel_id=1, source_target_pairs={{0,1},{1,0},{2,3},{3,2},{4,5},{5,4},{6,7},{7,6},{8,9},{9,8},{10,11... | collective-permute-start | bytes 1572872 | tf_op jit(solution)/shard_map/ppermute | solution.py:426
  93.4 1.6 %collective-permute-start.19 = (f32[128,640]{1,0:T(8,128)S(1)}, f32[128,640]{1,0:T(8,128)S(1)}, u32[]{:S(2)}, u32[]{:S(2)}) collective-permute-start(f32[128,640]{1,0:T(8,128)S(1)} %bitcast.2), channel_id=1, source_target_pairs={{0,1},{1,0},{2,3},{3,2},{4,5},{5,4},{6,7},{7,6},{8,9},{9,8},{10,11... | collective-permute-start | bytes 983048 | tf_op jit(solution)/shard_map/ppermute | solution.py:441
